TPU v7x, 128 devices: a whole 4x4x4 slice. The times are simulated.
128 devices in a mesh: rx: 8 (over x, core), ry: 16 (over z, y).
Axes of the slice: x: 4, y: 4, z: 4, core: 2. Of those that a mesh axis runs over, the one named last changes fastest.
Arguments:
- noisy_input: bfloat16 [147456, 12, 128], P(('rx', 'ry')), may hold values from -6 to 6
- adjacency: bfloat16 [1152, 6, 128, 128], P(('rx', 'ry')), may hold values from -0.21875 to 0.21875
- neighbours: int32 [1152, 6], P(('rx', 'ry')), may hold values from 0 to 8, as said below
- norm_gain: float32 [128], replicated, may hold values from 0.1 to 1.9
- w_mix: bfloat16 [128, 128], replicated, may hold values from -0.5 to 0.5
- pool_weight: bfloat16 [147456], P(('rx', 'ry')), may hold values from 0.049804688 to 0.29882812
- cluster: int32 [147456], P(('rx', 'ry')), may hold values from 0 to 143, as said below
- owner_ids: int32 [18432, 1], P(('rx', 'ry')), may hold values from 0 to 127; in each aligned block of 144 rows (0 to 143, 144 to 287, ...) at most 2 rows name the same one
- w_coarse: bfloat16 [128, 128], replicated, may hold values from -0.5 to 0.5
- w_region: bfloat16 [128, 128], replicated, may hold values from -0.5 to 0.5
- w_out: bfloat16 [128, 128], replicated, may hold values from -0.5 to 0.5
Outputs:
- denoised: bfloat16 [147456, 12, 128], P(('rx', 'ry'))
Inputs may be any that keep to these rules, and one draw needn't show every extreme that they name: `neighbours`: the 6 codes of one block are different. `cluster`: among the 1152 nodes of one device's square each value is taken by exactly 8 nodes. `owner_ids`: in each aligned block of 144 rows no value is named by more than 2 rows, and one value is named by exactly 2 rows in some or all blocks; every value is named by some row.
All inputs are finite; a program needn't handle non-finite values.
Results may differ from a plain program's by a relative error of at most 0.015.
Values may be sent and summed in bfloat16 or wider, within the bound.
No kernel may reach another device: no remote copies, remote signals or barrier semaphores. Data moves between devices by JAX's collectives and lax.ppermute only.
A program may use at most 128 MiB of HBM per device.

v0:
```python
import functools
import jax
import jax.numpy as jnp
from jax import lax
from jax.experimental import pallas as pl
from jax.experimental.pallas import tpu as pltpu
from jax.sharding import PartitionSpec as P

GB, BLK, NB, C = 3, 128, 6, 128
EXT = GB + 2
ROWS = GB * GB * BLK
SIDE = GB * BLK
PAIR = 2
WIDE = PAIR * C
LATE = [(0, 3 + 3), (3, 3), (6, 0), (0, 0), (6, 6), (2, 3 + 5), (5, 5), (8, 2), (2, 2), (8, 8)]
bf16, f32 = jnp.bfloat16, jnp.float32


def silu(v):
    return v / (1.0 + jnp.exp(-v))


def dot(a, b):
    return jnp.dot(a, b, preferred_element_type=f32)


def span(k):
    return slice(k * BLK, (k + 1) * BLK)


def ext_row(codes, j, n):
    code = codes[j * NB + n]
    e = (j // GB + code // 3) * EXT + j % GB + code % 3
    return pl.ds(pl.multiple_of(e * BLK, BLK), BLK)


def fill(ext, own, yl, yr, xu, xd):
    @pl.when(pl.program_id(0) == 0)
    def _():
        for e in (0, EXT - 1, 2 * EXT, 3 * EXT - 1, (EXT - 1) * EXT, EXT * EXT - 1):
            ext[span(e), :] = jnp.zeros((BLK, WIDE), bf16)

    for s in range(PAIR):
        lanes = span(s)

        def put(row, col, block):
            ext[span(row * EXT + col), lanes] = block

        for a in range(GB):
            for b in range(GB):
                put(a + 1, b + 1, own[s, span(a * GB + b), :])
            put(0, a + 1, xu[s, span(a), :])
            put(EXT - 1, a + 1, xd[s, span(a), :])
        for e, row in enumerate((1, GB)):
            put(row, 0, yl[s, span(e), :])
            put(row, EXT - 1, yr[s, span(e), :])


def early_sum(codes, adj, ext, j):
    weights = jnp.concatenate([adj[j, n] for n in range(NB)], axis=1)
    feats = jnp.concatenate([ext[ext_row(codes, j, n), :] for n in range(NB)], axis=0)
    return dot(weights, feats)


def late_sum(late, j, mids, ups, downs):
    side = 0 if j % GB == 0 else 1
    k = side * 5 + j // GB
    if j // GB == 1:
        return dot(late[k], mids[side])
    corner, block = (3, ups[side]) if j // GB == 0 else (4, downs[side])
    return dot(jnp.concatenate([late[k], late[side * 5 + corner]], axis=1), jnp.concatenate([mids[side], block], axis=0))


def joined(ref, k):
    return jnp.concatenate([ref[s, span(k), :] for s in range(PAIR)], axis=1)


def mix_in(diffused, base, gain, w_mix):
    v = diffused.astype(bf16).astype(f32)
    ms = jnp.mean(v * v, axis=1, keepdims=True)
    normed = (v * lax.rsqrt(ms + 1e-6) * gain[...]).astype(bf16)
    return (base.astype(f32) + silu(dot(normed, w_mix[...]))).astype(bf16)


def encode_early(codes, own, yl, yr, xu, xd, adj, gain, w_mix, acc, mid, ext):
    fill(ext, own, yl, yr, xu, xd)
    for j in range(GB * GB):
        total = early_sum(codes, adj, ext, j)
        a, b = j // GB, j % GB
        for s in range(PAIR):
            v = total[:, span(s)]
            if b == 1:
                mid[s, span(a), :] = mix_in(v, own[s, span(j), :], gain, w_mix)
            else:
                acc[s, span(a if b == 0 else GB + a), :] = v


def encode_late(own, acc, mid, ml, mr, cu, cd, late, gain, w_mix, w_coarse, pool, unpool, spread, tails,
                d1, al, ar, bl, br, du, dd, part, enc):
    mids, ups, downs = (joined(ml, 0), joined(mr, 0)), (joined(cu, 0), joined(cu, 1)), (joined(cd, 0), joined(cd, 1))
    for j in range(GB * GB):
        a, b = j // GB, j % GB
        if b == 1:
            for s in range(PAIR):
                enc[span(j), span(s)] = mid[s, span(a), :]
            continue
        rest = late_sum(late, j, mids, ups, downs)
        for s in range(PAIR):
            v = acc[s, span(a if b == 0 else GB + a), :] + rest[:, span(s)]
            enc[span(j), span(s)] = mix_in(v, own[s, span(j), :], gain, w_mix)
    pooled = dot(pool[...], enc[...]).astype(bf16)
    lifted = jnp.concatenate([silu(dot(pooled[:, span(s)], w_coarse[...])).astype(bf16) for s in range(PAIR)], axis=1)
    part[...] = dot(spread[...], lifted).astype(bf16)
    refined = (pooled.astype(f32) + lifted.astype(f32)).astype(bf16)
    for j in range(GB * GB):
        a, b = j // GB, j % GB
        back = (enc[span(j), :].astype(f32) + dot(unpool[span(j), :], refined)).astype(bf16)
        for s in range(PAIR):
            v = back[:, span(s)]
            d1[s, span(j), :] = v
            if b != 1 and a != 1:
                (al if b == 0 else ar)[s, span(a // 2), :] = v
            if b != 1 and a == 1:
                (bl if b == 0 else br)[s, :BLK, :] = v
                (bl if b == 0 else br)[s, BLK:, :] = tails[b // 2]
            if a == 0:
                du[s, span(b), :] = v
            if a == GB - 1:
                dd[s, span(b), :] = v


def decode_early(codes, own, yl, yr, xu, xd, adj, acc, ext):
    fill(ext, own, yl, yr, xu, xd)
    for j in range(GB * GB):
        total = early_sum(codes, adj, ext, j)
        for s in range(PAIR):
            acc[s, span(j), :] = total[:, span(s)]


def decode_late(own, acc, ml, mr, cu, cd, late, mown, region, w_region, w_out, hot, out):
    mids, ups, downs = (joined(ml, 0), joined(mr, 0)), (joined(cu, 0), joined(cu, 1)), (joined(cd, 0), joined(cd, 1))
    reach = jnp.concatenate([dot(region[:, span(s)], w_region[...]).astype(bf16) for s in range(PAIR)], axis=1)
    for j in range(GB * GB):
        rest = dot(mown[j], reach)
        if j % GB != 1:
            rest += late_sum(late, j, mids, ups, downs)
        extra = dot(hot[span(j), :], reach)
        for s in range(PAIR):
            second = (acc[s, span(j), :] + rest[:, span(s)]).astype(bf16)
            dec = (own[s, span(j), :].astype(f32) + extra[:, span(s)]).astype(bf16).astype(f32)
            out[s, span(j), :] = (dec + silu(dot(second, w_out[...]))).astype(bf16)


def late_kernel(codes, adj, late):
    for k, (j, code) in enumerate(LATE):
        total = jnp.zeros((BLK, BLK), f32)
        for n in range(NB):
            total += jnp.where(codes[j * NB + n] == code, adj[j, n].astype(f32), 0.0)
        late[k] = total.astype(bf16)


def owners_kernel(codes, adj, owners, mown, hot):
    ids = lax.broadcasted_iota(jnp.int32, (C, BLK), 0)
    for e in range(EXT * EXT):
        a, b = e // EXT, e % EXT
        if b in (0, EXT - 1):
            k = 32 + (b > 0) * TAIL + a
        elif a in (0, EXT - 1):
            k = 16 + (a > 0) * TAIL + b - 1
        else:
            k = (a - 1) * GB + b - 1
        row = owners[k : k + 1, :].astype(f32).astype(jnp.int32) - 1
        hot[span(e), :] = (ids == row).astype(f32).astype(bf16)
    for j in range(GB * GB):
        acc = jnp.zeros((BLK, C), f32)
        for n in range(NB):
            acc += lax.dot_general(
                adj[j, n], hot[ext_row(codes, j, n), :], (((1,), (1,)), ((), ())), preferred_element_type=f32
            )
        mown[j] = acc.astype(bf16)


def whole(shape):
    return pl.BlockSpec(shape, lambda p, *_: (0,) * len(shape), pipeline_mode=pl.Buffered(1))


def by_step(rows):
    return pl.BlockSpec((PAIR, rows, C), lambda p, *_: (p, 0, 0))


def by_lane(rows):
    return pl.BlockSpec((rows, WIDE), lambda p, *_: (0, p))


def call(kernel, name, steps, args, specs, outs, out_specs, scratch, flops, prefetch=0, exps=0):
    size = lambda v: v.size * v.dtype.itemsize
    return pl.pallas_call(
        kernel,
        grid_spec=pltpu.PrefetchScalarGridSpec(
            num_scalar_prefetch=prefetch, grid=(steps // PAIR,), in_specs=specs, out_specs=out_specs, scratch_shapes=scratch
        ),
        out_shape=outs,
        compiler_params=pltpu.CompilerParams(vmem_limit_bytes=VMEM << 20, dimension_semantics=("arbitrary",)),
        name=name,
        cost_estimate=pl.CostEstimate(
            flops=flops, bytes_accessed=sum(map(size, args)) + sum(map(size, outs)), transcendentals=exps
        ),
    )(*args)


VMEM = 28
TAIL = 8


def sds(shape, dtype=bf16):
    return jax.ShapeDtypeStruct(shape, dtype)


def shift(block, axis, up):
    count = lax.axis_size(axis)
    pairs = [(i, i + 1) for i in range(count - 1)]
    return lax.ppermute(block, axis, pairs if up else [(b, a) for a, b in pairs])


def corners(yl, yr):
    cu = shift(jnp.concatenate([yl[:, BLK:], yr[:, BLK:]], axis=1), "rx", True)
    cd = shift(jnp.concatenate([yl[:, :BLK], yr[:, :BLK]], axis=1), "rx", False)
    return cu, cd


def with_owners(block, owners):
    rows = jnp.broadcast_to(jnp.pad(owners, ((0, TAIL - GB), (0, 0)))[None], (block.shape[0], TAIL, C))
    return jnp.concatenate([block, rows], axis=1)


def on_device(noisy_input, adjacency, neighbours, norm_gain, w_mix, pool_weight, cluster, owner_ids, w_coarse, w_region, w_out):
    steps = noisy_input.shape[1]
    x = noisy_input.transpose(1, 0, 2)
    codes = neighbours.reshape(-1)
    crows = owner_ids.shape[0]
    devices = lax.axis_size("rx") * lax.axis_size("ry")
    squares = x.reshape(steps, GB, GB, BLK, C)
    flat = lambda v: v.reshape(steps, -1, C)
    work = steps * ROWS * C * 2

    owner = owner_ids[:, 0]
    coarse = jnp.arange(crows, dtype=jnp.int32)
    ids = jnp.arange(devices, dtype=jnp.int32)
    hit = cluster[None, :] == coarse[:, None]
    node_owner = jnp.sum(jnp.where(hit, owner[:, None], 0), axis=0)
    owners = (node_owner + 1).astype(bf16).reshape(GB * GB, BLK)

    yl = shift(flat(squares[:, ::2, GB - 1]), "ry", True)
    yr = shift(flat(squares[:, ::2, 0]), "ry", False)
    xu = shift(with_owners(flat(squares[:, GB - 1]), owners[-GB:]), "rx", True)
    xd = shift(with_owners(flat(squares[:, 0]), owners[:GB]), "rx", False)
    ml = shift(flat(squares[:, 1, GB - 1]), "ry", True)
    right = flat(squares[:, 1, 0])
    right, xu = lax.optimization_barrier((right, xu))
    mr = shift(right, "ry", False)
    pool = jnp.where(hit, pool_weight[None, :], jnp.zeros((), bf16))
    unpool = (cluster[:, None] == coarse[None, :]).astype(bf16)
    spread = (owner[None, :] == ids[:, None]).astype(bf16)
    hot = (node_owner[:, None] == ids[None, :]).astype(bf16)
    column = lambda b: jnp.concatenate([xu[0, SIDE + b : SIDE + b + 1], owners[b::GB], xd[0, SIDE + b : SIDE + b + 1]])
    tails = jnp.pad(jnp.stack([column(0), column(GB - 1)]), ((0, 0), (0, TAIL - EXT), (0, 0)))
    tops = jnp.stack([xu[0, SIDE:], xd[0, SIDE:]])
    gain = norm_gain.reshape(1, C)
    ext = pltpu.VMEM((EXT * EXT * BLK, WIDE), bf16)
    square = (BLK, C)

    (late,) = call(late_kernel, "late_weights", PAIR, [codes, adjacency], [whole(adjacency.shape)],
                   [sds((len(LATE),) + square)], [whole((len(LATE),) + square)], [], 1 << 20, prefetch=1)
    cu, cd = corners(yl, yr)
    xu, xd, late, pool, unpool, spread, hot, tails, tops = lax.optimization_barrier((xu, xd, late, pool, unpool, spread, hot, tails, tops))
    early = lambda: [by_step(ROWS)] + [by_step(v.shape[1]) for v in (yl, yr, xu, xd)] + [whole(adjacency.shape)]
    acc, mid = call(
        encode_early, "encode_early", steps, [codes, x, yl, yr, xu, xd, adjacency, gain, w_mix],
        early() + [whole((1, C)), whole(square)],
        [sds((steps, 2 * SIDE, C), f32), sds((steps, SIDE, C))], [by_step(2 * SIDE), by_step(SIDE)], [ext],
        work * (NB * BLK + C // 3), prefetch=1, exps=work // 6)
    halo = lambda: [by_step(v.shape[1]) for v in (ml, mr, cu, cd)] + [whole(late.shape)]
    d1, al, ar, bl, br, du, dd, part = call(
        encode_late, "encode_late", steps,
        [x, acc, mid, ml, mr, cu, cd, late, gain, w_mix, w_coarse, pool, unpool, spread, tails],
        [by_step(ROWS), by_step(2 * SIDE), by_step(SIDE)] + halo()
        + [whole((1, C)), whole(square), whole(square), whole(pool.shape), whole(unpool.shape), whole(spread.shape), whole(tails.shape)],
        [sds((steps, r, C)) for r in (ROWS, 2 * BLK, 2 * BLK, BLK + TAIL, BLK + TAIL, SIDE, SIDE)] + [sds((devices, steps * C))],
        [by_step(r) for r in (ROWS, 2 * BLK, 2 * BLK, BLK + TAIL, BLK + TAIL, SIDE, SIDE)] + [by_lane(devices)],
        [pltpu.VMEM((ROWS, WIDE), bf16)], work * (C + 3 * crows), exps=work // 3)

    yl = shift(ar, "ry", True)
    yr = shift(al, "ry", False)
    xu = shift(dd, "rx", True)
    xd = shift(du, "rx", False)
    ml = shift(br, "ry", True)
    bl, xu = lax.optimization_barrier((bl, xu))
    mr = shift(bl, "ry", False)
    half = (devices, 2, steps * C // 2)
    arrived = lax.all_to_all(part.reshape(half), ("rx", "ry"), split_axis=0, concat_axis=0, tiled=True)
    region = (jnp.sum(arrived.astype(f32), axis=0, keepdims=True) / float(crows)).astype(bf16)
    region = lax.all_to_all(jnp.broadcast_to(region, half), ("rx", "ry"), split_axis=0, concat_axis=0, tiled=True)
    region = region.reshape(devices, steps * C)
    cu, cd = corners(yl, yr)
    owners = jnp.concatenate([owners, jnp.zeros((16 - GB * GB, BLK), bf16), tops[0], tops[1], ml[0, BLK:], mr[0, BLK:]])
    (mown,) = call(owners_kernel, "owner_mix", PAIR, [codes, adjacency, owners], [whole(adjacency.shape), whole(owners.shape)],
                   [sds((GB * GB,) + square)], [whole((GB * GB,) + square)],
                   [pltpu.VMEM((EXT * EXT * BLK, C), bf16)], GB * GB * NB * 2 * BLK**3, prefetch=1)
    (acc,) = call(decode_early, "decode_early", steps, [codes, d1, yl, yr, xu, xd, adjacency], early(),
                  [sds((steps, ROWS, C), f32)], [by_step(ROWS)], [ext], work * NB * BLK, prefetch=1)
    (out,) = call(
        decode_late, "decode_late", steps, [d1, acc, ml, mr, cu, cd, late, mown, region, w_region, w_out, hot],
        [by_step(ROWS)] * 2 + halo()
        + [whole(mown.shape), by_lane(devices), whole(square), whole(square), whole(hot.shape)],
        [sds((steps, ROWS, C))], [by_step(ROWS)], [], work * 3 * C, exps=work // 2)
    return out.transpose(1, 0, 2)


def solution(mesh):
    nodes = P(("rx", "ry"))
    in_specs = (
        P(("rx", "ry"), None, None),
        P(("rx", "ry"), None, None, None),
        P(("rx", "ry"), None),
        P(),
        P(),
        nodes,
        nodes,
        P(("rx", "ry"), None),
        P(),
        P(),
        P(),
    )
    out_specs = P(("rx", "ry"), None, None)
    return jax.shard_map(on_device, mesh=mesh, in_specs=in_specs, out_specs=out_specs, check_vma=False)
```

profile of v0, /device:TPU:1, one launch (start us, length us, event | category | flops | bytes accessed | tf_op | source)
XLA Modules:
  0.0 167.1 jit_solution(204608291917057209)
XLA Ops:
  0.9 1.8 %fusion.8 = (bf16[12,1,3,128,128]{4,3,2,1,0:T(8,128)(2,1)S(1)}, bf16[12,1,3,128,128]{4,3,2,1,0:T(8,128)(2,1)S(1)}) fusion(bf16[12,3,3,128,128]{4,3,2,1,0:T(8,128)(2,1)} %bitcast.48), kind=kLoop, calls=%fused_computation.38 | loop fusion | bytes 4718592 | tf_op jit(solution)/shard_map/slice | solution.py:256
  2.8 1.1 pad_maximum_fusion
  3.9 4.6 %collective-permute-start.2 = (bf16[12,392,128]{2,1,0:T(8,128)(2,1)}, bf16[12,392,128]{2,1,0:T(8,128)(2,1)}, u32[]{:S(2)}, u32[]{:S(2)}) collective-permute-start(bf16[12,392,128]{2,1,0:T(8,128)(2,1)} %pad_maximum_fusion), channel_id=1, source_target_pairs={{0,16},{16,32},{32,48},{48,64},{64,80},{80,96},{96,112},{1,17},{17... | collective-permute-start | bytes 3612680 | tf_op jit(solution)/shard_map/ppermute | solution.py:222
  8.6 1.1 pad_maximum_fusion.1
  9.7 1.9 %collective-permute-start.3 = (bf16[12,392,128]{2,1,0:T(8,128)(2,1)}, bf16[12,392,128]{2,1,0:T(8,128)(2,1)}, u32[]{:S(2)}, u32[]{:S(2)}) collective-permute-start(bf16[12,392,128]{2,1,0:T(8,128)(2,1)} %pad_maximum_fusion.1), channel_id=1, source_target_pairs={{16,0},{32,16},{48,32},{64,48},{80,64},{96,80},{112,96},{17,1},{33... | collective-permute-start | bytes 3612680 | tf_op jit(solution)/shard_map/ppermute | solution.py:222
  11.6 1.3 fusion.9
  12.9 4.2 %collective-permute-start = (bf16[12,256,128]{2,1,0:T(8,128)(2,1)}, bf16[12,256,128]{2,1,0:T(8,128)(2,1)}, u32[]{:S(2)}, u32[]{:S(2)}) collective-permute-start(bf16[12,256,128]{2,1,0:T(8,128)(2,1)} %bitcast.2), channel_id=1, source_target_pairs={{0,1},{1,2},{2,3},{3,4},{4,5},{5,6},{6,7},{7,8},{8,9},{9,10},{10,1... | collective-permute-start | bytes 2359304 | tf_op jit(solution)/shard_map/ppermute | solution.py:222
  17.1 1.3 collective-permute-start.1
  18.4 1.0 slice_bitcast_fusion
  19.4 4.8 %collective-permute-start.4 = (bf16[12,128,128]{2,1,0:T(8,128)(2,1)}, bf16[12,128,128]{2,1,0:T(8,128)(2,1)}, u32[]{:S(2)}, u32[]{:S(2)}) collective-permute-start(bf16[12,128,128]{2,1,0:T(8,128)(2,1)} %get-tuple-element.51), channel_id=1, source_target_pairs={{0,1},{1,2},{2,3},{3,4},{4,5},{5,6},{6,7},{7,8},{8,9},{9,10},{10,1... | collective-permute-start | bytes 1179656 | tf_op jit(solution)/shard_map/ppermute | solution.py:222
  24.2 1.0 fusion.unpool
  26.0 1.0 fusion.2.hot
  28.3 1.5 copy-done.3
  29.8 0.9 late_weights.1.late
  31.5 2.3 %collective-permute-done.yl = bf16[12,256,128]{2,1,0:T(8,128)(2,1)} collective-permute-done((bf16[12,256,128]{2,1,0:T(8,128)(2,1)}, bf16[12,256,128]{2,1,0:T(8,128)(2,1)}, u32[]{:S(2)}, u32[]{:S(2)}) %collective-permute-start) | collective-permute-done | bytes 786464 | tf_op jit(solution)/shard_map/ppermute | solution.py:222
  33.8 1.2 fusion.12
  35.0 3.7 %collective-permute-done.1.yr = bf16[12,256,128]{2,1,0:T(8,128)(2,1)} collective-permute-done((bf16[12,256,128]{2,1,0:T(8,128)(2,1)}, bf16[12,256,128]{2,1,0:T(8,128)(2,1)}, u32[]{:S(2)}, u32[]{:S(2)}) %collective-permute-start.1) | collective-permute-done | bytes 786464 | tf_op jit(solution)/shard_map/ppermute | solution.py:222
  38.7 1.2 fusion.13
  40.0 3.7 %collective-permute-start.6 = (bf16[12,256,128]{2,1,0:T(8,128)(2,1)S(1)}, bf16[12,256,128]{2,1,0:T(8,128)(2,1)S(1)}, u32[]{:S(2)}, u32[]{:S(2)}) collective-permute-start(bf16[12,256,128]{2,1,0:T(8,128)(2,1)S(1)} %pad_maximum_fusion.2), channel_id=1, source_target_pairs={{0,16},{16,32},{32,48},{48,64},{64,80},{80,96},{96,112},{1,17},{17... | collective-permute-start | bytes 2359304 | tf_op jit(solution)/shard_map/ppermute | solution.py:222
  43.8 1.9 %collective-permute-start.7 = (bf16[12,256,128]{2,1,0:T(8,128)(2,1)S(1)}, bf16[12,256,128]{2,1,0:T(8,128)(2,1)S(1)}, u32[]{:S(2)}, u32[]{:S(2)}) collective-permute-start(bf16[12,256,128]{2,1,0:T(8,128)(2,1)S(1)} %pad_maximum_fusion.3), channel_id=1, source_target_pairs={{16,0},{32,16},{48,32},{64,48},{80,64},{96,80},{112,96},{17,1},{33... | collective-permute-start | bytes 2359304 | tf_op jit(solution)/shard_map/ppermute | solution.py:222
  45.7 1.3 collective-permute-start.5
  50.6 10.8 %encode_early.1 = (f32[12,768,128]{2,1,0:T(8,128)S(1)}, bf16[12,384,128]{2,1,0:T(8,128)(2,1)S(1)}) custom-call(s32[54]{0:T(128)S(1)} %reshape.43.codes, bf16[12,1152,128]{2,1,0:T(8,128)(2,1)S(1)} %bitcast.51, bf16[12,256,128]{2,1,0:T(8,128)(2,1)} %collective-permute-done.yl, bf16[12,256,128]{2,1,0:T(8,128)(2,1)} %collective-permute-done.1.yr, ...), custom_call_target="tpu_custom_call" | custom-call | flops 2866544640 | bytes 15221464 | tf_op jit(solution)/shard_map/encode_early/pallas_call | solution.py:197
  61.5 11.3 %encode_late.1 = (bf16[12,1152,128]{2,1,0:T(8,128)(2,1)S(1)}, bf16[12,256,128]{2,1,0:T(8,128)(2,1)S(1)}, bf16[12,256,128]{2,1,0:T(8,128)(2,1)}, bf16[12,136,128]...) custom-call(bf16[12,1152,128]{2,1,0:T(8,128)(2,1)S(1)} %bitcast.52, ...), custom_call_target="tpu_custom_call" | custom-call | flops 1981808640 | bytes 21594624 | tf_op jit(solution)/shard_map/encode_late/pallas_call | solution.py:197
  72.8 1.8 %copy-done.5 = bf16[12,1152,128]{2,1,0:T(8,128)(2,1)} copy-done((bf16[12,1152,128]{2,1,0:T(8,128)(2,1)}, bf16[12,1152,128]{2,1,0:T(8,128)(2,1)S(1)}, u32[]{:S(2)}) %copy-start.5) | copy-done | bytes 3538968
  76.2 4.2 %collective-permute-start.8 = (bf16[12,256,128]{2,1,0:T(8,128)(2,1)}, bf16[12,256,128]{2,1,0:T(8,128)(2,1)S(1)}, u32[]{:S(2)}, u32[]{:S(2)}) collective-permute-start(bf16[12,256,128]{2,1,0:T(8,128)(2,1)} %get-tuple-element.40), channel_id=1, source_target_pairs={{0,1},{1,2},{2,3},{3,4},{4,5},{5,6},{6,7},{7,8},{8,9},{9,10},{10,1... | collective-permute-start | bytes 2359304 | tf_op jit(solution)/shard_map/ppermute | solution.py:222
  80.3 1.8 %reshape.47 = bf16[128,2,768]{2,1,0:T(2,128)(2,1)} reshape(bf16[128,1536]{1,0:T(8,128)(2,1)} %copy-done.14) | data formatting | bytes 786432 | tf_op jit(solution)/shard_map/reshape | solution.py:300
  82.2 13.6 %all-to-all-start = ((bf16[128,2,768]{2,1,0:T(2,128)(2,1)}), bf16[128,2,768]{2,1,0:T(2,128)(2,1)S(1)}, u32[]{:S(2)}, u32[]{:S(2)}) async-start(bf16[128,2,768]{2,1,0:T(2,128)(2,1)} %reshape.47), calls=%async_computation | async-start | bytes 786432 | tf_op jit(solution)/shard_map/all_to_all | solution.py:300
  95.8 1.3 collective-permute-start.9
  97.1 3.5 %collective-permute-start.10 = (bf16[12,384,128]{2,1,0:T(8,128)(2,1)}, bf16[12,384,128]{2,1,0:T(8,128)(2,1)}, u32[]{:S(2)}, u32[]{:S(2)}) collective-permute-start(bf16[12,384,128]{2,1,0:T(8,128)(2,1)} %get-tuple-element.43), channel_id=1, source_target_pairs={{0,16},{16,32},{32,48},{48,64},{64,80},{80,96},{96,112},{1,17},{17... | collective-permute-start | bytes 3538952 | tf_op jit(solution)/shard_map/ppermute | solution.py:222
  100.6 5.0 %collective-permute-start.12 = (bf16[12,136,128]{2,1,0:T(8,128)(2,1)}, bf16[12,136,128]{2,1,0:T(8,128)(2,1)}, u32[]{:S(2)}, u32[]{:S(2)}) collective-permute-start(bf16[12,136,128]{2,1,0:T(8,128)(2,1)} %get-tuple-element.46), channel_id=1, source_target_pairs={{0,1},{1,2},{2,3},{3,4},{4,5},{5,6},{6,7},{7,8},{8,9},{9,10},{10,1... | collective-permute-start | bytes 1253384 | tf_op jit(solution)/shard_map/ppermute | solution.py:222
  105.7 2.0 %collective-permute-start.11 = (bf16[12,384,128]{2,1,0:T(8,128)(2,1)}, bf16[12,384,128]{2,1,0:T(8,128)(2,1)}, u32[]{:S(2)}, u32[]{:S(2)}) collective-permute-start(bf16[12,384,128]{2,1,0:T(8,128)(2,1)} %get-tuple-element.45), channel_id=1, source_target_pairs={{16,0},{32,16},{48,32},{64,48},{80,64},{96,80},{112,96},{17,1},{33... | collective-permute-start | bytes 3538952 | tf_op jit(solution)/shard_map/ppermute | solution.py:222
  107.7 3.2 %all-to-all-done = bf16[128,2,768]{2,1,0:T(2,128)(2,1)S(1)} async-done(((bf16[128,2,768]{2,1,0:T(2,128)(2,1)}), bf16[128,2,768]{2,1,0:T(2,128)(2,1)S(1)}, u32[]{:S(2)}, u32[]{:S(2)}) %all-to-all-start) | async-done | bytes 393248 | tf_op jit(solution)/shard_map/all_to_all | solution.py:300
  111.2 1.0 broadcast_in_dim.63
  112.2 8.1 %all-to-all-start.1 = ((bf16[128,2,768]{2,1,0:T(2,128)(2,1)}), bf16[128,2,768]{2,1,0:T(2,128)(2,1)}, u32[]{:S(2)}, u32[]{:S(2)}) async-start(bf16[128,2,768]{2,1,0:T(2,128)(2,1)} %broadcast_in_dim.63), calls=%async_computation.1 | async-start | bytes 786432 | tf_op jit(solution)/shard_map/all_to_all | solution.py:302
  120.5 0.9 pad_maximum_fusion.5
  121.4 3.2 %collective-permute-start.15 = (bf16[12,256,128]{2,1,0:T(8,128)(2,1)}, bf16[12,256,128]{2,1,0:T(8,128)(2,1)}, u32[]{:S(2)}, u32[]{:S(2)}) collective-permute-start(bf16[12,256,128]{2,1,0:T(8,128)(2,1)} %pad_maximum_fusion.5), channel_id=1, source_target_pairs={{16,0},{32,16},{48,32},{64,48},{80,64},{96,80},{112,96},{17,1},{33... | collective-permute-start | bytes 2359304 | tf_op jit(solution)/shard_map/ppermute | solution.py:222
  124.6 1.0 pad_maximum_fusion.4
  125.6 2.5 %collective-permute-start.14 = (bf16[12,256,128]{2,1,0:T(8,128)(2,1)}, bf16[12,256,128]{2,1,0:T(8,128)(2,1)}, u32[]{:S(2)}, u32[]{:S(2)}) collective-permute-start(bf16[12,256,128]{2,1,0:T(8,128)(2,1)} %pad_maximum_fusion.4), channel_id=1, source_target_pairs={{0,16},{16,32},{32,48},{48,64},{64,80},{80,96},{96,112},{1,17},{17... | collective-permute-start | bytes 2359304 | tf_op jit(solution)/shard_map/ppermute | solution.py:222
  128.1 1.5 collective-permute-start.13
  130.2 3.2 %all-to-all-done.1 = bf16[128,2,768]{2,1,0:T(2,128)(2,1)} async-done(((bf16[128,2,768]{2,1,0:T(2,128)(2,1)}), bf16[128,2,768]{2,1,0:T(2,128)(2,1)}, u32[]{:S(2)}, u32[]{:S(2)}) %all-to-all-start.1) | async-done | bytes 393248 | tf_op jit(solution)/shard_map/all_to_all | solution.py:302
  133.4 1.8 %copy.22 = bf16[16,8,2,768]{3,1,2,0:T(8,128)(2,1)} copy(bf16[16,8,2,768]{3,2,1,0:T(2,128)(2,1)} %bitcast.29) | data formatting | bytes 786432
  135.2 2.0 %copy-done.6 = bf16[12,1152,128]{2,1,0:T(8,128)(2,1)S(1)} copy-done((bf16[12,1152,128]{2,1,0:T(8,128)(2,1)S(1)}, bf16[12,1152,128]{2,1,0:T(8,128)(2,1)}, u32[]{:S(2)}) %copy-start.6) | copy-done | bytes 3538968
  137.2 7.5 %decode_early.1.acc = f32[12,1152,128]{2,1,0:T(8,128)S(1)} custom-call(s32[54]{0:T(128)S(1)} %reshape.43.codes, bf16[12,1152,128]{2,1,0:T(8,128)(2,1)S(1)} %copy-done.6, bf16[12,256,128]{2,1,0:T(8,128)(2,1)S(1)} %collective-permute-done.8.yl, bf16[12,256,128]{2,1,0:T(8,128)(2,1)S(1)} %collective-permute-done.9.yr, ...), custom_call_target="tpu_custom_call" | custom-call | flops 2717908992 | bytes 16318680 | tf_op jit(solution)/shard_map/decode_early/pallas_call | solution.py:197
  144.7 2.8 %copy-done = f32[12,1152,128]{2,1,0:T(8,128)} copy-done((f32[12,1152,128]{2,1,0:T(8,128)}, f32[12,1152,128]{2,1,0:T(8,128)S(1)}, u32[]{:S(2)}) %copy-start) | copy-done | bytes 7077912
  148.4 2.0 %owner_mix.1.mown = bf16[9,128,128]{2,1,0:T(8,128)(2,1)S(1)} custom-call(s32[54]{0:T(128)S(1)} %reshape.43.codes, bf16[9,6,128,128]{3,2,1,0:T(8,128)(2,1)S(1)} %copy-done.4, bf16[48,128]{1,0:T(8,128)(2,1)S(1)} %concatenate.35.owners), custom_call_target="tpu_custom_call" | custom-call | flops 226492416 | bytes 2076888 | tf_op jit(solution)/shard_map/owner_mix/pallas_call | solution.py:197
  150.6 3.0 %copy-done.1 = f32[12,1152,128]{2,1,0:T(8,128)S(1)} copy-done((f32[12,1152,128]{2,1,0:T(8,128)S(1)}, f32[12,1152,128]{2,1,0:T(8,128)}, u32[]{:S(2)}) %copy-start.1) | copy-done | bytes 7077912
  153.6 2.0 %copy-done.7 = bf16[12,1152,128]{2,1,0:T(8,128)(2,1)S(1)} copy-done((bf16[12,1152,128]{2,1,0:T(8,128)(2,1)S(1)}, bf16[12,1152,128]{2,1,0:T(8,128)(2,1)}, u32[]{:S(2)}) %copy-start.7) | copy-done | bytes 3538968
  155.6 11.5 %decode_late.1 = bf16[12,1152,128]{2,1,0:T(8,128)(2,1)} custom-call(bf16[12,1152,128]{2,1,0:T(8,128)(2,1)S(1)} %copy-done.7, f32[12,1152,128]{2,1,0:T(8,128)S(1)} %copy-done.1, bf16[12,136,128]{2,1,0:T(8,128)(2,1)} %collective-permute-done.12.ml, bf16[12,136,128]{2,1,0:T(8,128)(2,1)} %collective-permute-done.13.mr, ...), custom_call_target="tpu_custom_call" | custom-call | flops 1358954496 | bytes 17940480 | tf_op jit(solution)/shard_map/decode_late/pallas_call | solution.py:197
  (100 shorter events, 11.2 us)
Async XLA Ops:
  2.7 5.8 %copy-start.29 = (pred[8]{0:T(512)(128)(4,1)S(1)}, pred[8]{0:T(512)(128)(4,1)}, u32[]{:S(2)}) copy-start(pred[8]{0:T(512)(128)(4,1)} %constant.12.clone.1) | copy-start | bytes 28
  2.7 8.9 %copy-start.2 = (bf16[1152,12,128]{2,0,1:T(8,128)(2,1)S(1)}, bf16[1152,12,128]{2,0,1:T(8,128)(2,1)}, u32[]{:S(2)}) copy-start(bf16[1152,12,128]{2,0,1:T(8,128)(2,1)} %param.11) | copy-start | bytes 10616836
  3.9 41.9 %collective-permute-start.2 = (bf16[12,392,128]{2,1,0:T(8,128)(2,1)}, bf16[12,392,128]{2,1,0:T(8,128)(2,1)}, u32[]{:S(2)}, u32[]{:S(2)}) collective-permute-start(bf16[12,392,128]{2,1,0:T(8,128)(2,1)} %pad_maximum_fusion), channel_id=1, source_target_pairs={{0,16},{16,32},{32,48},{48,64},{64,80},{80,96},{96,112},{1,17},{17... | collective-permute-start | bytes 3612680 | tf_op jit(solution)/shard_map/ppermute | solution.py:222
  9.7 38.1 %collective-permute-start.3 = (bf16[12,392,128]{2,1,0:T(8,128)(2,1)}, bf16[12,392,128]{2,1,0:T(8,128)(2,1)}, u32[]{:S(2)}, u32[]{:S(2)}) collective-permute-start(bf16[12,392,128]{2,1,0:T(8,128)(2,1)} %pad_maximum_fusion.1), channel_id=1, source_target_pairs={{16,0},{32,16},{48,32},{64,48},{80,64},{96,80},{112,96},{17,1},{33... | collective-permute-start | bytes 3612680 | tf_op jit(solution)/shard_map/ppermute | solution.py:222
  12.9 11.3 %copy-start.23 = (s32[1152]{0:T(1024)S(1)}, s32[1152]{0:T(1024)}, u32[]{:S(2)}) copy-start(s32[1152]{0:T(1024)} %param.17) | copy-start | bytes 13828
  12.9 12.3 %copy-start.25 = (bf16[1152]{0:T(1024)(128)(2,1)S(1)}, bf16[1152]{0:T(1024)(128)(2,1)}, u32[]{:S(2)}) copy-start(bf16[1152]{0:T(1024)(128)(2,1)} %param.16) | copy-start | bytes 6916
  12.9 15.2 %copy-start.26 = (s32[9,6]{0,1:T(8,128)S(1)}, s32[9,6]{0,1:T(8,128)}, u32[]{:S(2)}) copy-start(s32[9,6]{0,1:T(8,128)} %param.13) | copy-start | bytes 652
  12.9 20.9 %collective-permute-start = (bf16[12,256,128]{2,1,0:T(8,128)(2,1)}, bf16[12,256,128]{2,1,0:T(8,128)(2,1)}, u32[]{:S(2)}, u32[]{:S(2)}) collective-permute-start(bf16[12,256,128]{2,1,0:T(8,128)(2,1)} %bitcast.2), channel_id=1, source_target_pairs={{0,1},{1,2},{2,3},{3,4},{4,5},{5,6},{6,7},{7,8},{8,9},{9,10},{10,1... | collective-permute-start | bytes 2359304 | tf_op jit(solution)/shard_map/ppermute | solution.py:222
  17.1 21.6 %collective-permute-start.1 = (bf16[12,256,128]{2,1,0:T(8,128)(2,1)}, bf16[12,256,128]{2,1,0:T(8,128)(2,1)}, u32[]{:S(2)}, u32[]{:S(2)}) collective-permute-start(bf16[12,256,128]{2,1,0:T(8,128)(2,1)} %bitcast.4), channel_id=1, source_target_pairs={{1,0},{2,1},{3,2},{4,3},{5,4},{6,5},{7,6},{8,7},{9,8},{10,9},{11,1... | collective-permute-start | bytes 2359304 | tf_op jit(solution)/shard_map/ppermute | solution.py:222
  19.4 42.0 %collective-permute-start.4 = (bf16[12,128,128]{2,1,0:T(8,128)(2,1)}, bf16[12,128,128]{2,1,0:T(8,128)(2,1)}, u32[]{:S(2)}, u32[]{:S(2)}) collective-permute-start(bf16[12,128,128]{2,1,0:T(8,128)(2,1)} %get-tuple-element.51), channel_id=1, source_target_pairs={{0,1},{1,2},{2,3},{3,4},{4,5},{5,6},{6,7},{7,8},{8,9},{9,10},{10,1... | collective-permute-start | bytes 1179656 | tf_op jit(solution)/shard_map/ppermute | solution.py:222
  28.3 1.5 copy-start.3
  30.7 30.7 %copy-start.8 = (bf16[10,128,128]{2,1,0:T(8,128)(2,1)}, bf16[10,128,128]{2,1,0:T(8,128)(2,1)S(1)}, u32[]{:S(2)}) copy-start(bf16[10,128,128]{2,1,0:T(8,128)(2,1)S(1)} %late_weights.1.late) | copy-start | bytes 983044
  39.9 5.9 %copy-start.22 = (bf16[12,128,128]{2,1,0:T(8,128)(2,1)S(1)}, bf16[12,128,128]{2,1,0:T(8,128)(2,1)}, u32[]{:S(2)}) copy-start(bf16[12,128,128]{2,1,0:T(8,128)(2,1)} %get-tuple-element.33) | copy-start | bytes 1179652
  39.9 8.7 %copy-start.27 = (bf16[3,128]{1,0:T(4,128)(2,1)S(1)}, bf16[3,128]{1,0:T(4,128)(2,1)}, u32[]{:S(2)}) copy-start(bf16[3,128]{1,0:T(4,128)(2,1)} %slice.102) | copy-start | bytes 2308
  39.9 8.7 %copy-start.28 = (bf16[3,128]{1,0:T(4,128)(2,1)S(1)}, bf16[3,128]{1,0:T(4,128)(2,1)}, u32[]{:S(2)}) copy-start(bf16[3,128]{1,0:T(4,128)(2,1)} %slice.105) | copy-start | bytes 2308
  39.9 10.6 %copy-start.15 = (bf16[128,128]{1,0:T(8,128)(2,1)S(1)}, bf16[128,128]{1,0:T(8,128)(2,1)}, u32[]{:S(2)}) copy-start(bf16[128,128]{1,0:T(8,128)(2,1)} %w_mix.3) | copy-start | bytes 98308
  39.9 10.6 %copy-start.19 = (f32[128]{0:T(128)S(1)}, f32[128]{0:T(128)}, u32[]{:S(2)}) copy-start(f32[128]{0:T(128)} %param.14) | copy-start | bytes 1540
  40.0 21.4 %collective-permute-start.6 = (bf16[12,256,128]{2,1,0:T(8,128)(2,1)S(1)}, bf16[12,256,128]{2,1,0:T(8,128)(2,1)S(1)}, u32[]{:S(2)}, u32[]{:S(2)}) collective-permute-start(bf16[12,256,128]{2,1,0:T(8,128)(2,1)S(1)} %pad_maximum_fusion.2), channel_id=1, source_target_pairs={{0,16},{16,32},{32,48},{48,64},{64,80},{80,96},{96,112},{1,17},{17... | collective-permute-start | bytes 2359304 | tf_op jit(solution)/shard_map/ppermute | solution.py:222
  43.8 17.6 %collective-permute-start.7 = (bf16[12,256,128]{2,1,0:T(8,128)(2,1)S(1)}, bf16[12,256,128]{2,1,0:T(8,128)(2,1)S(1)}, u32[]{:S(2)}, u32[]{:S(2)}) collective-permute-start(bf16[12,256,128]{2,1,0:T(8,128)(2,1)S(1)} %pad_maximum_fusion.3), channel_id=1, source_target_pairs={{16,0},{32,16},{48,32},{64,48},{80,64},{96,80},{112,96},{17,1},{33... | collective-permute-start | bytes 2359304 | tf_op jit(solution)/shard_map/ppermute | solution.py:222
  45.7 15.7 %collective-permute-start.5 = (bf16[12,128,128]{2,1,0:T(8,128)(2,1)S(1)}, bf16[12,128,128]{2,1,0:T(8,128)(2,1)S(1)}, u32[]{:S(2)}, u32[]{:S(2)}) collective-permute-start(bf16[12,128,128]{2,1,0:T(8,128)(2,1)S(1)} %copy-done.22), channel_id=1, source_target_pairs={{1,0},{2,1},{3,2},{4,3},{5,4},{6,5},{7,6},{8,7},{9,8},{10,9},{11,1... | collective-permute-start | bytes 1179656 | tf_op jit(solution)/shard_map/ppermute | solution.py:222
  50.5 10.9 %copy-start.10 = (bf16[1152,144]{1,0:T(8,128)(2,1)S(1)}, bf16[1152,144]{1,0:T(8,128)(2,1)}, u32[]{:S(2)}) copy-start(bf16[1152,144]{1,0:T(8,128)(2,1)} %fusion.unpool) | copy-start | bytes 995332
  50.5 10.9 %copy-start.12 = (bf16[144,1152]{1,0:T(8,128)(2,1)S(1)}, bf16[144,1152]{1,0:T(8,128)(2,1)}, u32[]{:S(2)}) copy-start(bf16[144,1152]{1,0:T(8,128)(2,1)} %fusion.1.pool) | copy-start | bytes 995332
  50.5 10.9 %copy-start.16 = (bf16[128,128]{1,0:T(8,128)(2,1)S(1)}, bf16[128,128]{1,0:T(8,128)(2,1)}, u32[]{:S(2)}) copy-start(bf16[128,128]{1,0:T(8,128)(2,1)} %w_coarse.1) | copy-start | bytes 98308
  72.8 1.8 %copy-start.5 = (bf16[12,1152,128]{2,1,0:T(8,128)(2,1)}, bf16[12,1152,128]{2,1,0:T(8,128)(2,1)S(1)}, u32[]{:S(2)}) copy-start(bf16[12,1152,128]{2,1,0:T(8,128)(2,1)S(1)} %get-tuple-element.39.own) | copy-start | bytes 10616836
  74.6 0.7 copy-start.14
  75.3 0.9 copy-start.20
  76.2 19.6 %copy-start.21 = (bf16[12,256,128]{2,1,0:T(8,128)(2,1)S(1)}, bf16[12,256,128]{2,1,0:T(8,128)(2,1)}, u32[]{:S(2)}) copy-start(bf16[12,256,128]{2,1,0:T(8,128)(2,1)} %copy-done.20) | copy-start | bytes 2359300
  76.2 44.2 %collective-permute-start.8 = (bf16[12,256,128]{2,1,0:T(8,128)(2,1)}, bf16[12,256,128]{2,1,0:T(8,128)(2,1)S(1)}, u32[]{:S(2)}, u32[]{:S(2)}) collective-permute-start(bf16[12,256,128]{2,1,0:T(8,128)(2,1)} %get-tuple-element.40), channel_id=1, source_target_pairs={{0,1},{1,2},{2,3},{3,4},{4,5},{5,6},{6,7},{7,8},{8,9},{9,10},{10,1... | collective-permute-start | bytes 2359304 | tf_op jit(solution)/shard_map/ppermute | solution.py:222
  82.2 28.7 %all-to-all-start = ((bf16[128,2,768]{2,1,0:T(2,128)(2,1)}), bf16[128,2,768]{2,1,0:T(2,128)(2,1)S(1)}, u32[]{:S(2)}, u32[]{:S(2)}) async-start(bf16[128,2,768]{2,1,0:T(2,128)(2,1)} %reshape.47), calls=%async_computation | async-start | bytes 786432 | tf_op jit(solution)/shard_map/all_to_all | solution.py:300
  95.8 24.6 %collective-permute-start.9 = (bf16[12,256,128]{2,1,0:T(8,128)(2,1)S(1)}, bf16[12,256,128]{2,1,0:T(8,128)(2,1)S(1)}, u32[]{:S(2)}, u32[]{:S(2)}) collective-permute-start(bf16[12,256,128]{2,1,0:T(8,128)(2,1)S(1)} %copy-done.21), channel_id=1, source_target_pairs={{1,0},{2,1},{3,2},{4,3},{5,4},{6,5},{7,6},{8,7},{9,8},{10,9},{11,1... | collective-permute-start | bytes 2359304 | tf_op jit(solution)/shard_map/ppermute | solution.py:222
  97.1 31.0 %collective-permute-start.10 = (bf16[12,384,128]{2,1,0:T(8,128)(2,1)}, bf16[12,384,128]{2,1,0:T(8,128)(2,1)}, u32[]{:S(2)}, u32[]{:S(2)}) collective-permute-start(bf16[12,384,128]{2,1,0:T(8,128)(2,1)} %get-tuple-element.43), channel_id=1, source_target_pairs={{0,16},{16,32},{32,48},{48,64},{64,80},{80,96},{96,112},{1,17},{17... | collective-permute-start | bytes 3538952 | tf_op jit(solution)/shard_map/ppermute | solution.py:222
  100.6 29.0 %collective-permute-start.12 = (bf16[12,136,128]{2,1,0:T(8,128)(2,1)}, bf16[12,136,128]{2,1,0:T(8,128)(2,1)}, u32[]{:S(2)}, u32[]{:S(2)}) collective-permute-start(bf16[12,136,128]{2,1,0:T(8,128)(2,1)} %get-tuple-element.46), channel_id=1, source_target_pairs={{0,1},{1,2},{2,3},{3,4},{4,5},{5,6},{6,7},{7,8},{8,9},{9,10},{10,1... | collective-permute-start | bytes 1253384 | tf_op jit(solution)/shard_map/ppermute | solution.py:222
  105.7 29.6 %collective-permute-start.11 = (bf16[12,384,128]{2,1,0:T(8,128)(2,1)}, bf16[12,384,128]{2,1,0:T(8,128)(2,1)}, u32[]{:S(2)}, u32[]{:S(2)}) collective-permute-start(bf16[12,384,128]{2,1,0:T(8,128)(2,1)} %get-tuple-element.45), channel_id=1, source_target_pairs={{16,0},{32,16},{48,32},{64,48},{80,64},{96,80},{112,96},{17,1},{33... | collective-permute-start | bytes 3538952 | tf_op jit(solution)/shard_map/ppermute | solution.py:222
  112.2 21.2 %all-to-all-start.1 = ((bf16[128,2,768]{2,1,0:T(2,128)(2,1)}), bf16[128,2,768]{2,1,0:T(2,128)(2,1)}, u32[]{:S(2)}, u32[]{:S(2)}) async-start(bf16[128,2,768]{2,1,0:T(2,128)(2,1)} %broadcast_in_dim.63), calls=%async_computation.1 | async-start | bytes 786432 | tf_op jit(solution)/shard_map/all_to_all | solution.py:302
  120.5 7.6 %copy-start.24 = (bf16[2,8,128]{2,1,0:T(8,128)(2,1)S(1)}, bf16[2,8,128]{2,1,0:T(8,128)(2,1)}, u32[]{:S(2)}) copy-start(bf16[2,8,128]{2,1,0:T(8,128)(2,1)} %pad_maximum_fusion.6) | copy-start | bytes 12292
  121.4 13.8 %copy-start.4 = (bf16[9,6,128,128]{3,2,1,0:T(8,128)(2,1)S(1)}, bf16[9,6,128,128]{3,2,1,0:T(8,128)(2,1)}, u32[]{:S(2)}) copy-start(bf16[9,6,128,128]{3,2,1,0:T(8,128)(2,1)} %adj.7) | copy-start | bytes 5308420
  121.4 29.0 %collective-permute-start.15 = (bf16[12,256,128]{2,1,0:T(8,128)(2,1)}, bf16[12,256,128]{2,1,0:T(8,128)(2,1)}, u32[]{:S(2)}, u32[]{:S(2)}) collective-permute-start(bf16[12,256,128]{2,1,0:T(8,128)(2,1)} %pad_maximum_fusion.5), channel_id=1, source_target_pairs={{16,0},{32,16},{48,32},{64,48},{80,64},{96,80},{112,96},{17,1},{33... | collective-permute-start | bytes 2359304 | tf_op jit(solution)/shard_map/ppermute | solution.py:222
  125.6 24.9 %collective-permute-start.14 = (bf16[12,256,128]{2,1,0:T(8,128)(2,1)}, bf16[12,256,128]{2,1,0:T(8,128)(2,1)}, u32[]{:S(2)}, u32[]{:S(2)}) collective-permute-start(bf16[12,256,128]{2,1,0:T(8,128)(2,1)} %pad_maximum_fusion.4), channel_id=1, source_target_pairs={{0,16},{16,32},{32,48},{48,64},{64,80},{80,96},{96,112},{1,17},{17... | collective-permute-start | bytes 2359304 | tf_op jit(solution)/shard_map/ppermute | solution.py:222
  128.1 19.5 %collective-permute-start.13 = (bf16[12,136,128]{2,1,0:T(8,128)(2,1)}, bf16[12,136,128]{2,1,0:T(8,128)(2,1)}, u32[]{:S(2)}, u32[]{:S(2)}) collective-permute-start(bf16[12,136,128]{2,1,0:T(8,128)(2,1)} %get-tuple-element.47), channel_id=1, source_target_pairs={{1,0},{2,1},{3,2},{4,3},{5,4},{6,5},{7,6},{8,7},{9,8},{10,9},{11,1... | collective-permute-start | bytes 1253384 | tf_op jit(solution)/shard_map/ppermute | solution.py:222
  135.2 2.0 %copy-start.6 = (bf16[12,1152,128]{2,1,0:T(8,128)(2,1)S(1)}, bf16[12,1152,128]{2,1,0:T(8,128)(2,1)}, u32[]{:S(2)}) copy-start(bf16[12,1152,128]{2,1,0:T(8,128)(2,1)} %copy-done.5) | copy-start | bytes 10616836
  144.7 2.8 %copy-start = (f32[12,1152,128]{2,1,0:T(8,128)}, f32[12,1152,128]{2,1,0:T(8,128)S(1)}, u32[]{:S(2)}) copy-start(f32[12,1152,128]{2,1,0:T(8,128)S(1)} %decode_early.1.acc) | copy-start | bytes 21233668
  147.6 2.9 %copy-start.9 = (bf16[10,128,128]{2,1,0:T(8,128)(2,1)S(1)}, bf16[10,128,128]{2,1,0:T(8,128)(2,1)}, u32[]{:S(2)}) copy-start(bf16[10,128,128]{2,1,0:T(8,128)(2,1)} %copy-done.8) | copy-start | bytes 983044
  147.6 3.0 %copy-start.11 = (bf16[16,8,2,768]{3,1,2,0:T(8,128)(2,1)S(1)}, bf16[16,8,2,768]{3,1,2,0:T(8,128)(2,1)}, u32[]{:S(2)}) copy-start(bf16[16,8,2,768]{3,1,2,0:T(8,128)(2,1)} %copy.22) | copy-start | bytes 1179652
  147.6 3.0 %copy-start.13 = (bf16[1152,128]{1,0:T(8,128)(2,1)S(1)}, bf16[1152,128]{1,0:T(8,128)(2,1)}, u32[]{:S(2)}) copy-start(bf16[1152,128]{1,0:T(8,128)(2,1)} %fusion.2.hot) | copy-start | bytes 884740
  147.6 3.0 %copy-start.17 = (bf16[128,128]{1,0:T(8,128)(2,1)S(1)}, bf16[128,128]{1,0:T(8,128)(2,1)}, u32[]{:S(2)}) copy-start(bf16[128,128]{1,0:T(8,128)(2,1)} %w_region.1) | copy-start | bytes 98308
  147.6 3.0 %copy-start.18 = (bf16[128,128]{1,0:T(8,128)(2,1)S(1)}, bf16[128,128]{1,0:T(8,128)(2,1)}, u32[]{:S(2)}) copy-start(bf16[128,128]{1,0:T(8,128)(2,1)} %w_out.1) | copy-start | bytes 98308
  150.5 3.0 %copy-start.1 = (f32[12,1152,128]{2,1,0:T(8,128)S(1)}, f32[12,1152,128]{2,1,0:T(8,128)}, u32[]{:S(2)}) copy-start(f32[12,1152,128]{2,1,0:T(8,128)} %copy-done) | copy-start | bytes 21233668
  153.6 2.0 %copy-start.7 = (bf16[12,1152,128]{2,1,0:T(8,128)(2,1)S(1)}, bf16[12,1152,128]{2,1,0:T(8,128)(2,1)}, u32[]{:S(2)}) copy-start(bf16[12,1152,128]{2,1,0:T(8,128)(2,1)} %copy-done.5) | copy-start | bytes 10616836
where the time goes:
time: 169 us; the launch traced here: 167 us
  starting transfers between devices  68.6 us (41%)
  Pallas kernels  44.1 us (26%)
  local copies, waits for them, and re-layouts  31.7 us (19%)
  waiting for transfers between devices  12.4 us (7%)
  other arithmetic  9.67 us (6%)
    ppermute x16, starting transfers between devices, shift(): lax.ppermute(block, axis, pairs if up else [(b, a) for a, b in pairs])  46.9 us
    pallas_call x6, Pallas kernels, call(): pl.pallas_call(kernel, grid_spec=pltpu.PrefetchScalarGridSpec(num_scalar_...  44.1 us
    unnamed x62, local copies, waits for them, and re-layouts  16.7 us
    all_to_all x1, starting transfers between devices, on_device(): lax.all_to_all(part.reshape(half), ('rx', 'ry'), split_axis=0, concat_axi...  13.6 us
    all_to_all x1, starting transfers between devices, on_device(): lax.all_to_all(jnp.broadcast_to(region, half), ('rx', 'ry'), split_axis=0...  8.13 us
    ppermute x16, waiting for transfers between devices, shift(): lax.ppermute(block, axis, pairs if up else [(b, a) for a, b in pairs])  6.04 us
  transfers between devices with their start and end apart: 18, of which 4 were waited for; matrix products, arithmetic and copies ran while one was open for 14% of the time, Pallas kernels for 13%

commit v1 on v0

v1 whole, which is shorter than its diff:
```python
import functools
import jax
import jax.numpy as jnp
from jax import lax
from jax.experimental import pallas as pl
from jax.experimental.pallas import tpu as pltpu
from jax.sharding import PartitionSpec as P

GB, BLK, NB, C = 3, 128, 6, 128
EXT = GB + 2
ROWS = GB * GB * BLK
SIDE = GB * BLK
PAIR = 2
WIDE = PAIR * C
bf16, f32 = jnp.bfloat16, jnp.float32


def silu(v):
    return v / (1.0 + jnp.exp(-v))


def dot(a, b):
    return jnp.dot(a, b, preferred_element_type=f32)


def span(k):
    return slice(k * BLK, (k + 1) * BLK)


def ext_row(codes, j, n):
    code = codes[j * NB + n]
    e = (j // GB + code // 3) * EXT + j % GB + code % 3
    return pl.ds(pl.multiple_of(e * BLK, BLK), BLK)


def fill(ext, own, xu=None, xd=None):
    @pl.when(pl.program_id(0) == 0)
    def _():
        if xu is None:
            ext[...] = jnp.zeros(ext.shape, bf16)
        for e in range(EXT):
            ext[span(e * EXT), :] = jnp.zeros((BLK, WIDE), bf16)
            ext[span(e * EXT + EXT - 1), :] = jnp.zeros((BLK, WIDE), bf16)

    for s in range(PAIR):
        lanes = span(s)

        def put(row, col, block):
            ext[span(row * EXT + col), lanes] = block

        for a in range(GB):
            for b in range(GB):
                put(a + 1, b + 1, own[s, span(a * GB + b), :])
            if xu is not None:
                put(0, a + 1, xu[s, span(a), :])
                put(EXT - 1, a + 1, xd[s, span(a), :])


def early_sum(codes, adj, ext, j):
    weights = jnp.concatenate([adj[j, n] for n in range(NB)], axis=1)
    feats = jnp.concatenate([ext[ext_row(codes, j, n), :] for n in range(NB)], axis=0)
    return dot(weights, feats)


def side_term(late, j, columns):
    a, side = j // GB, int(j % GB > 0)
    return late[side * GB + a], columns[side][a * BLK : (a + GB) * BLK, :]


def row_term(late, j, rows):
    b, low = j % GB, int(j >= GB)
    first, last = max(b - 1, 0), min(b + 1, GB - 1)
    lanes = slice((first - b + 1) * BLK, (last - b + 2) * BLK)
    return late[(2 + low) * GB + b][:, lanes], rows[low][first * BLK : (last + 1) * BLK, :]


def side_columns(yl, yr, cu, cd):
    return [jnp.concatenate([joined(cu, k)] + [joined(y, a) for a in range(GB)] + [joined(cd, k)], axis=0)
            for k, y in enumerate((yl, yr))]


def joined(ref, k):
    return jnp.concatenate([ref[s, span(k), :] for s in range(PAIR)], axis=1)


def mix_in(diffused, base, gain, w_mix):
    v = diffused.astype(bf16).astype(f32)
    ms = jnp.mean(v * v, axis=1, keepdims=True)
    normed = (v * lax.rsqrt(ms + 1e-6) * gain[...]).astype(bf16)
    return (base.astype(f32) + silu(dot(normed, w_mix[...]))).astype(bf16)


def encode_early(codes, own, xu, xd, adj, gain, w_mix, acc, mid, ext):
    fill(ext, own, xu, xd)
    for j in range(GB * GB):
        total = early_sum(codes, adj, ext, j)
        a, b = j // GB, j % GB
        for s in range(PAIR):
            v = total[:, span(s)]
            if b == 1:
                mid[s, span(a), :] = mix_in(v, own[s, span(j), :], gain, w_mix)
            else:
                acc[s, span(a if b == 0 else GB + a), :] = v


def encode_late(own, acc, mid, yl, yr, cu, cd, cut, cdt, late, gain, w_mix, w_coarse, pool, unpool, spread, owners,
                d1, dl, dr, part, enc):
    columns = side_columns(yl, yr, cu, cd)
    for j in range(GB * GB):
        a, b = j // GB, j % GB
        if b == 1:
            for s in range(PAIR):
                enc[span(j), span(s)] = mid[s, span(a), :]
            continue
        rest = dot(*side_term(late, j, columns))
        for s in range(PAIR):
            v = acc[s, span(a if b == 0 else GB + a), :] + rest[:, span(s)]
            enc[span(j), span(s)] = mix_in(v, own[s, span(j), :], gain, w_mix)
    pooled = dot(pool[...], enc[...]).astype(bf16)
    lifted = jnp.concatenate([silu(dot(pooled[:, span(s)], w_coarse[...])).astype(bf16) for s in range(PAIR)], axis=1)
    part[...] = dot(spread[...], lifted).astype(bf16)
    refined = (pooled.astype(f32) + lifted.astype(f32)).astype(bf16)
    for s in range(PAIR):
        for k, out in ((0, dl), (GB - 1, dr)):
            ids = [cut[0, k : k + 1, :]] + [owners[a * GB + k : a * GB + k + 1, :] for a in range(GB)]
            ids += [cdt[0, k : k + 1, :], jnp.zeros((TAIL - EXT, C), bf16)]
            out[s, SIDE:, :] = jnp.concatenate([v.astype(f32) for v in ids], axis=0).astype(bf16)
    for j in range(GB * GB):
        a, b = j // GB, j % GB
        back = (enc[span(j), :].astype(f32) + dot(unpool[span(j), :], refined)).astype(bf16)
        for s in range(PAIR):
            v = back[:, span(s)]
            d1[s, span(j), :] = v
            if b != 1:
                (dl if b == 0 else dr)[s, span(a), :] = v


def decode_early(codes, own, adj, acc, ext):
    fill(ext, own)
    for j in range(GB * GB):
        total = early_sum(codes, adj, ext, j)
        for s in range(PAIR):
            acc[s, span(j), :] = total[:, span(s)]


def decode_late(own, acc, yl, yr, cu, cd, xu, xd, late, mown, region, w_region, w_out, hot, out):
    columns = side_columns(yl, yr, cu, cd)
    rows = [jnp.concatenate([joined(x, b) for b in range(GB)], axis=0) for x in (xu, xd)]
    reach = jnp.concatenate([dot(region[:, span(s)], w_region[...]).astype(bf16) for s in range(PAIR)], axis=1)
    for j in range(GB * GB):
        terms = [(mown[j], reach)]
        if j % GB != 1:
            terms.append(side_term(late, j, columns))
        if j // GB != 1:
            terms.append(row_term(late, j, rows))
        rest = dot(jnp.concatenate([w for w, _ in terms], axis=1), jnp.concatenate([v for _, v in terms], axis=0))
        extra = dot(hot[span(j), :], reach)
        for s in range(PAIR):
            second = (acc[s, span(j), :] + rest[:, span(s)]).astype(bf16)
            dec = (own[s, span(j), :].astype(f32) + extra[:, span(s)]).astype(bf16).astype(f32)
            out[s, span(j), :] = (dec + silu(dot(second, w_out[...]))).astype(bf16)


def late_kernel(codes, adj, late):
    for k in range(4 * GB):
        side, a = k // GB % 2, k % GB
        j = a * GB + side * (GB - 1) if k < 2 * GB else side * (GB - 1) * GB + a
        for d in range(GB):
            code = d * GB + side * (GB - 1) if k < 2 * GB else side * (GB - 1) * GB + d
            total = jnp.zeros((BLK, BLK), f32)
            for n in range(NB):
                total += jnp.where(codes[j * NB + n] == code, adj[j, n].astype(f32), 0.0)
            late[k, :, span(d)] = total.astype(bf16)


def owners_kernel(codes, adj, owners, cut, cdt, ylt, yrt, mown, hot):
    ids = lax.broadcasted_iota(jnp.int32, (C, BLK), 0)
    for e in range(EXT * EXT):
        a, b = e // EXT, e % EXT
        if b in (0, EXT - 1):
            row = (yrt if b else ylt)[0, a : a + 1, :]
        elif a in (0, EXT - 1):
            row = (cdt if a else cut)[0, b - 1 : b, :]
        else:
            k = (a - 1) * GB + b - 1
            row = owners[k : k + 1, :]
        row = row.astype(f32).astype(jnp.int32) - 1
        hot[span(e), :] = (ids == row).astype(f32).astype(bf16)
    for j in range(GB * GB):
        acc = jnp.zeros((BLK, C), f32)
        for n in range(NB):
            acc += lax.dot_general(
                adj[j, n], hot[ext_row(codes, j, n), :], (((1,), (1,)), ((), ())), preferred_element_type=f32
            )
        mown[j] = acc.astype(bf16)


def whole(shape):
    return pl.BlockSpec(shape, lambda p, *_: (0,) * len(shape), pipeline_mode=pl.Buffered(1))


def by_step(rows):
    return pl.BlockSpec((PAIR, rows, C), lambda p, *_: (p, 0, 0))


def by_lane(rows):
    return pl.BlockSpec((rows, WIDE), lambda p, *_: (0, p))


def call(kernel, name, steps, args, specs, outs, out_specs, scratch, flops, prefetch=0, exps=0, vmem=60):
    size = lambda v: v.size * v.dtype.itemsize
    return pl.pallas_call(
        kernel,
        grid_spec=pltpu.PrefetchScalarGridSpec(
            num_scalar_prefetch=prefetch, grid=(steps // PAIR,), in_specs=specs, out_specs=out_specs, scratch_shapes=scratch
        ),
        out_shape=outs,
        compiler_params=pltpu.CompilerParams(vmem_limit_bytes=vmem << 20, dimension_semantics=("arbitrary",)),
        name=name,
        cost_estimate=pl.CostEstimate(
            flops=flops, bytes_accessed=sum(map(size, args)) + sum(map(size, outs)), transcendentals=exps
        ),
    )(*args)


TAIL = 8
HINT = 1 << 34


def sds(shape, dtype=bf16):
    return jax.ShapeDtypeStruct(shape, dtype)


def shift(block, axis, up):
    count = lax.axis_size(axis)
    pairs = [(i, i + 1) for i in range(count - 1)]
    return lax.ppermute(block, axis, pairs if up else [(b, a) for a, b in pairs])


def copy_all(copies):
    for copy in copies:
        copy.start()
    for copy in copies:
        copy.wait()


def corner_kernel(yl, yr, tails, up, down, sems):
    copies = []
    for e, (out, row) in enumerate(((up, GB - 1), (down, 0))):
        for k, y in enumerate((yl, yr)):
            copies.append(pltpu.make_async_copy(y.at[:, span(row), :], out.at[:, span(k), :], sems.at[3 * e + k]))
        copies.append(pltpu.make_async_copy(tails.at[e], out.at[0, 2 * BLK :, :], sems.at[3 * e + 2]))
    copy_all(copies)


def rows_kernel(x, top, bottom, sems):
    copy_all([
        pltpu.make_async_copy(x.at[:, span(0).start : SIDE, :], top, sems.at[0]),
        pltpu.make_async_copy(x.at[:, ROWS - SIDE :, :], bottom, sems.at[1]),
    ])


def place(n):
    return [pl.BlockSpec(memory_space=pl.ANY)] * n


def rows_halo(x):
    top, bottom = call(rows_kernel, "pack_rows", PAIR, [x], place(1), [sds((x.shape[0], SIDE, C))] * 2, place(2),
                       [pltpu.SemaphoreType.DMA((2,))], HINT)
    return shift(bottom, "rx", True), shift(top, "rx", False), top


def corners(yl, yr, tails):
    shape = sds((yl.shape[0], 2 * BLK + TAIL, C))
    up, down = call(corner_kernel, "pack_corners", PAIR, [yl, yr, tails], place(3), [shape] * 2, place(2),
                    [pltpu.SemaphoreType.DMA((6,))], 1, vmem=4)
    return shift(up, "rx", True), shift(down, "rx", False)


def on_device(noisy_input, adjacency, neighbours, norm_gain, w_mix, pool_weight, cluster, owner_ids, w_coarse, w_region, w_out):
    steps = noisy_input.shape[1]
    x = noisy_input.transpose(1, 0, 2)
    codes = neighbours.reshape(-1)
    crows = owner_ids.shape[0]
    devices = lax.axis_size("rx") * lax.axis_size("ry")
    squares = x.reshape(steps, GB, GB, BLK, C)
    flat = lambda v: v.reshape(steps, -1, C)
    work = steps * ROWS * C * 2

    owner = owner_ids[:, 0]
    coarse = jnp.arange(crows, dtype=jnp.int32)
    ids = jnp.arange(devices, dtype=jnp.int32)
    hit = cluster[None, :] == coarse[:, None]
    node_owner = jnp.sum(jnp.where(hit, owner[:, None], 0), axis=0)
    owners = (node_owner + 1).astype(bf16).reshape(GB * GB, BLK)

    right, left = flat(squares[:, :, GB - 1]), flat(squares[:, :, 0])
    yl = shift(right, "ry", True)
    yr = shift(left, "ry", False)
    x_late, _, _ = lax.optimization_barrier((x, right, left))
    xu, xd, _ = rows_halo(x_late)
    pool = jnp.where(hit, pool_weight[None, :], jnp.zeros((), bf16))
    unpool = (cluster[:, None] == coarse[None, :]).astype(bf16)
    spread = (owner[None, :] == ids[:, None]).astype(bf16)
    hot = (node_owner[:, None] == ids[None, :]).astype(bf16)
    triple = lambda a: jnp.pad(owners[a * GB : (a + 1) * GB], ((0, TAIL - GB), (0, 0)))
    tails = jnp.stack([triple(GB - 1), triple(0)])
    owners = jnp.pad(owners, ((0, 16 - GB * GB), (0, 0)))
    gain = norm_gain.reshape(1, C)
    ext = pltpu.VMEM((EXT * EXT * BLK, WIDE), bf16)
    square = (BLK, C)

    (late,) = call(late_kernel, "late_weights", PAIR, [codes, adjacency], [whole(adjacency.shape)],
                   [sds((4 * GB, BLK, SIDE))], [whole((4 * GB, BLK, SIDE))], [], 1 << 20, prefetch=1)
    xu, xd, late, pool, unpool, spread, hot, tails, owners = lax.optimization_barrier((xu, xd, late, pool, unpool, spread, hot, tails, owners))
    early = lambda: [by_step(ROWS)] + [by_step(v.shape[1]) for v in (xu, xd)] + [whole(adjacency.shape)]
    acc, mid = call(
        encode_early, "encode_early", steps, [codes, x, xu, xd, adjacency, gain, w_mix],
        early() + [whole((1, C)), whole(square)],
        [sds((steps, 2 * SIDE, C), f32), sds((steps, SIDE, C))], [by_step(2 * SIDE), by_step(SIDE)], [ext],
        work * (NB * BLK + C // 3), prefetch=1, exps=work // 6)
    yl, yr, acc, mid = lax.optimization_barrier((yl, yr, acc, mid))
    cu, cd = corners(yl, yr, tails)
    halo = lambda: [by_step(v.shape[1]) for v in (yl, yr, cu, cd)]
    tail = lambda v: pl.BlockSpec((1, TAIL, C), lambda p, *_: (0, v.shape[1] // TAIL - 1, 0))
    first_cu, first_cd = cu, cd
    d1, dl, dr, part = call(
        encode_late, "encode_late", steps,
        [x, acc, mid, yl, yr, cu, cd, cu, cd, late, gain, w_mix, w_coarse, pool, unpool, spread, owners],
        [by_step(ROWS), by_step(2 * SIDE), by_step(SIDE)] + halo() + [tail(cu), tail(cd), whole(late.shape)]
        + [whole((1, C)), whole(square), whole(square), whole(pool.shape), whole(unpool.shape), whole(spread.shape), whole(owners.shape)],
        [sds((steps, r, C)) for r in (ROWS, SIDE + TAIL, SIDE + TAIL)] + [sds((devices, steps * C))],
        [by_step(r) for r in (ROWS, SIDE + TAIL, SIDE + TAIL)] + [by_lane(devices)],
        [pltpu.VMEM((ROWS, WIDE), bf16)], work * (C + 3 * crows), exps=work // 3)

    yl = shift(dr, "ry", True)
    yr = shift(dl, "ry", False)
    xu, xd, top = rows_halo(d1)
    part, _ = lax.optimization_barrier((part, top))
    (acc,) = call(decode_early, "decode_early", steps, [codes, d1, adjacency], [by_step(ROWS), whole(adjacency.shape)],
                  [sds((steps, ROWS, C), f32)], [by_step(ROWS)], [ext], work * NB * BLK, prefetch=1)
    half = (devices, 2, steps * C // 2)
    arrived = lax.all_to_all(part.reshape(half), ("rx", "ry"), split_axis=0, concat_axis=0, tiled=True)
    region = (jnp.sum(arrived.astype(f32), axis=0, keepdims=True) / float(crows)).astype(bf16)
    everyone = jnp.broadcast_to(region, half)
    everyone, _, _, _ = lax.optimization_barrier((everyone, xu, xd, acc))
    region = lax.all_to_all(everyone, ("rx", "ry"), split_axis=0, concat_axis=0, tiled=True)
    region = region.reshape(devices, steps * C)
    yl, yr, _, _ = lax.optimization_barrier((yl, yr, acc, everyone))
    cu, cd = corners(yl, yr, tails)
    (mown,) = call(owners_kernel, "owner_mix", PAIR, [codes, adjacency, owners, first_cu, first_cd, yl, yr],
                   [whole(adjacency.shape), whole(owners.shape)] + [tail(v) for v in (first_cu, first_cd, yl, yr)],
                   [sds((GB * GB,) + square)], [whole((GB * GB,) + square)],
                   [pltpu.VMEM((EXT * EXT * BLK, C), bf16)], HINT, prefetch=1)
    (out,) = call(
        decode_late, "decode_late", steps, [d1, acc, yl, yr, cu, cd, xu, xd, late, mown, region, w_region, w_out, hot],
        [by_step(ROWS)] * 2 + halo() + [by_step(SIDE)] * 2 + [whole(late.shape)]
        + [whole(mown.shape), by_lane(devices), whole(square), whole(square), whole(hot.shape)],
        [sds((steps, ROWS, C))], [by_step(ROWS)], [], work * 3 * C, exps=work // 2)
    return out.transpose(1, 0, 2)


def solution(mesh):
    nodes = P(("rx", "ry"))
    in_specs = (
        P(("rx", "ry"), None, None),
        P(("rx", "ry"), None, None, None),
        P(("rx", "ry"), None),
        P(),
        P(),
        nodes,
        nodes,
        P(("rx", "ry"), None),
        P(),
        P(),
        P(),
    )
    out_specs = P(("rx", "ry"), None, None)
    return jax.shard_map(on_device, mesh=mesh, in_specs=in_specs, out_specs=out_specs, check_vma=False)
```

time: 169 us -> 307 us (1.82)
  Pallas kernels: 44.1 us -> 211 us
  local copies, waits for them, and re-layouts: 31.7 us -> 12 us
  starting transfers between devices: 68.6 us -> 51.5 us
  waiting for transfers between devices: 12.4 us -> 26.9 us
  other arithmetic: 9.67 us -> 4.05 us
    pallas_call x6 -> x10, Pallas kernels: 44.1 us -> 211 us  [call(): pl.pallas_call(kernel, grid_spec=pltpu.PrefetchScalarGridSpec(num_scalar_...]
    ppermute x16 -> x12, waiting for transfers between devices: 6.04 us -> 21.9 us  [shift(): lax.ppermute(block, axis, pairs if up else [(b, a) for a, b in pairs])]
    ppermute x16 -> x12, starting transfers between devices: 46.9 us -> 32.2 us  [shift(): lax.ppermute(block, axis, pairs if up else [(b, a) for a, b in pairs])]
    unnamed x62 -> x30, local copies, waits for them, and re-layouts: 16.7 us -> 5.64 us
    slice x11 -> x2, local copies, waits for them, and re-layouts: 8.07 us -> 3.33 us  [the longest x1 3.32 us: on_device(): right, left = (flat(squares[:, :, GB - 1]), flat(squares[:, :, 0]))]
    concatenate x6 -> x0, other arithmetic: 4.22 us -> none  [the longest x2 2.22 us: with_owners(): return jnp.concatenate([block, rows], axis=1)]
    squeeze x6 -> x0, local copies, waits for them, and re-layouts: 3.93 us -> none  [the longest x1 1.02 us: on_device(): ml = shift(flat(squares[:, 1, GB - 1]), 'ry', True)]
  transfers between devices with their start and end apart: 18 -> 14, of which waited for: 4 -> 8; matrix products, arithmetic and copies ran while one was open for 14% -> 3% of each run, Pallas kernels for 13% -> 58%
where the time goes in v1:
time: 307 us; the launch traced here: 306 us
  Pallas kernels  211 us (69%)
  starting transfers between devices  51.5 us (17%)
  waiting for transfers between devices  26.9 us (9%)
  local copies, waits for them, and re-layouts  12 us (4%)
  other arithmetic  4.05 us (1%)
    pallas_call x10, Pallas kernels, call(): pl.pallas_call(kernel, grid_spec=pltpu.PrefetchScalarGridSpec(num_scalar_...  211 us
    ppermute x12, starting transfers between devices, shift(): lax.ppermute(block, axis, pairs if up else [(b, a) for a, b in pairs])  32.2 us
    ppermute x12, waiting for transfers between devices, shift(): lax.ppermute(block, axis, pairs if up else [(b, a) for a, b in pairs])  21.9 us
    all_to_all x1, starting transfers between devices, on_device(): lax.all_to_all(part.reshape(half), ('rx', 'ry'), split_axis=0, concat_axi...  11.8 us
    all_to_all x1, starting transfers between devices, on_device(): lax.all_to_all(everyone, ('rx', 'ry'), split_axis=0, concat_axis=0, tiled...  7.49 us
  transfers between devices with their start and end apart: 14, of which 8 were waited for; matrix products, arithmetic and copies ran while one was open for 3% of the time, Pallas kernels for 58%

profile of v1, /device:TPU:1, one launch (start us, length us, event | category | flops | bytes accessed | tf_op | source)
XLA Modules:
  0.0 305.7 jit_solution(1145616233633913974)
XLA Ops:
  0.0 3.3 %fusion.6 = (bf16[12,3,1,128,128]{4,3,2,1,0:T(8,128)(2,1)}, bf16[12,3,1,128,128]{4,3,2,1,0:T(8,128)(2,1)}) fusion(bf16[12,3,3,128,128]{4,3,2,1,0:T(8,128)(2,1)} %bitcast.28), kind=kLoop, calls=%fused_computation.18 | loop fusion | bytes 4718592 | tf_op jit(solution)/shard_map/slice | solution.py:297
  3.3 4.1 %collective-permute-start = (bf16[12,384,128]{2,1,0:T(8,128)(2,1)}, bf16[12,384,128]{2,1,0:T(8,128)(2,1)S(1)}, u32[]{:S(2)}, u32[]{:S(2)}) collective-permute-start(bf16[12,384,128]{2,1,0:T(8,128)(2,1)} %bitcast.2), channel_id=1, source_target_pairs={{0,1},{1,2},{2,3},{3,4},{4,5},{5,6},{6,7},{7,8},{8,9},{9,10},{10,1... | collective-permute-start | bytes 3538952 | tf_op jit(solution)/shard_map/ppermute | solution.py:237
  7.4 1.3 collective-permute-start.1
  8.8 72.6 %pack_rows.2 = (bf16[12,384,128]{2,1,0:T(8,128)(2,1)}, bf16[12,384,128]{2,1,0:T(8,128)(2,1)}) custom-call(bf16[12,1152,128]{2,1,0:T(8,128)(2,1)} %bitcast.29), custom_call_target="tpu_custom_call" | custom-call | flops 17179869184 | bytes 5898240 | tf_op jit(solution)/shard_map/pack_rows/pallas_call | solution.py:212
  81.4 4.0 %collective-permute-start.2 = (bf16[12,384,128]{2,1,0:T(8,128)(2,1)}, bf16[12,384,128]{2,1,0:T(8,128)(2,1)}, u32[]{:S(2)}, u32[]{:S(2)}) collective-permute-start(bf16[12,384,128]{2,1,0:T(8,128)(2,1)} %get-tuple-element.38), channel_id=1, source_target_pairs={{0,16},{16,32},{32,48},{48,64},{64,80},{80,96},{96,112},{1,17},{17... | collective-permute-start | bytes 3538952 | tf_op jit(solution)/shard_map/ppermute | solution.py:237
  85.4 1.9 collective-permute-start.3
  87.5 0.8 fusion.1.pool
  88.5 0.7 reshape.42.codes
  89.1 0.6 pad.13.owners
  89.7 4.6 %late_weights.1.late = bf16[12,128,384]{2,1,0:T(8,128)(2,1)} custom-call(s32[54]{0:T(128)} %reshape.42.codes, bf16[9,6,128,128]{3,2,1,0:T(8,128)(2,1)} %adj.7), custom_call_target="tpu_custom_call" | custom-call | flops 1048576 | bytes 2949336 | tf_op jit(solution)/shard_map/late_weights/pallas_call | solution.py:212
  94.3 0.6 fusion.3.spread
  94.9 0.9 fusion.2.hot
  95.9 1.0 fusion.unpool
  96.9 1.9 collective-permute-done.2.xu
  98.8 4.4 %collective-permute-done.3.xd = bf16[12,384,128]{2,1,0:T(8,128)(2,1)} collective-permute-done((bf16[12,384,128]{2,1,0:T(8,128)(2,1)}, bf16[12,384,128]{2,1,0:T(8,128)(2,1)}, u32[]{:S(2)}, u32[]{:S(2)}) %collective-permute-start.3) | collective-permute-done | bytes 1179680 | tf_op jit(solution)/shard_map/ppermute | solution.py:237
  103.2 12.6 %encode_early.1 = (f32[12,768,128]{2,1,0:T(8,128)}, bf16[12,384,128]{2,1,0:T(8,128)(2,1)}) custom-call(s32[54]{0:T(128)} %reshape.42.codes, bf16[12,1152,128]{2,1,0:T(8,128)(2,1)} %bitcast.30, bf16[12,384,128]{2,1,0:T(8,128)(2,1)} %collective-permute-done.2.xu, bf16[12,384,128]{2,1,0:T(8,128)(2,1)} %collective-permute-done.3.xd, ...), custom_call_target="tpu_custom_call" | custom-call | flops 2866544640 | bytes 13599448 | tf_op jit(solution)/shard_map/encode_early/pallas_call | solution.py:212
  116.0 0.8 copy-done.2
  116.8 0.4 copy-done.3
  117.2 1.9 collective-permute-start.4
  119.1 2.5 collective-permute-start.5
  121.6 6.7 %collective-permute-done.4.cu.cut = bf16[12,264,128]{2,1,0:T(8,128)(2,1)S(1)} collective-permute-done((bf16[12,264,128]{2,1,0:T(8,128)(2,1)S(1)}, bf16[12,264,128]{2,1,0:T(8,128)(2,1)S(1)}, u32[]{:S(2)}, u32[]{:S(2)}) %collective-permute-start.4) | collective-permute-done | bytes 811040 | tf_op jit(solution)/shard_map/ppermute | solution.py:237
  128.3 4.4 %collective-permute-done.5.cd.cdt = bf16[12,264,128]{2,1,0:T(8,128)(2,1)S(1)} collective-permute-done((bf16[12,264,128]{2,1,0:T(8,128)(2,1)S(1)}, bf16[12,264,128]{2,1,0:T(8,128)(2,1)S(1)}, u32[]{:S(2)}, u32[]{:S(2)}) %collective-permute-start.5) | collective-permute-done | bytes 811040 | tf_op jit(solution)/shard_map/ppermute | solution.py:237
  132.7 0.9 copy-done.5
  133.6 17.3 %encode_late.1 = (bf16[12,1152,128]{2,1,0:T(8,128)(2,1)}, bf16[12,392,128]{2,1,0:T(8,128)(2,1)}, bf16[12,392,128]{2,1,0:T(8,128)(2,1)}, bf16[128,1536]{1,0:T(8,128)(2,1)}) custom-call(bf16[12,1152,128]{2,1,0:T(8,128)(2,1)} %bitcast.31, f32[12,768,128]{2,1,0:T(8,128)} %get-tuple-element.44.acc, bf16[12,384,128]{2,1,0:T(8,128)(2,1)} %get-tuple-element.45.mid, ...), custom_call_target="tpu_custom_call" | custom-call | flops 1981808640 | bytes 23331328 | tf_op jit(solution)/shard_map/encode_late/pallas_call | solution.py:212
  150.9 4.3 %collective-permute-start.6 = (bf16[12,392,128]{2,1,0:T(8,128)(2,1)}, bf16[12,392,128]{2,1,0:T(8,128)(2,1)S(1)}, u32[]{:S(2)}, u32[]{:S(2)}) collective-permute-start(bf16[12,392,128]{2,1,0:T(8,128)(2,1)} %get-tuple-element.57), channel_id=1, source_target_pairs={{0,1},{1,2},{2,3},{3,4},{4,5},{5,6},{6,7},{7,8},{8,9},{9,10},{10,1... | collective-permute-start | bytes 3612680 | tf_op jit(solution)/shard_map/ppermute | solution.py:237
  155.2 1.3 collective-permute-start.7
  156.6 72.6 %pack_rows.3 = (bf16[12,384,128]{2,1,0:T(8,128)(2,1)}, bf16[12,384,128]{2,1,0:T(8,128)(2,1)}) custom-call(bf16[12,1152,128]{2,1,0:T(8,128)(2,1)} %get-tuple-element.56.own.x), custom_call_target="tpu_custom_call" | custom-call | flops 17179869184 | bytes 5898240 | tf_op jit(solution)/shard_map/pack_rows/pallas_call | solution.py:212
  229.2 2.0 collective-permute-start.8
  231.2 3.3 %collective-permute-start.9 = (bf16[12,384,128]{2,1,0:T(8,128)(2,1)}, bf16[12,384,128]{2,1,0:T(8,128)(2,1)}, u32[]{:S(2)}, u32[]{:S(2)}) collective-permute-start(bf16[12,384,128]{2,1,0:T(8,128)(2,1)} %get-tuple-element.60), channel_id=1, source_target_pairs={{16,0},{32,16},{48,32},{64,48},{80,64},{96,80},{112,96},{17,1},{33... | collective-permute-start | bytes 3538952 | tf_op jit(solution)/shard_map/ppermute | solution.py:237
  234.5 0.9 reshape.45
  235.4 11.8 %all-to-all-start = ((bf16[128,2,768]{2,1,0:T(2,128)(2,1)}), bf16[128,2,768]{2,1,0:T(2,128)(2,1)S(1)}, u32[]{:S(2)}, u32[]{:S(2)}) async-start(bf16[128,2,768]{2,1,0:T(2,128)(2,1)} %reshape.45), calls=%async_computation | async-start | bytes 786432 | tf_op jit(solution)/shard_map/all_to_all | solution.py:343
  247.1 9.9 %decode_early.1.acc = f32[12,1152,128]{2,1,0:T(8,128)} custom-call(s32[54]{0:T(128)} %reshape.42.codes, bf16[12,1152,128]{2,1,0:T(8,128)(2,1)} %get-tuple-element.56.own.x, bf16[9,6,128,128]{3,2,1,0:T(8,128)(2,1)} %adj.7), custom_call_target="tpu_custom_call" | custom-call | flops 2717908992 | bytes 12386520 | tf_op jit(solution)/shard_map/decode_early/pallas_call | solution.py:212
  257.1 4.3 %all-to-all-done = bf16[128,2,768]{2,1,0:T(2,128)(2,1)S(1)} async-done(((bf16[128,2,768]{2,1,0:T(2,128)(2,1)}), bf16[128,2,768]{2,1,0:T(2,128)(2,1)S(1)}, u32[]{:S(2)}, u32[]{:S(2)}) %all-to-all-start) | async-done | bytes 393248 | tf_op jit(solution)/shard_map/all_to_all | solution.py:343
  261.3 0.4 convert_reduce_fusion
  261.7 1.0 broadcast_in_dim.42
  262.7 7.5 %all-to-all-start.1 = ((bf16[128,2,768]{2,1,0:T(2,128)(2,1)}), bf16[128,2,768]{2,1,0:T(2,128)(2,1)}, u32[]{:S(2)}, u32[]{:S(2)}) async-start(bf16[128,2,768]{2,1,0:T(2,128)(2,1)} %broadcast_in_dim.42), calls=%async_computation.1 | async-start | bytes 786432 | tf_op jit(solution)/shard_map/all_to_all | solution.py:347
  270.2 1.0 pack_corners.3
  271.3 0.3 copy-done
  271.5 0.4 copy-done.1
  271.9 3.5 %collective-permute-start.10 = (bf16[12,264,128]{2,1,0:T(8,128)(2,1)}, bf16[12,264,128]{2,1,0:T(8,128)(2,1)S(1)}, u32[]{:S(2)}, u32[]{:S(2)}) collective-permute-start(bf16[12,264,128]{2,1,0:T(8,128)(2,1)} %get-tuple-element.66), channel_id=1, source_target_pairs={{0,16},{16,32},{32,48},{48,64},{64,80},{80,96},{96,112},{1,17},{17... | collective-permute-start | bytes 2433032 | tf_op jit(solution)/shard_map/ppermute | solution.py:237
  275.5 2.1 collective-permute-start.11
  277.6 4.4 %owner_mix.1.mown = bf16[9,128,128]{2,1,0:T(8,128)(2,1)} custom-call(s32[54]{0:T(128)} %reshape.42.codes, bf16[9,6,128,128]{3,2,1,0:T(8,128)(2,1)} %adj.7, bf16[16,128]{1,0:T(8,128)(2,1)} %pad.13.owners, bf16[12,264,128]{2,1,0:T(8,128)(2,1)} %copy-done.4, bf16[12,264,128]{2,1,0:T(8,128)(2,1)} %copy-done.5, bf16[12,392,128]{2,1,0:T(8,128)(2,1)} %copy-done, ...), custom_call_target="tpu_custom_call" | custom-call | flops 17179869184 | bytes 6099160 | tf_op jit(solution)/shard_map/owner_mix/pallas_call | solution.py:212
  281.9 0.7 all-to-all-done.1
  282.7 1.8 copy.20
  284.5 0.5 collective-permute-done.10.cu
  285.0 4.1 %collective-permute-done.11.cd = bf16[12,264,128]{2,1,0:T(8,128)(2,1)S(1)} collective-permute-done((bf16[12,264,128]{2,1,0:T(8,128)(2,1)S(1)}, bf16[12,264,128]{2,1,0:T(8,128)(2,1)S(1)}, u32[]{:S(2)}, u32[]{:S(2)}) %collective-permute-start.11) | collective-permute-done | bytes 811040 | tf_op jit(solution)/shard_map/ppermute | solution.py:237
  289.0 0.9 copy-done.7
  289.9 15.8 %decode_late.1 = bf16[12,1152,128]{2,1,0:T(8,128)(2,1)} custom-call(bf16[12,1152,128]{2,1,0:T(8,128)(2,1)} %get-tuple-element.56.own.x, f32[12,1152,128]{2,1,0:T(8,128)} %decode_early.1.acc, bf16[12,392,128]{2,1,0:T(8,128)(2,1)} %copy-done, bf16[12,392,128]{2,1,0:T(8,128)(2,1)} %copy-done.1, bf16[12,264,128]{2,1,0:T(8,128)(2,1)} %copy-done.6, ...), custom_call_target="tpu_custom_call" | custom-call | flops 1358954496 | bytes 22773760 | tf_op jit(solution)/shard_map/decode_late/pallas_call | solution.py:212
  (37 shorter events, 0.6 us)
Async XLA Ops:
  3.3 112.4 %collective-permute-start = (bf16[12,384,128]{2,1,0:T(8,128)(2,1)}, bf16[12,384,128]{2,1,0:T(8,128)(2,1)S(1)}, u32[]{:S(2)}, u32[]{:S(2)}) collective-permute-start(bf16[12,384,128]{2,1,0:T(8,128)(2,1)} %bitcast.2), channel_id=1, source_target_pairs={{0,1},{1,2},{2,3},{3,4},{4,5},{5,6},{6,7},{7,8},{8,9},{9,10},{10,1... | collective-permute-start | bytes 3538952 | tf_op jit(solution)/shard_map/ppermute | solution.py:237
  7.4 108.3 %collective-permute-start.1 = (bf16[12,384,128]{2,1,0:T(8,128)(2,1)}, bf16[12,384,128]{2,1,0:T(8,128)(2,1)S(1)}, u32[]{:S(2)}, u32[]{:S(2)}) collective-permute-start(bf16[12,384,128]{2,1,0:T(8,128)(2,1)} %bitcast.3), channel_id=1, source_target_pairs={{1,0},{2,1},{3,2},{4,3},{5,4},{6,5},{7,6},{8,7},{9,8},{10,9},{11,1... | collective-permute-start | bytes 3538952 | tf_op jit(solution)/shard_map/ppermute | solution.py:237
  8.7 78.6 %copy-start.9 = (s32[1152]{0:T(1024)S(1)}, s32[1152]{0:T(1024)}, u32[]{:S(2)}) copy-start(s32[1152]{0:T(1024)} %param.17) | copy-start | bytes 13828
  8.7 78.6 %copy-start.11 = (s32[144,1]{0,1:T(1,128)S(1)}, s32[144,1]{0,1:T(1,128)}, u32[]{:S(2)}) copy-start(s32[144,1]{0,1:T(1,128)} %param.18) | copy-start | bytes 1732
  8.7 78.8 %copy-start.10 = (bf16[1152]{0:T(1024)(128)(2,1)S(1)}, bf16[1152]{0:T(1024)(128)(2,1)}, u32[]{:S(2)}) copy-start(bf16[1152]{0:T(1024)(128)(2,1)} %param.16) | copy-start | bytes 6916
  8.8 79.6 %copy-start.13 = (pred[8]{0:T(512)(128)(4,1)S(1)}, pred[8]{0:T(512)(128)(4,1)}, u32[]{:S(2)}) copy-start(pred[8]{0:T(512)(128)(4,1)} %constant.11.clone.1) | copy-start | bytes 28
  8.8 79.6 %copy-start.12 = (s32[9,6]{0,1:T(8,128)S(1)}, s32[9,6]{0,1:T(8,128)}, u32[]{:S(2)}) copy-start(s32[9,6]{0,1:T(8,128)} %param.13) | copy-start | bytes 652
  81.4 17.4 %collective-permute-start.2 = (bf16[12,384,128]{2,1,0:T(8,128)(2,1)}, bf16[12,384,128]{2,1,0:T(8,128)(2,1)}, u32[]{:S(2)}, u32[]{:S(2)}) collective-permute-start(bf16[12,384,128]{2,1,0:T(8,128)(2,1)} %get-tuple-element.38), channel_id=1, source_target_pairs={{0,16},{16,32},{32,48},{48,64},{64,80},{80,96},{96,112},{1,17},{17... | collective-permute-start | bytes 3538952 | tf_op jit(solution)/shard_map/ppermute | solution.py:237
  85.4 17.8 %collective-permute-start.3 = (bf16[12,384,128]{2,1,0:T(8,128)(2,1)}, bf16[12,384,128]{2,1,0:T(8,128)(2,1)}, u32[]{:S(2)}, u32[]{:S(2)}) collective-permute-start(bf16[12,384,128]{2,1,0:T(8,128)(2,1)} %get-tuple-element.39), channel_id=1, source_target_pairs={{16,0},{32,16},{48,32},{64,48},{80,64},{96,80},{112,96},{17,1},{33... | collective-permute-start | bytes 3538952 | tf_op jit(solution)/shard_map/ppermute | solution.py:237
  115.8 1.0 copy-start.2
  115.8 1.4 copy-start.3
  117.2 11.1 %collective-permute-start.4 = (bf16[12,264,128]{2,1,0:T(8,128)(2,1)S(1)}, bf16[12,264,128]{2,1,0:T(8,128)(2,1)S(1)}, u32[]{:S(2)}, u32[]{:S(2)}) collective-permute-start(bf16[12,264,128]{2,1,0:T(8,128)(2,1)S(1)} %get-tuple-element.49), channel_id=1, source_target_pairs={{0,16},{16,32},{32,48},{48,64},{64,80},{80,96},{96,112},{1,17},{17... | collective-permute-start | bytes 2433032 | tf_op jit(solution)/shard_map/ppermute | solution.py:237
  119.1 13.6 %collective-permute-start.5 = (bf16[12,264,128]{2,1,0:T(8,128)(2,1)S(1)}, bf16[12,264,128]{2,1,0:T(8,128)(2,1)S(1)}, u32[]{:S(2)}, u32[]{:S(2)}) collective-permute-start(bf16[12,264,128]{2,1,0:T(8,128)(2,1)S(1)} %get-tuple-element.50), channel_id=1, source_target_pairs={{16,0},{32,16},{48,32},{64,48},{80,64},{96,80},{112,96},{17,1},{33... | collective-permute-start | bytes 2433032 | tf_op jit(solution)/shard_map/ppermute | solution.py:237
  128.3 4.4 %copy-start.4 = (bf16[12,264,128]{2,1,0:T(8,128)(2,1)}, bf16[12,264,128]{2,1,0:T(8,128)(2,1)S(1)}, u32[]{:S(2)}) copy-start(bf16[12,264,128]{2,1,0:T(8,128)(2,1)S(1)} %collective-permute-done.4.cu.cut) | copy-start | bytes 2433028
  132.7 0.9 copy-start.5
  150.9 119.3 %collective-permute-start.6 = (bf16[12,392,128]{2,1,0:T(8,128)(2,1)}, bf16[12,392,128]{2,1,0:T(8,128)(2,1)S(1)}, u32[]{:S(2)}, u32[]{:S(2)}) collective-permute-start(bf16[12,392,128]{2,1,0:T(8,128)(2,1)} %get-tuple-element.57), channel_id=1, source_target_pairs={{0,1},{1,2},{2,3},{3,4},{4,5},{5,6},{6,7},{7,8},{8,9},{9,10},{10,1... | collective-permute-start | bytes 3612680 | tf_op jit(solution)/shard_map/ppermute | solution.py:237
  155.2 115.0 %collective-permute-start.7 = (bf16[12,392,128]{2,1,0:T(8,128)(2,1)}, bf16[12,392,128]{2,1,0:T(8,128)(2,1)S(1)}, u32[]{:S(2)}, u32[]{:S(2)}) collective-permute-start(bf16[12,392,128]{2,1,0:T(8,128)(2,1)} %get-tuple-element.58), channel_id=1, source_target_pairs={{1,0},{2,1},{3,2},{4,3},{5,4},{6,5},{7,6},{8,7},{9,8},{10,9},{11,1... | collective-permute-start | bytes 3612680 | tf_op jit(solution)/shard_map/ppermute | solution.py:237
  156.5 78.0 %copy-start.8 = (bf16[128,1536]{1,0:T(8,128)(2,1)S(1)}, bf16[128,1536]{1,0:T(8,128)(2,1)}, u32[]{:S(2)}) copy-start(bf16[128,1536]{1,0:T(8,128)(2,1)} %get-tuple-element.61) | copy-start | bytes 1179652
  229.2 32.6 %collective-permute-start.8 = (bf16[12,384,128]{2,1,0:T(8,128)(2,1)}, bf16[12,384,128]{2,1,0:T(8,128)(2,1)}, u32[]{:S(2)}, u32[]{:S(2)}) collective-permute-start(bf16[12,384,128]{2,1,0:T(8,128)(2,1)} %get-tuple-element.62), channel_id=1, source_target_pairs={{0,16},{16,32},{32,48},{48,64},{64,80},{80,96},{96,112},{1,17},{17... | collective-permute-start | bytes 3538952 | tf_op jit(solution)/shard_map/ppermute | solution.py:237
  231.2 30.5 %collective-permute-start.9 = (bf16[12,384,128]{2,1,0:T(8,128)(2,1)}, bf16[12,384,128]{2,1,0:T(8,128)(2,1)}, u32[]{:S(2)}, u32[]{:S(2)}) collective-permute-start(bf16[12,384,128]{2,1,0:T(8,128)(2,1)} %get-tuple-element.60), channel_id=1, source_target_pairs={{16,0},{32,16},{48,32},{64,48},{80,64},{96,80},{112,96},{17,1},{33... | collective-permute-start | bytes 3538952 | tf_op jit(solution)/shard_map/ppermute | solution.py:237
  235.4 25.9 %all-to-all-start = ((bf16[128,2,768]{2,1,0:T(2,128)(2,1)}), bf16[128,2,768]{2,1,0:T(2,128)(2,1)S(1)}, u32[]{:S(2)}, u32[]{:S(2)}) async-start(bf16[128,2,768]{2,1,0:T(2,128)(2,1)} %reshape.45), calls=%async_computation | async-start | bytes 786432 | tf_op jit(solution)/shard_map/all_to_all | solution.py:343
  262.7 20.0 %all-to-all-start.1 = ((bf16[128,2,768]{2,1,0:T(2,128)(2,1)}), bf16[128,2,768]{2,1,0:T(2,128)(2,1)}, u32[]{:S(2)}, u32[]{:S(2)}) async-start(bf16[128,2,768]{2,1,0:T(2,128)(2,1)} %broadcast_in_dim.42), calls=%async_computation.1 | async-start | bytes 786432 | tf_op jit(solution)/shard_map/all_to_all | solution.py:347
  270.2 1.3 copy-start
  270.2 1.7 copy-start.1
  271.9 13.0 %collective-permute-start.10 = (bf16[12,264,128]{2,1,0:T(8,128)(2,1)}, bf16[12,264,128]{2,1,0:T(8,128)(2,1)S(1)}, u32[]{:S(2)}, u32[]{:S(2)}) collective-permute-start(bf16[12,264,128]{2,1,0:T(8,128)(2,1)} %get-tuple-element.66), channel_id=1, source_target_pairs={{0,16},{16,32},{32,48},{48,64},{64,80},{80,96},{96,112},{1,17},{17... | collective-permute-start | bytes 2433032 | tf_op jit(solution)/shard_map/ppermute | solution.py:237
  275.5 13.6 %collective-permute-start.11 = (bf16[12,264,128]{2,1,0:T(8,128)(2,1)S(1)}, bf16[12,264,128]{2,1,0:T(8,128)(2,1)S(1)}, u32[]{:S(2)}, u32[]{:S(2)}) collective-permute-start(bf16[12,264,128]{2,1,0:T(8,128)(2,1)S(1)} %get-tuple-element.67), channel_id=1, source_target_pairs={{16,0},{32,16},{48,32},{64,48},{80,64},{96,80},{112,96},{17,1},{33... | collective-permute-start | bytes 2433032 | tf_op jit(solution)/shard_map/ppermute | solution.py:237
  285.0 4.1 %copy-start.6 = (bf16[12,264,128]{2,1,0:T(8,128)(2,1)}, bf16[12,264,128]{2,1,0:T(8,128)(2,1)S(1)}, u32[]{:S(2)}) copy-start(bf16[12,264,128]{2,1,0:T(8,128)(2,1)S(1)} %collective-permute-done.10.cu) | copy-start | bytes 2433028
  289.0 0.9 copy-start.7

commit v2 on v1

--- a/solution.py
+++ b/solution.py
@@ -10,9 +10,10 @@
 EXT = GB + 2
 ROWS = GB * GB * BLK
 SIDE = GB * BLK
-PAIR = 2
+PAIR = 4
 WIDE = PAIR * C
 bf16, f32 = jnp.bfloat16, jnp.float32
+ACC = bf16
 
 
 def silu(v):
@@ -83,11 +84,25 @@
     return jnp.concatenate([ref[s, span(k), :] for s in range(PAIR)], axis=1)
 
 
-def mix_in(diffused, base, gain, w_mix):
+def twice(w):
+    zero = jnp.zeros((C, C), bf16)
+    return jnp.concatenate([jnp.concatenate([w, zero], axis=1), jnp.concatenate([zero, w], axis=1)], axis=0)
+
+
+def mix(values, w):
+    parts = [dot(jnp.concatenate(values[s : s + 2], axis=1), w[...]) for s in range(0, PAIR, 2)]
+    return [silu(parts[s // 2][:, span(s % 2)]) for s in range(PAIR)]
+
+
+def norm(diffused, gain):
     v = diffused.astype(bf16).astype(f32)
     ms = jnp.mean(v * v, axis=1, keepdims=True)
-    normed = (v * lax.rsqrt(ms + 1e-6) * gain[...]).astype(bf16)
-    return (base.astype(f32) + silu(dot(normed, w_mix[...]))).astype(bf16)
+    return (v * lax.rsqrt(ms + 1e-6) * gain[...]).astype(bf16)
+
+
+def mix_in(diffused, own, j, gain, w_mix):
+    mixed = mix([norm(v, gain) for v in diffused], w_mix)
+    return [(own[s, span(j), :].astype(f32) + mixed[s]).astype(bf16) for s in range(PAIR)]
 
 
 def encode_early(codes, own, xu, xd, adj, gain, w_mix, acc, mid, ext):
@@ -95,12 +110,14 @@
     for j in range(GB * GB):
         total = early_sum(codes, adj, ext, j)
         a, b = j // GB, j % GB
+        parts = [total[:, span(s)] for s in range(PAIR)]
+        if b == 1:
+            parts = mix_in(parts, own, j, gain, w_mix)
         for s in range(PAIR):
-            v = total[:, span(s)]
             if b == 1:
-                mid[s, span(a), :] = mix_in(v, own[s, span(j), :], gain, w_mix)
+                mid[s, span(a), :] = parts[s]
             else:
-                acc[s, span(a if b == 0 else GB + a), :] = v
+                acc[s, span(a if b == 0 else GB + a), :] = parts[s].astype(ACC)
 
 
 def encode_late(own, acc, mid, yl, yr, cu, cd, cut, cdt, late, gain, w_mix, w_coarse, pool, unpool, spread, owners,
@@ -113,11 +130,11 @@
                 enc[span(j), span(s)] = mid[s, span(a), :]
             continue
         rest = dot(*side_term(late, j, columns))
-        for s in range(PAIR):
-            v = acc[s, span(a if b == 0 else GB + a), :] + rest[:, span(s)]
-            enc[span(j), span(s)] = mix_in(v, own[s, span(j), :], gain, w_mix)
+        parts = [acc[s, span(a if b == 0 else GB + a), :] + rest[:, span(s)] for s in range(PAIR)]
+        for s, v in enumerate(mix_in(parts, own, j, gain, w_mix)):
+            enc[span(j), span(s)] = v
     pooled = dot(pool[...], enc[...]).astype(bf16)
-    lifted = jnp.concatenate([silu(dot(pooled[:, span(s)], w_coarse[...])).astype(bf16) for s in range(PAIR)], axis=1)
+    lifted = jnp.concatenate(mix([pooled[:, span(s)] for s in range(PAIR)], w_coarse), axis=1).astype(bf16)
     part[...] = dot(spread[...], lifted).astype(bf16)
     refined = (pooled.astype(f32) + lifted.astype(f32)).astype(bf16)
     for s in range(PAIR):
@@ -140,7 +157,7 @@
     for j in range(GB * GB):
         total = early_sum(codes, adj, ext, j)
         for s in range(PAIR):
-            acc[s, span(j), :] = total[:, span(s)]
+            acc[s, span(j), :] = total[:, span(s)].astype(ACC)
 
 
 def decode_late(own, acc, yl, yr, cu, cd, xu, xd, late, mown, region, w_region, w_out, hot, out):
@@ -155,10 +172,10 @@
             terms.append(row_term(late, j, rows))
         rest = dot(jnp.concatenate([w for w, _ in terms], axis=1), jnp.concatenate([v for _, v in terms], axis=0))
         extra = dot(hot[span(j), :], reach)
+        mixed = mix([(acc[s, span(j), :] + rest[:, span(s)]).astype(bf16) for s in range(PAIR)], w_out)
         for s in range(PAIR):
-            second = (acc[s, span(j), :] + rest[:, span(s)]).astype(bf16)
             dec = (own[s, span(j), :].astype(f32) + extra[:, span(s)]).astype(bf16).astype(f32)
-            out[s, span(j), :] = (dec + silu(dot(second, w_out[...]))).astype(bf16)
+            out[s, span(j), :] = (dec + mixed[s]).astype(bf16)
 
 
 def late_kernel(codes, adj, late):
@@ -207,7 +224,7 @@
     return pl.BlockSpec((rows, WIDE), lambda p, *_: (0, p))
 
 
-def call(kernel, name, steps, args, specs, outs, out_specs, scratch, flops, prefetch=0, exps=0, vmem=60):
+def call(kernel, name, steps, args, specs, outs, out_specs, scratch, flops, prefetch=0, exps=0, vmem=None):
     size = lambda v: v.size * v.dtype.itemsize
     return pl.pallas_call(
         kernel,
@@ -215,7 +232,7 @@
             num_scalar_prefetch=prefetch, grid=(steps // PAIR,), in_specs=specs, out_specs=out_specs, scratch_shapes=scratch
         ),
         out_shape=outs,
-        compiler_params=pltpu.CompilerParams(vmem_limit_bytes=vmem << 20, dimension_semantics=("arbitrary",)),
+        compiler_params=pltpu.CompilerParams(vmem_limit_bytes=(vmem or VMEM) << 20, dimension_semantics=("arbitrary",)),
         name=name,
         cost_estimate=pl.CostEstimate(
             flops=flops, bytes_accessed=sum(map(size, args)) + sum(map(size, outs)), transcendentals=exps
@@ -225,6 +242,7 @@
 
 TAIL = 8
 HINT = 1 << 34
+VMEM = 28
 
 
 def sds(shape, dtype=bf16):
@@ -237,44 +255,35 @@
     return lax.ppermute(block, axis, pairs if up else [(b, a) for a, b in pairs])
 
 
-def copy_all(copies):
-    for copy in copies:
-        copy.start()
-    for copy in copies:
-        copy.wait()
-
-
-def corner_kernel(yl, yr, tails, up, down, sems):
-    copies = []
-    for e, (out, row) in enumerate(((up, GB - 1), (down, 0))):
-        for k, y in enumerate((yl, yr)):
-            copies.append(pltpu.make_async_copy(y.at[:, span(row), :], out.at[:, span(k), :], sems.at[3 * e + k]))
-        copies.append(pltpu.make_async_copy(tails.at[e], out.at[0, 2 * BLK :, :], sems.at[3 * e + 2]))
-    copy_all(copies)
-
-
-def rows_kernel(x, top, bottom, sems):
-    copy_all([
-        pltpu.make_async_copy(x.at[:, span(0).start : SIDE, :], top, sems.at[0]),
-        pltpu.make_async_copy(x.at[:, ROWS - SIDE :, :], bottom, sems.at[1]),
-    ])
-
-
-def place(n):
-    return [pl.BlockSpec(memory_space=pl.ANY)] * n
-
-
-def rows_halo(x):
-    top, bottom = call(rows_kernel, "pack_rows", PAIR, [x], place(1), [sds((x.shape[0], SIDE, C))] * 2, place(2),
-                       [pltpu.SemaphoreType.DMA((2,))], HINT)
+def corner_kernel(lt, lb, rt, rb, tails, up, down):
+    for out, left, right, k in ((up, lb, rb, 0), (down, lt, rt, 1)):
+        out[:, :BLK, :] = left[...]
+        out[:, BLK : 2 * BLK, :] = right[...]
+        out[:, 2 * BLK :, :] = jnp.broadcast_to(tails[k][None], (out.shape[0], TAIL, C))
+
+
+def rows_kernel(x, top, bottom):
+    top[...] = x[:, :SIDE, :]
+    bottom[...] = x[:, ROWS - SIDE :, :]
+
+
+def rows_halo(x, hint):
+    top, bottom = call(rows_kernel, "pack_rows", x.shape[0], [x], [by_step(ROWS)],
+                       [sds((x.shape[0], SIDE, C))] * 2, [by_step(SIDE)] * 2, [], hint)
     return shift(bottom, "rx", True), shift(top, "rx", False), top
 
 
 def corners(yl, yr, tails):
-    shape = sds((yl.shape[0], 2 * BLK + TAIL, C))
-    up, down = call(corner_kernel, "pack_corners", PAIR, [yl, yr, tails], place(3), [shape] * 2, place(2),
-                    [pltpu.SemaphoreType.DMA((6,))], 1, vmem=4)
+    steps = yl.shape[0]
+    block = lambda a: pl.BlockSpec((PAIR, BLK, C), lambda p, *_: (p, a, 0))
+    up, down = call(corner_kernel, "pack_corners", steps, [yl, yl, yr, yr, tails],
+                    [block(0), block(GB - 1)] * 2 + [whole(tails.shape)],
+                    [sds((steps, 2 * BLK + TAIL, C))] * 2, [by_step(2 * BLK + TAIL)] * 2, [], 1, vmem=8)
     return shift(up, "rx", True), shift(down, "rx", False)
+
+
+def part_kernel(part, out):
+    out[...] = part[...]
 
 
 def on_device(noisy_input, adjacency, neighbours, norm_gain, w_mix, pool_weight, cluster, owner_ids, w_coarse, w_region, w_out):
@@ -298,7 +307,7 @@
     yl = shift(right, "ry", True)
     yr = shift(left, "ry", False)
     x_late, _, _ = lax.optimization_barrier((x, right, left))
-    xu, xd, _ = rows_halo(x_late)
+    xu, xd, _ = rows_halo(x_late, HINT)
     pool = jnp.where(hit, pool_weight[None, :], jnp.zeros((), bf16))
     unpool = (cluster[:, None] == coarse[None, :]).astype(bf16)
     spread = (owner[None, :] == ids[:, None]).astype(bf16)
@@ -307,19 +316,20 @@
     tails = jnp.stack([triple(GB - 1), triple(0)])
     owners = jnp.pad(owners, ((0, 16 - GB * GB), (0, 0)))
     gain = norm_gain.reshape(1, C)
+    w_mix, w_coarse, w_out = twice(w_mix), twice(w_coarse), twice(w_out)
+    double = (2 * C, 2 * C)
     ext = pltpu.VMEM((EXT * EXT * BLK, WIDE), bf16)
     square = (BLK, C)
 
     (late,) = call(late_kernel, "late_weights", PAIR, [codes, adjacency], [whole(adjacency.shape)],
                    [sds((4 * GB, BLK, SIDE))], [whole((4 * GB, BLK, SIDE))], [], 1 << 20, prefetch=1)
-    xu, xd, late, pool, unpool, spread, hot, tails, owners = lax.optimization_barrier((xu, xd, late, pool, unpool, spread, hot, tails, owners))
+    xu, xd, late, pool, unpool, spread, hot, tails, owners, w_mix, w_coarse, w_out = lax.optimization_barrier((xu, xd, late, pool, unpool, spread, hot, tails, owners, w_mix, w_coarse, w_out))
     early = lambda: [by_step(ROWS)] + [by_step(v.shape[1]) for v in (xu, xd)] + [whole(adjacency.shape)]
     acc, mid = call(
         encode_early, "encode_early", steps, [codes, x, xu, xd, adjacency, gain, w_mix],
-        early() + [whole((1, C)), whole(square)],
-        [sds((steps, 2 * SIDE, C), f32), sds((steps, SIDE, C))], [by_step(2 * SIDE), by_step(SIDE)], [ext],
+        early() + [whole((1, C)), whole(double)],
+        [sds((steps, 2 * SIDE, C), ACC), sds((steps, SIDE, C))], [by_step(2 * SIDE), by_step(SIDE)], [ext],
         work * (NB * BLK + C // 3), prefetch=1, exps=work // 6)
-    yl, yr, acc, mid = lax.optimization_barrier((yl, yr, acc, mid))
     cu, cd = corners(yl, yr, tails)
     halo = lambda: [by_step(v.shape[1]) for v in (yl, yr, cu, cd)]
     tail = lambda v: pl.BlockSpec((1, TAIL, C), lambda p, *_: (0, v.shape[1] // TAIL - 1, 0))
@@ -328,22 +338,23 @@
         encode_late, "encode_late", steps,
         [x, acc, mid, yl, yr, cu, cd, cu, cd, late, gain, w_mix, w_coarse, pool, unpool, spread, owners],
         [by_step(ROWS), by_step(2 * SIDE), by_step(SIDE)] + halo() + [tail(cu), tail(cd), whole(late.shape)]
-        + [whole((1, C)), whole(square), whole(square), whole(pool.shape), whole(unpool.shape), whole(spread.shape), whole(owners.shape)],
+        + [whole((1, C)), whole(double), whole(double), whole(pool.shape), whole(unpool.shape), whole(spread.shape), whole(owners.shape)],
         [sds((steps, r, C)) for r in (ROWS, SIDE + TAIL, SIDE + TAIL)] + [sds((devices, steps * C))],
         [by_step(r) for r in (ROWS, SIDE + TAIL, SIDE + TAIL)] + [by_lane(devices)],
         [pltpu.VMEM((ROWS, WIDE), bf16)], work * (C + 3 * crows), exps=work // 3)
 
     yl = shift(dr, "ry", True)
     yr = shift(dl, "ry", False)
-    xu, xd, top = rows_halo(d1)
-    part, _ = lax.optimization_barrier((part, top))
+    (part,) = call(part_kernel, "part", PAIR, [part], [whole(part.shape)], [sds(part.shape)], [whole(part.shape)], [], HINT, vmem=4)
+    part = part.reshape(devices, 2, steps * C // 2)
     (acc,) = call(decode_early, "decode_early", steps, [codes, d1, adjacency], [by_step(ROWS), whole(adjacency.shape)],
-                  [sds((steps, ROWS, C), f32)], [by_step(ROWS)], [ext], work * NB * BLK, prefetch=1)
+                  [sds((steps, ROWS, C), ACC)], [by_step(ROWS)], [ext], work * NB * BLK, prefetch=1)
+    xu, xd, top = rows_halo(d1, 1)
     half = (devices, 2, steps * C // 2)
-    arrived = lax.all_to_all(part.reshape(half), ("rx", "ry"), split_axis=0, concat_axis=0, tiled=True)
+    arrived = lax.all_to_all(part, ("rx", "ry"), split_axis=0, concat_axis=0, tiled=True)
     region = (jnp.sum(arrived.astype(f32), axis=0, keepdims=True) / float(crows)).astype(bf16)
     everyone = jnp.broadcast_to(region, half)
-    everyone, _, _, _ = lax.optimization_barrier((everyone, xu, xd, acc))
+    everyone, _ = lax.optimization_barrier((everyone, xu))
     region = lax.all_to_all(everyone, ("rx", "ry"), split_axis=0, concat_axis=0, tiled=True)
     region = region.reshape(devices, steps * C)
     yl, yr, _, _ = lax.optimization_barrier((yl, yr, acc, everyone))
@@ -355,8 +366,8 @@
     (out,) = call(
         decode_late, "decode_late", steps, [d1, acc, yl, yr, cu, cd, xu, xd, late, mown, region, w_region, w_out, hot],
         [by_step(ROWS)] * 2 + halo() + [by_step(SIDE)] * 2 + [whole(late.shape)]
-        + [whole(mown.shape), by_lane(devices), whole(square), whole(square), whole(hot.shape)],
-        [sds((steps, ROWS, C))], [by_step(ROWS)], [], work * 3 * C, exps=work // 2)
+        + [whole(mown.shape), by_lane(devices), whole(square), whole(double), whole(hot.shape)],
+        [sds((steps, ROWS, C))], [by_step(ROWS)], [], work * 3 * C, exps=work // 2, vmem=60)
     return out.transpose(1, 0, 2)
 
 

time: 307 us -> 151 us (0.49)
  Pallas kernels: 211 us -> 46.3 us
  starting transfers between devices: 51.5 us -> 57.9 us
  local copies, waits for them, and re-layouts: 12 us -> 16.4 us
    pallas_call x10 -> x11, Pallas kernels: 211 us -> 46.3 us  [call(): pl.pallas_call(kernel, grid_spec=pltpu.PrefetchScalarGridSpec(num_scalar_...]
    all_to_all x1, starting transfers between devices: 7.49 us -> 12.1 us  [on_device(): lax.all_to_all(everyone, ('rx', 'ry'), split_axis=0, concat_axis=0, tiled...]
    unnamed x30 -> x68, local copies, waits for them, and re-layouts: 5.64 us -> 10 us
  transfers between devices with their start and end apart: 14 -> 14, of which waited for: 8 -> 8; matrix products, arithmetic and copies ran while one was open for 3% -> 5% of each run, Pallas kernels for 58% -> 16%
where the time goes in v2:
time: 151 us
  starting transfers between devices  57.9 us (38%)
  Pallas kernels  46.3 us (31%)
  waiting for transfers between devices  25.3 us (17%)
  local copies, waits for them, and re-layouts  16.4 us (11%)
  other arithmetic  4.23 us (3%)
    pallas_call x11, Pallas kernels, call(): pl.pallas_call(kernel, grid_spec=pltpu.PrefetchScalarGridSpec(num_scalar_...  46.3 us
    ppermute x12, starting transfers between devices, shift(): lax.ppermute(block, axis, pairs if up else [(b, a) for a, b in pairs])  34.1 us
    ppermute x12, waiting for transfers between devices, shift(): lax.ppermute(block, axis, pairs if up else [(b, a) for a, b in pairs])  21.6 us
    all_to_all x1, starting transfers between devices, on_device(): lax.all_to_all(everyone, ('rx', 'ry'), split_axis=0, concat_axis=0, tiled...  12.1 us
    all_to_all x1, starting transfers between devices, on_device(): lax.all_to_all(part, ('rx', 'ry'), split_axis=0, concat_axis=0, tiled=True)  11.7 us
    unnamed x68, local copies, waits for them, and re-layouts  10 us
    slice x1, local copies, waits for them, and re-layouts, on_device(): right, left = (flat(squares[:, :, GB - 1]), flat(squares[:, :, 0]))  3.51 us
  transfers between devices with their start and end apart: 14, of which 8 were waited for; matrix products, arithmetic and copies ran while one was open for 5% of the time, Pallas kernels for 16%

profile of v2, /device:TPU:1, one launch (start us, length us, event | category | flops | bytes accessed | tf_op | source)
XLA Modules:
  0.0 150.7 jit_solution(9509493426372041394)
XLA Ops:
  0.0 3.5 %fusion.15 = (bf16[12,3,1,128,128]{4,3,2,1,0:T(8,128)(2,1)}, bf16[12,3,1,128,128]{4,3,2,1,0:T(8,128)(2,1)}) fusion(bf16[12,3,3,128,128]{4,3,2,1,0:T(8,128)(2,1)} %bitcast.28), kind=kLoop, calls=%fused_computation.29 | loop fusion | bytes 4718592 | tf_op jit(solution)/shard_map/slice | solution.py:306
  3.5 4.1 %collective-permute-start.2 = (bf16[12,384,128]{2,1,0:T(8,128)(2,1)}, bf16[12,384,128]{2,1,0:T(8,128)(2,1)S(1)}, u32[]{:S(2)}, u32[]{:S(2)}) collective-permute-start(bf16[12,384,128]{2,1,0:T(8,128)(2,1)} %bitcast.2), channel_id=1, source_target_pairs={{0,1},{1,2},{2,3},{3,4},{4,5},{5,6},{6,7},{7,8},{8,9},{9,10},{10,1... | collective-permute-start | bytes 3538952 | tf_op jit(solution)/shard_map/ppermute | solution.py:255
  7.6 1.3 collective-permute-start.3
  9.0 1.9 %pack_rows.2 = (bf16[12,384,128]{2,1,0:T(8,128)(2,1)}, bf16[12,384,128]{2,1,0:T(8,128)(2,1)}) custom-call(bf16[12,1152,128]{2,1,0:T(8,128)(2,1)S(1)} %bitcast.29), custom_call_target="tpu_custom_call" | custom-call | flops 17179869184 | bytes 5898240 | tf_op jit(solution)/shard_map/pack_rows/pallas_call | solution.py:229
  10.9 3.9 %collective-permute-start = (bf16[12,384,128]{2,1,0:T(8,128)(2,1)}, bf16[12,384,128]{2,1,0:T(8,128)(2,1)}, u32[]{:S(2)}, u32[]{:S(2)}) collective-permute-start(bf16[12,384,128]{2,1,0:T(8,128)(2,1)} %get-tuple-element.36), channel_id=1, source_target_pairs={{0,16},{16,32},{32,48},{48,64},{64,80},{80,96},{96,112},{1,17},{17... | collective-permute-start | bytes 3538952 | tf_op jit(solution)/shard_map/ppermute | solution.py:255
  14.9 1.9 %collective-permute-start.1 = (bf16[12,384,128]{2,1,0:T(8,128)(2,1)}, bf16[12,384,128]{2,1,0:T(8,128)(2,1)}, u32[]{:S(2)}, u32[]{:S(2)}) collective-permute-start(bf16[12,384,128]{2,1,0:T(8,128)(2,1)} %get-tuple-element.37), channel_id=1, source_target_pairs={{16,0},{32,16},{48,32},{64,48},{80,64},{96,80},{112,96},{17,1},{33... | collective-permute-start | bytes 3538952 | tf_op jit(solution)/shard_map/ppermute | solution.py:255
  17.0 1.0 fusion.2.hot
  18.0 0.7 fusion.11.w_out
  18.8 0.7 fusion.9
  19.6 1.5 copy-done.13
  21.1 2.0 %late_weights.1.late = bf16[12,128,384]{2,1,0:T(8,128)(2,1)S(1)} custom-call(s32[54]{0:T(128)S(1)} %reshape.41.codes, bf16[9,6,128,128]{3,2,1,0:T(8,128)(2,1)S(1)} %copy-done.13), custom_call_target="tpu_custom_call" | custom-call | flops 1048576 | bytes 2949336 | tf_op jit(solution)/shard_map/late_weights/pallas_call | solution.py:229
  23.4 4.9 %collective-permute-done.xu = bf16[12,384,128]{2,1,0:T(8,128)(2,1)} collective-permute-done((bf16[12,384,128]{2,1,0:T(8,128)(2,1)}, bf16[12,384,128]{2,1,0:T(8,128)(2,1)}, u32[]{:S(2)}, u32[]{:S(2)}) %collective-permute-start) | collective-permute-done | bytes 1179680 | tf_op jit(solution)/shard_map/ppermute | solution.py:255
  28.3 4.6 %collective-permute-done.1.xd = bf16[12,384,128]{2,1,0:T(8,128)(2,1)} collective-permute-done((bf16[12,384,128]{2,1,0:T(8,128)(2,1)}, bf16[12,384,128]{2,1,0:T(8,128)(2,1)}, u32[]{:S(2)}, u32[]{:S(2)}) %collective-permute-start.1) | collective-permute-done | bytes 1179680 | tf_op jit(solution)/shard_map/ppermute | solution.py:255
  32.9 3.3 %collective-permute-done.3.rt.rb.yr = bf16[12,384,128]{2,1,0:T(8,128)(2,1)S(1)} collective-permute-done((bf16[12,384,128]{2,1,0:T(8,128)(2,1)}, bf16[12,384,128]{2,1,0:T(8,128)(2,1)S(1)}, u32[]{:S(2)}, u32[]{:S(2)}) %collective-permute-start.3) | collective-permute-done | bytes 1179680 | tf_op jit(solution)/shard_map/ppermute | solution.py:255
  36.2 0.3 pack_corners.2
  36.6 0.7 copy-done.4
  37.3 4.9 %collective-permute-start.4 = (bf16[12,264,128]{2,1,0:T(8,128)(2,1)S(1)}, bf16[12,264,128]{2,1,0:T(8,128)(2,1)S(1)}, u32[]{:S(2)}, u32[]{:S(2)}) collective-permute-start(bf16[12,264,128]{2,1,0:T(8,128)(2,1)S(1)} %get-tuple-element.44), channel_id=1, source_target_pairs={{0,16},{16,32},{32,48},{48,64},{64,80},{80,96},{96,112},{1,17},{17... | collective-permute-start | bytes 2433032 | tf_op jit(solution)/shard_map/ppermute | solution.py:255
  42.1 1.9 %collective-permute-start.5 = (bf16[12,264,128]{2,1,0:T(8,128)(2,1)S(1)}, bf16[12,264,128]{2,1,0:T(8,128)(2,1)S(1)}, u32[]{:S(2)}, u32[]{:S(2)}) collective-permute-start(bf16[12,264,128]{2,1,0:T(8,128)(2,1)S(1)} %get-tuple-element.45), channel_id=1, source_target_pairs={{16,0},{32,16},{48,32},{64,48},{80,64},{96,80},{112,96},{17,1},{33... | collective-permute-start | bytes 2433032 | tf_op jit(solution)/shard_map/ppermute | solution.py:255
  44.1 8.9 %encode_early.1 = (bf16[12,768,128]{2,1,0:T(8,128)(2,1)S(1)}, bf16[12,384,128]{2,1,0:T(8,128)(2,1)S(1)}) custom-call(s32[54]{0:T(128)S(1)} %reshape.41.codes, bf16[12,1152,128]{2,1,0:T(8,128)(2,1)S(1)} %bitcast.30, bf16[12,384,128]{2,1,0:T(8,128)(2,1)} %collective-permute-done.xu, bf16[12,384,128]{2,1,0:T(8,128)(2,1)} %collective-permute-done.1.xd, ...), custom_call_target="tpu_custom_call" | custom-call | flops 2866544640 | bytes 11338456 | tf_op jit(solution)/shard_map/encode_early/pallas_call | solution.py:229
  53.1 2.7 %collective-permute-done.5.cd.cdt = bf16[12,264,128]{2,1,0:T(8,128)(2,1)S(1)} collective-permute-done((bf16[12,264,128]{2,1,0:T(8,128)(2,1)S(1)}, bf16[12,264,128]{2,1,0:T(8,128)(2,1)S(1)}, u32[]{:S(2)}, u32[]{:S(2)}) %collective-permute-start.5) | collective-permute-done | bytes 811040 | tf_op jit(solution)/shard_map/ppermute | solution.py:255
  55.7 1.1 copy-done.18
  56.8 9.8 %encode_late.1 = (bf16[12,1152,128]{2,1,0:T(8,128)(2,1)S(1)}, bf16[12,392,128]{2,1,0:T(8,128)(2,1)}, bf16[12,392,128]{2,1,0:T(8,128)(2,1)}, bf16[128,1536]{1,0:T(8,128)(2,1)S(1)}) custom-call(bf16[12,1152,128]{2,1,0:T(8,128)(2,1)S(1)} %bitcast.31, bf16[12,768,128]{2,1,0:T(8,128)(2,1)S(1)} %get-tuple-element.41.acc, ...), custom_call_target="tpu_custom_call" | custom-call | flops 1981808640 | bytes 21168640 | tf_op jit(solution)/shard_map/encode_late/pallas_call | solution.py:229
  66.6 4.3 %collective-permute-start.6 = (bf16[12,392,128]{2,1,0:T(8,128)(2,1)}, bf16[12,392,128]{2,1,0:T(8,128)(2,1)}, u32[]{:S(2)}, u32[]{:S(2)}) collective-permute-start(bf16[12,392,128]{2,1,0:T(8,128)(2,1)} %get-tuple-element.53), channel_id=1, source_target_pairs={{0,1},{1,2},{2,3},{3,4},{4,5},{5,6},{6,7},{7,8},{8,9},{9,10},{10,1... | collective-permute-start | bytes 3612680 | tf_op jit(solution)/shard_map/ppermute | solution.py:255
  70.8 1.3 collective-permute-start.7
  72.1 1.6 %pack_rows.3 = (bf16[12,384,128]{2,1,0:T(8,128)(2,1)S(1)}, bf16[12,384,128]{2,1,0:T(8,128)(2,1)}) custom-call(bf16[12,1152,128]{2,1,0:T(8,128)(2,1)S(1)} %get-tuple-element.52.own.x), custom_call_target="tpu_custom_call" | custom-call | flops 1 | bytes 5898240 | tf_op jit(solution)/shard_map/pack_rows/pallas_call | solution.py:229
  73.8 1.0 copy-done.23
  74.8 2.0 %collective-permute-start.8 = (bf16[12,384,128]{2,1,0:T(8,128)(2,1)}, bf16[12,384,128]{2,1,0:T(8,128)(2,1)}, u32[]{:S(2)}, u32[]{:S(2)}) collective-permute-start(bf16[12,384,128]{2,1,0:T(8,128)(2,1)} %get-tuple-element.56), channel_id=1, source_target_pairs={{0,16},{16,32},{32,48},{48,64},{64,80},{80,96},{96,112},{1,17},{17... | collective-permute-start | bytes 3538952 | tf_op jit(solution)/shard_map/ppermute | solution.py:255
  76.9 0.8 copy-done.20
  77.6 1.8 %reshape.45 = bf16[128,2,768]{2,1,0:T(2,128)(2,1)} reshape(bf16[128,1536]{1,0:T(8,128)(2,1)} %copy-done.20) | data formatting | bytes 786432 | tf_op jit(solution)/shard_map/reshape | solution.py:349
  79.5 11.7 %all-to-all-start = ((bf16[128,2,768]{2,1,0:T(2,128)(2,1)}), bf16[128,2,768]{2,1,0:T(2,128)(2,1)}, u32[]{:S(2)}, u32[]{:S(2)}) async-start(bf16[128,2,768]{2,1,0:T(2,128)(2,1)} %reshape.45), calls=%async_computation | async-start | bytes 786432 | tf_op jit(solution)/shard_map/all_to_all | solution.py:354
  91.2 3.0 %collective-permute-start.11 = (bf16[12,384,128]{2,1,0:T(8,128)(2,1)}, bf16[12,384,128]{2,1,0:T(8,128)(2,1)}, u32[]{:S(2)}, u32[]{:S(2)}) collective-permute-start(bf16[12,384,128]{2,1,0:T(8,128)(2,1)} %copy-done.23), channel_id=1, source_target_pairs={{16,0},{32,16},{48,32},{64,48},{80,64},{96,80},{112,96},{17,1},{33... | collective-permute-start | bytes 3538952 | tf_op jit(solution)/shard_map/ppermute | solution.py:255
  94.2 1.5 copy-done.15
  95.7 4.7 %decode_early.1.acc = bf16[12,1152,128]{2,1,0:T(8,128)(2,1)S(1)} custom-call(s32[54]{0:T(128)S(1)} %reshape.41.codes, bf16[12,1152,128]{2,1,0:T(8,128)(2,1)S(1)} %get-tuple-element.52.own.x, bf16[9,6,128,128]{3,2,1,0:T(8,128)(2,1)S(1)} %copy-done.15), custom_call_target="tpu_custom_call" | custom-call | flops 2717908992 | bytes 8847576 | tf_op jit(solution)/shard_map/decode_early/pallas_call | solution.py:229
  100.4 1.8 %copy-done.8 = bf16[12,1152,128]{2,1,0:T(8,128)(2,1)} copy-done((bf16[12,1152,128]{2,1,0:T(8,128)(2,1)}, bf16[12,1152,128]{2,1,0:T(8,128)(2,1)S(1)}, u32[]{:S(2)}) %copy-start.8) | copy-done | bytes 3538968
  102.2 2.4 %all-to-all-done = bf16[128,2,768]{2,1,0:T(2,128)(2,1)} async-done(((bf16[128,2,768]{2,1,0:T(2,128)(2,1)}), bf16[128,2,768]{2,1,0:T(2,128)(2,1)}, u32[]{:S(2)}, u32[]{:S(2)}) %all-to-all-start) | async-done | bytes 393248 | tf_op jit(solution)/shard_map/all_to_all | solution.py:354
  104.6 1.4 convert_reduce_fusion
  106.0 1.0 broadcast_in_dim.42
  107.0 12.1 %all-to-all-start.1 = ((bf16[128,2,768]{2,1,0:T(2,128)(2,1)}), bf16[128,2,768]{2,1,0:T(2,128)(2,1)S(1)}, u32[]{:S(2)}, u32[]{:S(2)}) async-start(bf16[128,2,768]{2,1,0:T(2,128)(2,1)} %broadcast_in_dim.42), calls=%async_computation.1 | async-start | bytes 786432 | tf_op jit(solution)/shard_map/all_to_all | solution.py:358
  119.1 2.5 %pack_corners.3 = (bf16[12,264,128]{2,1,0:T(8,128)(2,1)S(1)}, bf16[12,264,128]{2,1,0:T(8,128)(2,1)S(1)}) custom-call(bf16[12,392,128]{2,1,0:T(8,128)(2,1)} %collective-permute-done.6.lt.lb.ylt.yl, bf16[12,392,128]{2,1,0:T(8,128)(2,1)} %collective-permute-done.6.lt.lb.ylt.yl, bf16[12,392,128]{2,1,0:T(8,128)(2,1)} %collective-permute-done.7.rt.rb.yrt.yr, ...), custom_call_target="tpu_custom_call" | custom-call | flops 1 | bytes 6443008 | tf_op jit(solution)/shard_map/pack_corners/pallas_call | solution.py:229
  121.6 3.5 %collective-permute-start.9 = (bf16[12,264,128]{2,1,0:T(8,128)(2,1)S(1)}, bf16[12,264,128]{2,1,0:T(8,128)(2,1)S(1)}, u32[]{:S(2)}, u32[]{:S(2)}) collective-permute-start(bf16[12,264,128]{2,1,0:T(8,128)(2,1)S(1)} %get-tuple-element.60), channel_id=1, source_target_pairs={{0,16},{16,32},{32,48},{48,64},{64,80},{80,96},{96,112},{1,17},{17... | collective-permute-start | bytes 2433032 | tf_op jit(solution)/shard_map/ppermute | solution.py:255
  125.2 1.9 %collective-permute-start.10 = (bf16[12,264,128]{2,1,0:T(8,128)(2,1)S(1)}, bf16[12,264,128]{2,1,0:T(8,128)(2,1)}, u32[]{:S(2)}, u32[]{:S(2)}) collective-permute-start(bf16[12,264,128]{2,1,0:T(8,128)(2,1)S(1)} %get-tuple-element.61), channel_id=1, source_target_pairs={{16,0},{32,16},{48,32},{64,48},{80,64},{96,80},{112,96},{17,1},{33... | collective-permute-start | bytes 2433032 | tf_op jit(solution)/shard_map/ppermute | solution.py:255
  127.1 2.7 %owner_mix.1.mown = bf16[9,128,128]{2,1,0:T(8,128)(2,1)S(1)} custom-call(s32[54]{0:T(128)S(1)} %reshape.41.codes, bf16[9,6,128,128]{3,2,1,0:T(8,128)(2,1)S(1)} %copy-done.16, bf16[16,128]{1,0:T(8,128)(2,1)S(1)} %pad.19.owners, bf16[12,264,128]{2,1,0:T(8,128)(2,1)S(1)} %copy-done.10, bf16[12,264,128]{2,1,0:T(8,128)(2,1)S(1)} %copy-done.12, ...), custom_call_target="tpu_custom_call" | custom-call | flops 17179869184 | bytes 6099160 | tf_op jit(solution)/shard_map/owner_mix/pallas_call | solution.py:229
  129.8 0.7 copy-done.21
  130.6 1.3 all-to-all-done.1
  131.8 0.8 copy.20
  132.7 1.7 %collective-permute-done.9.cu = bf16[12,264,128]{2,1,0:T(8,128)(2,1)S(1)} collective-permute-done((bf16[12,264,128]{2,1,0:T(8,128)(2,1)S(1)}, bf16[12,264,128]{2,1,0:T(8,128)(2,1)S(1)}, u32[]{:S(2)}, u32[]{:S(2)}) %collective-permute-start.9) | collective-permute-done | bytes 811040 | tf_op jit(solution)/shard_map/ppermute | solution.py:255
  134.4 4.5 %collective-permute-done.10.cd = bf16[12,264,128]{2,1,0:T(8,128)(2,1)} collective-permute-done((bf16[12,264,128]{2,1,0:T(8,128)(2,1)S(1)}, bf16[12,264,128]{2,1,0:T(8,128)(2,1)}, u32[]{:S(2)}, u32[]{:S(2)}) %collective-permute-start.10) | collective-permute-done | bytes 811040 | tf_op jit(solution)/shard_map/ppermute | solution.py:255
  138.9 11.8 %decode_late.1 = bf16[12,1152,128]{2,1,0:T(8,128)(2,1)} custom-call(bf16[12,1152,128]{2,1,0:T(8,128)(2,1)} %copy-done, bf16[12,1152,128]{2,1,0:T(8,128)(2,1)} %copy-done.8, bf16[12,392,128]{2,1,0:T(8,128)(2,1)} %collective-permute-done.6.lt.lb.ylt.yl, bf16[12,392,128]{2,1,0:T(8,128)(2,1)} %collective-permute-done.7.rt.rb.yrt.yr, ...), custom_call_target="tpu_custom_call" | custom-call | flops 1358954496 | bytes 19333120 | tf_op jit(solution)/shard_map/decode_late/pallas_call | solution.py:229
  (78 shorter events, 0.9 us)
Async XLA Ops:
  0.0 8.9 %copy-start.6 = (bf16[1152,12,128]{2,0,1:T(8,128)(2,1)S(1)}, bf16[1152,12,128]{2,0,1:T(8,128)(2,1)}, u32[]{:S(2)}) copy-start(bf16[1152,12,128]{2,0,1:T(8,128)(2,1)} %param.11) | copy-start | bytes 10616836
  3.5 29.4 %collective-permute-start.2 = (bf16[12,384,128]{2,1,0:T(8,128)(2,1)}, bf16[12,384,128]{2,1,0:T(8,128)(2,1)S(1)}, u32[]{:S(2)}, u32[]{:S(2)}) collective-permute-start(bf16[12,384,128]{2,1,0:T(8,128)(2,1)} %bitcast.2), channel_id=1, source_target_pairs={{0,1},{1,2},{2,3},{3,4},{4,5},{5,6},{6,7},{7,8},{8,9},{9,10},{10,1... | collective-permute-start | bytes 3538952 | tf_op jit(solution)/shard_map/ppermute | solution.py:255
  7.6 28.6 %collective-permute-start.3 = (bf16[12,384,128]{2,1,0:T(8,128)(2,1)}, bf16[12,384,128]{2,1,0:T(8,128)(2,1)S(1)}, u32[]{:S(2)}, u32[]{:S(2)}) collective-permute-start(bf16[12,384,128]{2,1,0:T(8,128)(2,1)} %bitcast.3), channel_id=1, source_target_pairs={{1,0},{2,1},{3,2},{4,3},{5,4},{6,5},{7,6},{8,7},{9,8},{10,9},{11,1... | collective-permute-start | bytes 3538952 | tf_op jit(solution)/shard_map/ppermute | solution.py:255
  8.9 7.9 %copy-start.25 = (s32[1152]{0:T(1024)S(1)}, s32[1152]{0:T(1024)}, u32[]{:S(2)}) copy-start(s32[1152]{0:T(1024)} %param.17) | copy-start | bytes 13828
  8.9 7.9 %copy-start.30 = (s32[144,1]{0,1:T(1,128)S(1)}, s32[144,1]{0,1:T(1,128)}, u32[]{:S(2)}) copy-start(s32[144,1]{0,1:T(1,128)} %param.18) | copy-start | bytes 1732
  8.9 9.1 %copy-start.26 = (bf16[128,128]{1,0:T(8,128)(2,1)S(1)}, bf16[128,128]{1,0:T(8,128)(2,1)}, u32[]{:S(2)}) copy-start(bf16[128,128]{1,0:T(8,128)(2,1)} %param.21) | copy-start | bytes 98308
  9.0 9.7 %copy-start.32 = (pred[8]{0:T(512)(128)(4,1)S(1)}, pred[8]{0:T(512)(128)(4,1)}, u32[]{:S(2)}) copy-start(pred[8]{0:T(512)(128)(4,1)} %constant.12.clone.1) | copy-start | bytes 28
  9.0 9.8 %copy-start.27 = (bf16[128,128]{1,0:T(8,128)(2,1)S(1)}, bf16[128,128]{1,0:T(8,128)(2,1)}, u32[]{:S(2)}) copy-start(bf16[128,128]{1,0:T(8,128)(2,1)} %param.15) | copy-start | bytes 98308
  9.0 9.8 %copy-start.28 = (bf16[128,128]{1,0:T(8,128)(2,1)S(1)}, bf16[128,128]{1,0:T(8,128)(2,1)}, u32[]{:S(2)}) copy-start(bf16[128,128]{1,0:T(8,128)(2,1)} %param.19) | copy-start | bytes 98308
  9.0 10.4 %copy-start.31 = (s32[9,6]{0,1:T(8,128)S(1)}, s32[9,6]{0,1:T(8,128)}, u32[]{:S(2)}) copy-start(s32[9,6]{0,1:T(8,128)} %param.13) | copy-start | bytes 652
  10.9 17.4 %collective-permute-start = (bf16[12,384,128]{2,1,0:T(8,128)(2,1)}, bf16[12,384,128]{2,1,0:T(8,128)(2,1)}, u32[]{:S(2)}, u32[]{:S(2)}) collective-permute-start(bf16[12,384,128]{2,1,0:T(8,128)(2,1)} %get-tuple-element.36), channel_id=1, source_target_pairs={{0,16},{16,32},{32,48},{48,64},{64,80},{80,96},{96,112},{1,17},{17... | collective-permute-start | bytes 3538952 | tf_op jit(solution)/shard_map/ppermute | solution.py:255
  14.9 18.0 %collective-permute-start.1 = (bf16[12,384,128]{2,1,0:T(8,128)(2,1)}, bf16[12,384,128]{2,1,0:T(8,128)(2,1)}, u32[]{:S(2)}, u32[]{:S(2)}) collective-permute-start(bf16[12,384,128]{2,1,0:T(8,128)(2,1)} %get-tuple-element.37), channel_id=1, source_target_pairs={{16,0},{32,16},{48,32},{64,48},{80,64},{96,80},{112,96},{17,1},{33... | collective-permute-start | bytes 3538952 | tf_op jit(solution)/shard_map/ppermute | solution.py:255
  19.4 24.6 %copy-start.17 = (bf16[256,256]{1,0:T(8,128)(2,1)}, bf16[256,256]{1,0:T(8,128)(2,1)S(1)}, u32[]{:S(2)}) copy-start(bf16[256,256]{1,0:T(8,128)(2,1)S(1)} %get-tuple-element.40.w_mix) | copy-start | bytes 393220
  19.6 1.5 copy-start.13
  21.1 2.0 %copy-start.29 = (bf16[1152]{0:T(1024)(128)(2,1)S(1)}, bf16[1152]{0:T(1024)(128)(2,1)}, u32[]{:S(2)}) copy-start(bf16[1152]{0:T(1024)(128)(2,1)} %param.16) | copy-start | bytes 6916
  23.1 32.6 %copy-start.1 = (bf16[12,128,384]{2,1,0:T(8,128)(2,1)}, bf16[12,128,384]{2,1,0:T(8,128)(2,1)S(1)}, u32[]{:S(2)}) copy-start(bf16[12,128,384]{2,1,0:T(8,128)(2,1)S(1)} %late_weights.1.late) | copy-start | bytes 3538948
  23.2 20.9 %copy-start.14 = (bf16[9,6,128,128]{3,2,1,0:T(8,128)(2,1)S(1)}, bf16[9,6,128,128]{3,2,1,0:T(8,128)(2,1)}, u32[]{:S(2)}) copy-start(bf16[9,6,128,128]{3,2,1,0:T(8,128)(2,1)} %adj.7) | copy-start | bytes 5308420
  32.9 11.2 %copy-start.7 = (bf16[1152,12,128]{2,0,1:T(8,128)(2,1)S(1)}, bf16[1152,12,128]{2,0,1:T(8,128)(2,1)}, u32[]{:S(2)}) copy-start(bf16[1152,12,128]{2,0,1:T(8,128)(2,1)} %param.11) | copy-start | bytes 10616836
  32.9 11.2 %copy-start.22 = (f32[128]{0:T(128)S(1)}, f32[128]{0:T(128)}, u32[]{:S(2)}) copy-start(f32[128]{0:T(128)} %param.14) | copy-start | bytes 1540
  32.9 3.6 %copy-start.2 = (bf16[12,384,128]{2,1,0:T(8,128)(2,1)}, bf16[12,384,128]{2,1,0:T(8,128)(2,1)S(1)}, u32[]{:S(2)}) copy-start(bf16[12,384,128]{2,1,0:T(8,128)(2,1)S(1)} %collective-permute-done.2.lt.lb.yl) | copy-start | bytes 3538948
  36.2 1.0 copy-start.4
  37.3 15.8 %collective-permute-start.4 = (bf16[12,264,128]{2,1,0:T(8,128)(2,1)S(1)}, bf16[12,264,128]{2,1,0:T(8,128)(2,1)S(1)}, u32[]{:S(2)}, u32[]{:S(2)}) collective-permute-start(bf16[12,264,128]{2,1,0:T(8,128)(2,1)S(1)} %get-tuple-element.44), channel_id=1, source_target_pairs={{0,16},{16,32},{32,48},{48,64},{64,80},{80,96},{96,112},{1,17},{17... | collective-permute-start | bytes 2433032 | tf_op jit(solution)/shard_map/ppermute | solution.py:255
  42.1 13.6 %collective-permute-start.5 = (bf16[12,264,128]{2,1,0:T(8,128)(2,1)S(1)}, bf16[12,264,128]{2,1,0:T(8,128)(2,1)S(1)}, u32[]{:S(2)}, u32[]{:S(2)}) collective-permute-start(bf16[12,264,128]{2,1,0:T(8,128)(2,1)S(1)} %get-tuple-element.45), channel_id=1, source_target_pairs={{16,0},{32,16},{48,32},{64,48},{80,64},{96,80},{112,96},{17,1},{33... | collective-permute-start | bytes 2433032 | tf_op jit(solution)/shard_map/ppermute | solution.py:255
  44.1 11.6 %copy-start.3 = (bf16[12,384,128]{2,1,0:T(8,128)(2,1)S(1)}, bf16[12,384,128]{2,1,0:T(8,128)(2,1)}, u32[]{:S(2)}) copy-start(bf16[12,384,128]{2,1,0:T(8,128)(2,1)} %copy-done.2) | copy-start | bytes 3538948
  44.1 11.6 %copy-start.5 = (bf16[12,384,128]{2,1,0:T(8,128)(2,1)S(1)}, bf16[12,384,128]{2,1,0:T(8,128)(2,1)}, u32[]{:S(2)}) copy-start(bf16[12,384,128]{2,1,0:T(8,128)(2,1)} %copy-done.4) | copy-start | bytes 3538948
  44.1 11.6 %copy-start.19 = (bf16[256,256]{1,0:T(8,128)(2,1)S(1)}, bf16[256,256]{1,0:T(8,128)(2,1)}, u32[]{:S(2)}) copy-start(bf16[256,256]{1,0:T(8,128)(2,1)} %get-tuple-element.47.w_coarse) | copy-start | bytes 393220
  53.0 13.5 %copy-start.9 = (bf16[12,264,128]{2,1,0:T(8,128)(2,1)}, bf16[12,264,128]{2,1,0:T(8,128)(2,1)S(1)}, u32[]{:S(2)}) copy-start(bf16[12,264,128]{2,1,0:T(8,128)(2,1)S(1)} %collective-permute-done.4.cu.cut) | copy-start | bytes 2433028
  55.7 10.9 %copy-start.11 = (bf16[12,264,128]{2,1,0:T(8,128)(2,1)}, bf16[12,264,128]{2,1,0:T(8,128)(2,1)S(1)}, u32[]{:S(2)}) copy-start(bf16[12,264,128]{2,1,0:T(8,128)(2,1)S(1)} %collective-permute-done.5.cd.cdt) | copy-start | bytes 2433028
  55.7 1.1 copy-start.18
  66.6 27.6 %copy-start = (bf16[12,1152,128]{2,1,0:T(8,128)(2,1)}, bf16[12,1152,128]{2,1,0:T(8,128)(2,1)S(1)}, u32[]{:S(2)}) copy-start(bf16[12,1152,128]{2,1,0:T(8,128)(2,1)S(1)} %get-tuple-element.52.own.x) | copy-start | bytes 10616836
  66.6 52.5 %collective-permute-start.6 = (bf16[12,392,128]{2,1,0:T(8,128)(2,1)}, bf16[12,392,128]{2,1,0:T(8,128)(2,1)}, u32[]{:S(2)}, u32[]{:S(2)}) collective-permute-start(bf16[12,392,128]{2,1,0:T(8,128)(2,1)} %get-tuple-element.53), channel_id=1, source_target_pairs={{0,1},{1,2},{2,3},{3,4},{4,5},{5,6},{6,7},{7,8},{8,9},{9,10},{10,1... | collective-permute-start | bytes 3612680 | tf_op jit(solution)/shard_map/ppermute | solution.py:255
  70.8 48.3 %collective-permute-start.7 = (bf16[12,392,128]{2,1,0:T(8,128)(2,1)}, bf16[12,392,128]{2,1,0:T(8,128)(2,1)}, u32[]{:S(2)}, u32[]{:S(2)}) collective-permute-start(bf16[12,392,128]{2,1,0:T(8,128)(2,1)} %get-tuple-element.54), channel_id=1, source_target_pairs={{1,0},{2,1},{3,2},{4,3},{5,4},{6,5},{7,6},{8,7},{9,8},{10,9},{11,1... | collective-permute-start | bytes 3612680 | tf_op jit(solution)/shard_map/ppermute | solution.py:255
  73.8 1.0 copy-start.23
  74.8 31.2 %collective-permute-start.8 = (bf16[12,384,128]{2,1,0:T(8,128)(2,1)}, bf16[12,384,128]{2,1,0:T(8,128)(2,1)}, u32[]{:S(2)}, u32[]{:S(2)}) collective-permute-start(bf16[12,384,128]{2,1,0:T(8,128)(2,1)} %get-tuple-element.56), channel_id=1, source_target_pairs={{0,16},{16,32},{32,48},{48,64},{64,80},{80,96},{96,112},{1,17},{17... | collective-permute-start | bytes 3538952 | tf_op jit(solution)/shard_map/ppermute | solution.py:255
  76.9 0.8 copy-start.20
  79.5 25.2 %all-to-all-start = ((bf16[128,2,768]{2,1,0:T(2,128)(2,1)}), bf16[128,2,768]{2,1,0:T(2,128)(2,1)}, u32[]{:S(2)}, u32[]{:S(2)}) async-start(bf16[128,2,768]{2,1,0:T(2,128)(2,1)} %reshape.45), calls=%async_computation | async-start | bytes 786432 | tf_op jit(solution)/shard_map/all_to_all | solution.py:354
  91.2 41.5 %collective-permute-start.11 = (bf16[12,384,128]{2,1,0:T(8,128)(2,1)}, bf16[12,384,128]{2,1,0:T(8,128)(2,1)}, u32[]{:S(2)}, u32[]{:S(2)}) collective-permute-start(bf16[12,384,128]{2,1,0:T(8,128)(2,1)} %copy-done.23), channel_id=1, source_target_pairs={{16,0},{32,16},{48,32},{64,48},{80,64},{96,80},{112,96},{17,1},{33... | collective-permute-start | bytes 3538952 | tf_op jit(solution)/shard_map/ppermute | solution.py:255
  94.2 1.5 copy-start.15
  100.4 1.8 %copy-start.8 = (bf16[12,1152,128]{2,1,0:T(8,128)(2,1)}, bf16[12,1152,128]{2,1,0:T(8,128)(2,1)S(1)}, u32[]{:S(2)}) copy-start(bf16[12,1152,128]{2,1,0:T(8,128)(2,1)S(1)} %decode_early.1.acc) | copy-start | bytes 10616836
  107.0 24.9 %all-to-all-start.1 = ((bf16[128,2,768]{2,1,0:T(2,128)(2,1)}), bf16[128,2,768]{2,1,0:T(2,128)(2,1)S(1)}, u32[]{:S(2)}, u32[]{:S(2)}) async-start(bf16[128,2,768]{2,1,0:T(2,128)(2,1)} %broadcast_in_dim.42), calls=%async_computation.1 | async-start | bytes 786432 | tf_op jit(solution)/shard_map/all_to_all | solution.py:358
  119.1 8.0 %copy-start.10 = (bf16[12,264,128]{2,1,0:T(8,128)(2,1)S(1)}, bf16[12,264,128]{2,1,0:T(8,128)(2,1)}, u32[]{:S(2)}) copy-start(bf16[12,264,128]{2,1,0:T(8,128)(2,1)} %copy-done.9) | copy-start | bytes 2433028
  119.1 8.0 %copy-start.12 = (bf16[12,264,128]{2,1,0:T(8,128)(2,1)S(1)}, bf16[12,264,128]{2,1,0:T(8,128)(2,1)}, u32[]{:S(2)}) copy-start(bf16[12,264,128]{2,1,0:T(8,128)(2,1)} %copy-done.11) | copy-start | bytes 2433028
  119.1 8.0 %copy-start.16 = (bf16[9,6,128,128]{3,2,1,0:T(8,128)(2,1)S(1)}, bf16[9,6,128,128]{3,2,1,0:T(8,128)(2,1)}, u32[]{:S(2)}) copy-start(bf16[9,6,128,128]{3,2,1,0:T(8,128)(2,1)} %adj.7) | copy-start | bytes 5308420
  121.6 12.7 %collective-permute-start.9 = (bf16[12,264,128]{2,1,0:T(8,128)(2,1)S(1)}, bf16[12,264,128]{2,1,0:T(8,128)(2,1)S(1)}, u32[]{:S(2)}, u32[]{:S(2)}) collective-permute-start(bf16[12,264,128]{2,1,0:T(8,128)(2,1)S(1)} %get-tuple-element.60), channel_id=1, source_target_pairs={{0,16},{16,32},{32,48},{48,64},{64,80},{80,96},{96,112},{1,17},{17... | collective-permute-start | bytes 2433032 | tf_op jit(solution)/shard_map/ppermute | solution.py:255
  125.2 13.7 %collective-permute-start.10 = (bf16[12,264,128]{2,1,0:T(8,128)(2,1)S(1)}, bf16[12,264,128]{2,1,0:T(8,128)(2,1)}, u32[]{:S(2)}, u32[]{:S(2)}) collective-permute-start(bf16[12,264,128]{2,1,0:T(8,128)(2,1)S(1)} %get-tuple-element.61), channel_id=1, source_target_pairs={{16,0},{32,16},{48,32},{64,48},{80,64},{96,80},{112,96},{17,1},{33... | collective-permute-start | bytes 2433032 | tf_op jit(solution)/shard_map/ppermute | solution.py:255
  129.8 0.7 copy-start.21
  134.3 4.5 %copy-start.24 = (bf16[12,264,128]{2,1,0:T(8,128)(2,1)}, bf16[12,264,128]{2,1,0:T(8,128)(2,1)S(1)}, u32[]{:S(2)}) copy-start(bf16[12,264,128]{2,1,0:T(8,128)(2,1)S(1)} %collective-permute-done.9.cu) | copy-start | bytes 2433028

commit v3 on v2

--- a/solution.py
+++ b/solution.py
@@ -10,7 +10,7 @@
 EXT = GB + 2
 ROWS = GB * GB * BLK
 SIDE = GB * BLK
-PAIR = 4
+PAIR = 6
 WIDE = PAIR * C
 bf16, f32 = jnp.bfloat16, jnp.float32
 ACC = bf16
@@ -262,6 +262,19 @@
         out[:, 2 * BLK :, :] = jnp.broadcast_to(tails[k][None], (out.shape[0], TAIL, C))
 
 
+def sides_kernel(*refs):
+    for k, out in enumerate(refs[-2:]):
+        for a in range(GB):
+            out[:, span(a), :] = refs[k * GB + a][...]
+
+
+def sides(x):
+    block = lambda k: pl.BlockSpec((PAIR, BLK, C), lambda p, *_: (p, k, 0))
+    return call(sides_kernel, "pack_sides", x.shape[0], [x] * (2 * GB),
+                [block(a * GB + b) for b in (GB - 1, 0) for a in range(GB)],
+                [sds((x.shape[0], SIDE, C))] * 2, [by_step(SIDE)] * 2, [], 1, vmem=60)
+
+
 def rows_kernel(x, top, bottom):
     top[...] = x[:, :SIDE, :]
     bottom[...] = x[:, ROWS - SIDE :, :]
@@ -303,7 +316,7 @@
     node_owner = jnp.sum(jnp.where(hit, owner[:, None], 0), axis=0)
     owners = (node_owner + 1).astype(bf16).reshape(GB * GB, BLK)
 
-    right, left = flat(squares[:, :, GB - 1]), flat(squares[:, :, 0])
+    right, left = sides(x)
     yl = shift(right, "ry", True)
     yr = shift(left, "ry", False)
     x_late, _, _ = lax.optimization_barrier((x, right, left))
@@ -348,7 +361,7 @@
     (part,) = call(part_kernel, "part", PAIR, [part], [whole(part.shape)], [sds(part.shape)], [whole(part.shape)], [], HINT, vmem=4)
     part = part.reshape(devices, 2, steps * C // 2)
     (acc,) = call(decode_early, "decode_early", steps, [codes, d1, adjacency], [by_step(ROWS), whole(adjacency.shape)],
-                  [sds((steps, ROWS, C), ACC)], [by_step(ROWS)], [ext], work * NB * BLK, prefetch=1)
+                  [sds((steps, ROWS, C), ACC)], [by_step(ROWS)], [ext], work * NB * BLK, prefetch=1, vmem=60)
     xu, xd, top = rows_halo(d1, 1)
     half = (devices, 2, steps * C // 2)
     arrived = lax.all_to_all(part, ("rx", "ry"), split_axis=0, concat_axis=0, tiled=True)

time: 151 us -> 148 us (0.980)
  local copies, waits for them, and re-layouts: 16.4 us -> 9.05 us
  Pallas kernels: 46.3 us -> 49 us
    unnamed x68 -> x56, local copies, waits for them, and re-layouts: 10 us -> 6.44 us
    slice x1 -> x0, local copies, waits for them, and re-layouts: 3.51 us -> none  [on_device(): right, left = (flat(squares[:, :, GB - 1]), flat(squares[:, :, 0]))]
    pallas_call x11 -> x12, Pallas kernels: 46.3 us -> 49 us  [call(): pl.pallas_call(kernel, grid_spec=pltpu.PrefetchScalarGridSpec(num_scalar_...]
    ppermute x12, waiting for transfers between devices: 21.6 us -> 19.7 us  [shift(): lax.ppermute(block, axis, pairs if up else [(b, a) for a, b in pairs])]
    all_to_all x1, waiting for transfers between devices: 2.41 us -> 4.03 us  [on_device(): lax.all_to_all(part, ('rx', 'ry'), split_axis=0, concat_axis=0, tiled=True)]
  transfers between devices with their start and end apart: 14 -> 14, of which waited for: 8 -> 8; matrix products, arithmetic and copies ran while one was open for 5% -> 6% of each run, Pallas kernels for 16% -> 16%
where the time goes in v3:
time: 148 us; the launch traced here: 147 us
  starting transfers between devices  59 us (40%)
  Pallas kernels  49 us (33%)
  waiting for transfers between devices  26.5 us (18%)
  local copies, waits for them, and re-layouts  9.05 us (6%)
  other arithmetic  3.24 us (2%)
    pallas_call x12, Pallas kernels, call(): pl.pallas_call(kernel, grid_spec=pltpu.PrefetchScalarGridSpec(num_scalar_...  49 us
    ppermute x12, starting transfers between devices, shift(): lax.ppermute(block, axis, pairs if up else [(b, a) for a, b in pairs])  33.6 us
    ppermute x12, waiting for transfers between devices, shift(): lax.ppermute(block, axis, pairs if up else [(b, a) for a, b in pairs])  19.7 us
    all_to_all x1, starting transfers between devices, on_device(): lax.all_to_all(everyone, ('rx', 'ry'), split_axis=0, concat_axis=0, tiled...  13 us
    all_to_all x1, starting transfers between devices, on_device(): lax.all_to_all(part, ('rx', 'ry'), split_axis=0, concat_axis=0, tiled=True)  12.3 us
    unnamed x56, local copies, waits for them, and re-layouts  6.44 us
    all_to_all x1, waiting for transfers between devices, on_device(): lax.all_to_all(part, ('rx', 'ry'), split_axis=0, concat_axis=0, tiled=True)  4.03 us
  transfers between devices with their start and end apart: 14, of which 8 were waited for; matrix products, arithmetic and copies ran while one was open for 6% of the time, Pallas kernels for 16%

profile of v3, /device:TPU:1, one launch (start us, length us, event | category | flops | bytes accessed | tf_op | source)
XLA Modules:
  0.0 147.2 jit_solution(13793244338501277722)
XLA Ops:
  0.0 3.0 %pack_sides.1 = (bf16[12,384,128]{2,1,0:T(8,128)(2,1)}, bf16[12,384,128]{2,1,0:T(8,128)(2,1)}) custom-call(bf16[12,1152,128]{2,1,0:T(8,128)(2,1)} %bitcast.20, bf16[12,1152,128]{2,1,0:T(8,128)(2,1)} %bitcast.21, bf16[12,1152,128]{2,1,0:T(8,128)(2,1)} %bitcast.22, bf16[12,1152,128]{2,1,0:T(8,128)(2,1)} %bitcast.23, bf16[12,1152,128]{2,1,0:T(8,128)(2,1)} %bitcast.24, ...), custom_call_target="tpu_custom_call" | custom-call | flops 1 | bytes 23592960 | tf_op jit(solution)/shard_map/pack_sides/pallas_call | solution.py:229
  3.0 5.1 %collective-permute-start.2 = (bf16[12,384,128]{2,1,0:T(8,128)(2,1)}, bf16[12,384,128]{2,1,0:T(8,128)(2,1)}, u32[]{:S(2)}, u32[]{:S(2)}) collective-permute-start(bf16[12,384,128]{2,1,0:T(8,128)(2,1)} %get-tuple-element.37), channel_id=1, source_target_pairs={{0,1},{1,2},{2,3},{3,4},{4,5},{5,6},{6,7},{7,8},{8,9},{9,10},{10,1... | collective-permute-start | bytes 3538952 | tf_op jit(solution)/shard_map/ppermute | solution.py:255
  8.1 1.4 collective-permute-start.3
  9.5 1.5 %pack_rows.2 = (bf16[12,384,128]{2,1,0:T(8,128)(2,1)}, bf16[12,384,128]{2,1,0:T(8,128)(2,1)}) custom-call(bf16[12,1152,128]{2,1,0:T(8,128)(2,1)S(1)} %bitcast.26), custom_call_target="tpu_custom_call" | custom-call | flops 17179869184 | bytes 5898240 | tf_op jit(solution)/shard_map/pack_rows/pallas_call | solution.py:229
  11.0 3.9 %collective-permute-start = (bf16[12,384,128]{2,1,0:T(8,128)(2,1)}, bf16[12,384,128]{2,1,0:T(8,128)(2,1)}, u32[]{:S(2)}, u32[]{:S(2)}) collective-permute-start(bf16[12,384,128]{2,1,0:T(8,128)(2,1)} %get-tuple-element.40), channel_id=1, source_target_pairs={{0,16},{16,32},{32,48},{48,64},{64,80},{80,96},{96,112},{1,17},{17... | collective-permute-start | bytes 3538952 | tf_op jit(solution)/shard_map/ppermute | solution.py:255
  15.0 1.9 %collective-permute-start.1 = (bf16[12,384,128]{2,1,0:T(8,128)(2,1)}, bf16[12,384,128]{2,1,0:T(8,128)(2,1)}, u32[]{:S(2)}, u32[]{:S(2)}) collective-permute-start(bf16[12,384,128]{2,1,0:T(8,128)(2,1)} %get-tuple-element.41), channel_id=1, source_target_pairs={{16,0},{32,16},{48,32},{64,48},{80,64},{96,80},{112,96},{17,1},{33... | collective-permute-start | bytes 3538952 | tf_op jit(solution)/shard_map/ppermute | solution.py:255
  16.9 0.2 select_reduce_fusion
  17.1 0.9 fusion.2.hot
  18.0 0.7 fusion.11.w_out
  18.7 0.1 fusion.14
  18.8 0.7 fusion.9
  19.5 1.4 copy.13
  20.9 0.8 reshape.38.codes
  21.7 1.5 copy-done.9
  23.1 2.0 %late_weights.1.late = bf16[12,128,384]{2,1,0:T(8,128)(2,1)S(1)} custom-call(s32[54]{0:T(128)S(1)} %reshape.38.codes, bf16[9,6,128,128]{3,2,1,0:T(8,128)(2,1)S(1)} %copy-done.9), custom_call_target="tpu_custom_call" | custom-call | flops 1048576 | bytes 2949336 | tf_op jit(solution)/shard_map/late_weights/pallas_call | solution.py:229
  25.2 0.2 fusion.unpool
  25.5 2.9 %collective-permute-done.xu = bf16[12,384,128]{2,1,0:T(8,128)(2,1)} collective-permute-done((bf16[12,384,128]{2,1,0:T(8,128)(2,1)}, bf16[12,384,128]{2,1,0:T(8,128)(2,1)}, u32[]{:S(2)}, u32[]{:S(2)}) %collective-permute-start) | collective-permute-done | bytes 1179680 | tf_op jit(solution)/shard_map/ppermute | solution.py:255
  28.4 4.7 %collective-permute-done.1.xd = bf16[12,384,128]{2,1,0:T(8,128)(2,1)} collective-permute-done((bf16[12,384,128]{2,1,0:T(8,128)(2,1)}, bf16[12,384,128]{2,1,0:T(8,128)(2,1)}, u32[]{:S(2)}, u32[]{:S(2)}) %collective-permute-start.1) | collective-permute-done | bytes 1179680 | tf_op jit(solution)/shard_map/ppermute | solution.py:255
  33.1 3.8 %collective-permute-done.3.rt.rb.yr = bf16[12,384,128]{2,1,0:T(8,128)(2,1)} collective-permute-done((bf16[12,384,128]{2,1,0:T(8,128)(2,1)}, bf16[12,384,128]{2,1,0:T(8,128)(2,1)}, u32[]{:S(2)}, u32[]{:S(2)}) %collective-permute-start.3) | collective-permute-done | bytes 1179680 | tf_op jit(solution)/shard_map/ppermute | solution.py:255
  36.9 1.5 %pack_corners.2 = (bf16[12,264,128]{2,1,0:T(8,128)(2,1)S(1)}, bf16[12,264,128]{2,1,0:T(8,128)(2,1)S(1)}) custom-call(bf16[12,384,128]{2,1,0:T(8,128)(2,1)} %collective-permute-done.2.lt.lb.yl, bf16[12,384,128]{2,1,0:T(8,128)(2,1)} %collective-permute-done.2.lt.lb.yl, bf16[12,384,128]{2,1,0:T(8,128)(2,1)} %collective-permute-done.3.rt.rb.yr, ...), custom_call_target="tpu_custom_call" | custom-call | flops 1 | bytes 6344704 | tf_op jit(solution)/shard_map/pack_corners/pallas_call | solution.py:229
  38.5 4.9 %collective-permute-start.4 = (bf16[12,264,128]{2,1,0:T(8,128)(2,1)S(1)}, bf16[12,264,128]{2,1,0:T(8,128)(2,1)S(1)}, u32[]{:S(2)}, u32[]{:S(2)}) collective-permute-start(bf16[12,264,128]{2,1,0:T(8,128)(2,1)S(1)} %get-tuple-element.48), channel_id=1, source_target_pairs={{0,16},{16,32},{32,48},{48,64},{64,80},{80,96},{96,112},{1,17},{17... | collective-permute-start | bytes 2433032 | tf_op jit(solution)/shard_map/ppermute | solution.py:255
  43.3 1.9 %collective-permute-start.5 = (bf16[12,264,128]{2,1,0:T(8,128)(2,1)S(1)}, bf16[12,264,128]{2,1,0:T(8,128)(2,1)S(1)}, u32[]{:S(2)}, u32[]{:S(2)}) collective-permute-start(bf16[12,264,128]{2,1,0:T(8,128)(2,1)S(1)} %get-tuple-element.49), channel_id=1, source_target_pairs={{16,0},{32,16},{48,32},{64,48},{80,64},{96,80},{112,96},{17,1},{33... | collective-permute-start | bytes 2433032 | tf_op jit(solution)/shard_map/ppermute | solution.py:255
  45.3 7.7 %encode_early.1 = (bf16[12,768,128]{2,1,0:T(8,128)(2,1)S(1)}, bf16[12,384,128]{2,1,0:T(8,128)(2,1)S(1)}) custom-call(s32[54]{0:T(128)S(1)} %reshape.38.codes, bf16[12,1152,128]{2,1,0:T(8,128)(2,1)S(1)} %bitcast.27, bf16[12,384,128]{2,1,0:T(8,128)(2,1)} %collective-permute-done.xu, bf16[12,384,128]{2,1,0:T(8,128)(2,1)} %collective-permute-done.1.xd, ...), custom_call_target="tpu_custom_call" | custom-call | flops 2866544640 | bytes 11338456 | tf_op jit(solution)/shard_map/encode_early/pallas_call | solution.py:229
  53.1 3.9 %collective-permute-done.5.cd.cdt = bf16[12,264,128]{2,1,0:T(8,128)(2,1)S(1)} collective-permute-done((bf16[12,264,128]{2,1,0:T(8,128)(2,1)S(1)}, bf16[12,264,128]{2,1,0:T(8,128)(2,1)S(1)}, u32[]{:S(2)}, u32[]{:S(2)}) %collective-permute-start.5) | collective-permute-done | bytes 811040 | tf_op jit(solution)/shard_map/ppermute | solution.py:255
  56.9 9.5 %encode_late.1 = (bf16[12,1152,128]{2,1,0:T(8,128)(2,1)S(1)}, bf16[12,392,128]{2,1,0:T(8,128)(2,1)}, bf16[12,392,128]{2,1,0:T(8,128)(2,1)}, bf16[128,1536]{1,0:T(8,128)(2,1)S(1)}) custom-call(bf16[12,1152,128]{2,1,0:T(8,128)(2,1)S(1)} %bitcast.28, bf16[12,768,128]{2,1,0:T(8,128)(2,1)S(1)} %get-tuple-element.45.acc, ...), custom_call_target="tpu_custom_call" | custom-call | flops 1981808640 | bytes 21168640 | tf_op jit(solution)/shard_map/encode_late/pallas_call | solution.py:229
  66.4 2.3 %collective-permute-start.6 = (bf16[12,392,128]{2,1,0:T(8,128)(2,1)}, bf16[12,392,128]{2,1,0:T(8,128)(2,1)S(1)}, u32[]{:S(2)}, u32[]{:S(2)}) collective-permute-start(bf16[12,392,128]{2,1,0:T(8,128)(2,1)} %get-tuple-element.57), channel_id=1, source_target_pairs={{0,1},{1,2},{2,3},{3,4},{4,5},{5,6},{6,7},{7,8},{8,9},{9,10},{10,1... | collective-permute-start | bytes 3612680 | tf_op jit(solution)/shard_map/ppermute | solution.py:255
  68.7 1.3 collective-permute-start.7
  70.0 1.1 pack_rows.3
  71.2 1.0 copy-done.17
  72.2 2.0 %collective-permute-start.8 = (bf16[12,384,128]{2,1,0:T(8,128)(2,1)}, bf16[12,384,128]{2,1,0:T(8,128)(2,1)}, u32[]{:S(2)}, u32[]{:S(2)}) collective-permute-start(bf16[12,384,128]{2,1,0:T(8,128)(2,1)} %get-tuple-element.60), channel_id=1, source_target_pairs={{0,16},{16,32},{32,48},{48,64},{64,80},{80,96},{96,112},{1,17},{17... | collective-permute-start | bytes 3538952 | tf_op jit(solution)/shard_map/ppermute | solution.py:255
  74.2 0.9 reshape.41
  75.1 12.3 %all-to-all-start = ((bf16[128,2,768]{2,1,0:T(2,128)(2,1)}), bf16[128,2,768]{2,1,0:T(2,128)(2,1)S(1)}, u32[]{:S(2)}, u32[]{:S(2)}) async-start(bf16[128,2,768]{2,1,0:T(2,128)(2,1)} %reshape.41), calls=%async_computation | async-start | bytes 786432 | tf_op jit(solution)/shard_map/all_to_all | solution.py:367
  87.4 3.2 %collective-permute-start.11 = (bf16[12,384,128]{2,1,0:T(8,128)(2,1)}, bf16[12,384,128]{2,1,0:T(8,128)(2,1)}, u32[]{:S(2)}, u32[]{:S(2)}) collective-permute-start(bf16[12,384,128]{2,1,0:T(8,128)(2,1)} %copy-done.17), channel_id=1, source_target_pairs={{16,0},{32,16},{48,32},{64,48},{80,64},{96,80},{112,96},{17,1},{33... | collective-permute-start | bytes 3538952 | tf_op jit(solution)/shard_map/ppermute | solution.py:255
  90.6 8.3 %decode_early.1.acc = bf16[12,1152,128]{2,1,0:T(8,128)(2,1)} custom-call(s32[54]{0:T(128)} %copy-done.14, bf16[12,1152,128]{2,1,0:T(8,128)(2,1)} %copy-done.1, bf16[9,6,128,128]{3,2,1,0:T(8,128)(2,1)} %adj.7), custom_call_target="tpu_custom_call" | custom-call | flops 2717908992 | bytes 8847576 | tf_op jit(solution)/shard_map/decode_early/pallas_call | solution.py:229
  98.9 4.0 %all-to-all-done = bf16[128,2,768]{2,1,0:T(2,128)(2,1)S(1)} async-done(((bf16[128,2,768]{2,1,0:T(2,128)(2,1)}), bf16[128,2,768]{2,1,0:T(2,128)(2,1)S(1)}, u32[]{:S(2)}, u32[]{:S(2)}) %all-to-all-start) | async-done | bytes 393248 | tf_op jit(solution)/shard_map/all_to_all | solution.py:367
  102.9 0.4 convert_reduce_fusion
  103.3 1.0 broadcast_in_dim.42
  104.3 13.0 %all-to-all-start.1 = ((bf16[128,2,768]{2,1,0:T(2,128)(2,1)}), bf16[128,2,768]{2,1,0:T(2,128)(2,1)}, u32[]{:S(2)}, u32[]{:S(2)}) async-start(bf16[128,2,768]{2,1,0:T(2,128)(2,1)} %broadcast_in_dim.42), calls=%async_computation.1 | async-start | bytes 786432 | tf_op jit(solution)/shard_map/all_to_all | solution.py:371
  117.4 1.1 pack_corners.3
  118.5 3.8 %collective-permute-start.9 = (bf16[12,264,128]{2,1,0:T(8,128)(2,1)}, bf16[12,264,128]{2,1,0:T(8,128)(2,1)}, u32[]{:S(2)}, u32[]{:S(2)}) collective-permute-start(bf16[12,264,128]{2,1,0:T(8,128)(2,1)} %get-tuple-element.64), channel_id=1, source_target_pairs={{0,16},{16,32},{32,48},{48,64},{64,80},{80,96},{96,112},{1,17},{17... | collective-permute-start | bytes 2433032 | tf_op jit(solution)/shard_map/ppermute | solution.py:255
  122.3 1.9 %collective-permute-start.10 = (bf16[12,264,128]{2,1,0:T(8,128)(2,1)S(1)}, bf16[12,264,128]{2,1,0:T(8,128)(2,1)}, u32[]{:S(2)}, u32[]{:S(2)}) collective-permute-start(bf16[12,264,128]{2,1,0:T(8,128)(2,1)S(1)} %get-tuple-element.65), channel_id=1, source_target_pairs={{16,0},{32,16},{48,32},{64,48},{80,64},{96,80},{112,96},{17,1},{33... | collective-permute-start | bytes 2433032 | tf_op jit(solution)/shard_map/ppermute | solution.py:255
  124.3 2.0 %owner_mix.1.mown = bf16[9,128,128]{2,1,0:T(8,128)(2,1)S(1)} custom-call(s32[54]{0:T(128)S(1)} %copy-done.15, bf16[9,6,128,128]{3,2,1,0:T(8,128)(2,1)S(1)} %copy-done.10, bf16[16,128]{1,0:T(8,128)(2,1)S(1)} %pad.19.owners, bf16[12,264,128]{2,1,0:T(8,128)(2,1)S(1)} %copy-done.6, bf16[12,264,128]{2,1,0:T(8,128)(2,1)S(1)} %copy-done.8, ...), custom_call_target="tpu_custom_call" | custom-call | flops 17179869184 | bytes 6099160 | tf_op jit(solution)/shard_map/owner_mix/pallas_call | solution.py:229
  126.3 0.7 copy-done.13
  127.0 2.7 %all-to-all-done.1 = bf16[128,2,768]{2,1,0:T(2,128)(2,1)} async-done(((bf16[128,2,768]{2,1,0:T(2,128)(2,1)}), bf16[128,2,768]{2,1,0:T(2,128)(2,1)}, u32[]{:S(2)}, u32[]{:S(2)}) %all-to-all-start.1) | async-done | bytes 393248 | tf_op jit(solution)/shard_map/all_to_all | solution.py:371
  129.8 1.8 %copy.14 = bf16[16,8,2,768]{3,1,2,0:T(8,128)(2,1)} copy(bf16[16,8,2,768]{3,2,1,0:T(2,128)(2,1)} %bitcast.9) | data formatting | bytes 786432
  131.6 0.2 collective-permute-done.9.cu
  131.8 4.2 %collective-permute-done.10.cd = bf16[12,264,128]{2,1,0:T(8,128)(2,1)} collective-permute-done((bf16[12,264,128]{2,1,0:T(8,128)(2,1)S(1)}, bf16[12,264,128]{2,1,0:T(8,128)(2,1)}, u32[]{:S(2)}, u32[]{:S(2)}) %collective-permute-start.10) | collective-permute-done | bytes 811040 | tf_op jit(solution)/shard_map/ppermute | solution.py:255
  136.0 11.2 %decode_late.1 = bf16[12,1152,128]{2,1,0:T(8,128)(2,1)} custom-call(bf16[12,1152,128]{2,1,0:T(8,128)(2,1)} %copy-done.1, bf16[12,1152,128]{2,1,0:T(8,128)(2,1)} %decode_early.1.acc, bf16[12,392,128]{2,1,0:T(8,128)(2,1)} %copy-done.2, bf16[12,392,128]{2,1,0:T(8,128)(2,1)} %copy-done.3, bf16[12,264,128]{2,1,0:T(8,128)(2,1)} %collective-permute-done.9.cu, ...), custom_call_target="tpu_custom_call" | custom-call | flops 1358954496 | bytes 19333120 | tf_op jit(solution)/shard_map/decode_late/pallas_call | solution.py:229
  (66 shorter events, 0.3 us)
Async XLA Ops:
  0.0 9.5 %copy-start = (bf16[1152,12,128]{2,0,1:T(8,128)(2,1)S(1)}, bf16[1152,12,128]{2,0,1:T(8,128)(2,1)}, u32[]{:S(2)}) copy-start(bf16[1152,12,128]{2,0,1:T(8,128)(2,1)} %param.11) | copy-start | bytes 10616836
  3.0 30.1 %collective-permute-start.2 = (bf16[12,384,128]{2,1,0:T(8,128)(2,1)}, bf16[12,384,128]{2,1,0:T(8,128)(2,1)}, u32[]{:S(2)}, u32[]{:S(2)}) collective-permute-start(bf16[12,384,128]{2,1,0:T(8,128)(2,1)} %get-tuple-element.37), channel_id=1, source_target_pairs={{0,1},{1,2},{2,3},{3,4},{4,5},{5,6},{6,7},{7,8},{8,9},{9,10},{10,1... | collective-permute-start | bytes 3538952 | tf_op jit(solution)/shard_map/ppermute | solution.py:255
  8.0 8.9 %copy-start.18 = (s32[1152]{0:T(1024)S(1)}, s32[1152]{0:T(1024)}, u32[]{:S(2)}) copy-start(s32[1152]{0:T(1024)} %param.17) | copy-start | bytes 13828
  8.0 8.9 %copy-start.24 = (s32[144,1]{0,1:T(1,128)S(1)}, s32[144,1]{0,1:T(1,128)}, u32[]{:S(2)}) copy-start(s32[144,1]{0,1:T(1,128)} %param.18) | copy-start | bytes 1732
  8.0 10.0 %copy-start.20 = (bf16[128,128]{1,0:T(8,128)(2,1)S(1)}, bf16[128,128]{1,0:T(8,128)(2,1)}, u32[]{:S(2)}) copy-start(bf16[128,128]{1,0:T(8,128)(2,1)} %param.21) | copy-start | bytes 98308
  8.0 10.7 %copy-start.26 = (pred[8]{0:T(512)(128)(4,1)S(1)}, pred[8]{0:T(512)(128)(4,1)}, u32[]{:S(2)}) copy-start(pred[8]{0:T(512)(128)(4,1)} %constant.12.clone.1) | copy-start | bytes 28
  8.0 10.7 %copy-start.21 = (bf16[128,128]{1,0:T(8,128)(2,1)S(1)}, bf16[128,128]{1,0:T(8,128)(2,1)}, u32[]{:S(2)}) copy-start(bf16[128,128]{1,0:T(8,128)(2,1)} %param.15) | copy-start | bytes 98308
  8.0 10.7 %copy-start.22 = (bf16[128,128]{1,0:T(8,128)(2,1)S(1)}, bf16[128,128]{1,0:T(8,128)(2,1)}, u32[]{:S(2)}) copy-start(bf16[128,128]{1,0:T(8,128)(2,1)} %param.19) | copy-start | bytes 98308
  8.1 28.9 %collective-permute-start.3 = (bf16[12,384,128]{2,1,0:T(8,128)(2,1)}, bf16[12,384,128]{2,1,0:T(8,128)(2,1)}, u32[]{:S(2)}, u32[]{:S(2)}) collective-permute-start(bf16[12,384,128]{2,1,0:T(8,128)(2,1)} %get-tuple-element.38), channel_id=1, source_target_pairs={{1,0},{2,1},{3,2},{4,3},{5,4},{6,5},{7,6},{8,7},{9,8},{10,9},{11,1... | collective-permute-start | bytes 3538952 | tf_op jit(solution)/shard_map/ppermute | solution.py:255
  11.0 17.4 %collective-permute-start = (bf16[12,384,128]{2,1,0:T(8,128)(2,1)}, bf16[12,384,128]{2,1,0:T(8,128)(2,1)}, u32[]{:S(2)}, u32[]{:S(2)}) collective-permute-start(bf16[12,384,128]{2,1,0:T(8,128)(2,1)} %get-tuple-element.40), channel_id=1, source_target_pairs={{0,16},{16,32},{32,48},{48,64},{64,80},{80,96},{96,112},{1,17},{17... | collective-permute-start | bytes 3538952 | tf_op jit(solution)/shard_map/ppermute | solution.py:255
  15.0 18.1 %collective-permute-start.1 = (bf16[12,384,128]{2,1,0:T(8,128)(2,1)}, bf16[12,384,128]{2,1,0:T(8,128)(2,1)}, u32[]{:S(2)}, u32[]{:S(2)}) collective-permute-start(bf16[12,384,128]{2,1,0:T(8,128)(2,1)} %get-tuple-element.41), channel_id=1, source_target_pairs={{16,0},{32,16},{48,32},{64,48},{80,64},{96,80},{112,96},{17,1},{33... | collective-permute-start | bytes 3538952 | tf_op jit(solution)/shard_map/ppermute | solution.py:255
  21.6 23.6 %copy-start.14 = (s32[54]{0:T(128)}, s32[54]{0:T(128)S(1)}, u32[]{:S(2)}) copy-start(s32[54]{0:T(128)S(1)} %reshape.38.codes) | copy-start | bytes 652
  21.6 1.5 %copy-start.9 = (bf16[9,6,128,128]{3,2,1,0:T(8,128)(2,1)S(1)}, bf16[9,6,128,128]{3,2,1,0:T(8,128)(2,1)}, u32[]{:S(2)}) copy-start(bf16[9,6,128,128]{3,2,1,0:T(8,128)(2,1)} %adj.7) | copy-start | bytes 5308420
  23.1 2.0 %copy-start.25 = (s32[144,1]{0,1:T(1,128)S(1)}, s32[144,1]{0,1:T(1,128)}, u32[]{:S(2)}) copy-start(s32[144,1]{0,1:T(1,128)} %param.18) | copy-start | bytes 1732
  23.1 2.0 %copy-start.19 = (s32[1152]{0:T(1024)S(1)}, s32[1152]{0:T(1024)}, u32[]{:S(2)}) copy-start(s32[1152]{0:T(1024)} %param.17) | copy-start | bytes 13828
  23.1 2.0 %copy-start.23 = (bf16[1152]{0:T(1024)(128)(2,1)S(1)}, bf16[1152]{0:T(1024)(128)(2,1)}, u32[]{:S(2)}) copy-start(bf16[1152]{0:T(1024)(128)(2,1)} %param.16) | copy-start | bytes 6916
  25.1 31.8 %copy-start.4 = (bf16[12,128,384]{2,1,0:T(8,128)(2,1)}, bf16[12,128,384]{2,1,0:T(8,128)(2,1)S(1)}, u32[]{:S(2)}) copy-start(bf16[12,128,384]{2,1,0:T(8,128)(2,1)S(1)} %late_weights.1.late) | copy-start | bytes 3538948
  33.1 12.2 %copy-start.11 = (bf16[256,256]{1,0:T(8,128)(2,1)S(1)}, bf16[256,256]{1,0:T(8,128)(2,1)}, u32[]{:S(2)}) copy-start(bf16[256,256]{1,0:T(8,128)(2,1)} %get-tuple-element.44.w_mix) | copy-start | bytes 393220
  33.1 12.2 %copy-start.16 = (f32[128]{0:T(128)S(1)}, f32[128]{0:T(128)}, u32[]{:S(2)}) copy-start(f32[128]{0:T(128)} %param.14) | copy-start | bytes 1540
  38.5 14.6 %collective-permute-start.4 = (bf16[12,264,128]{2,1,0:T(8,128)(2,1)S(1)}, bf16[12,264,128]{2,1,0:T(8,128)(2,1)S(1)}, u32[]{:S(2)}, u32[]{:S(2)}) collective-permute-start(bf16[12,264,128]{2,1,0:T(8,128)(2,1)S(1)} %get-tuple-element.48), channel_id=1, source_target_pairs={{0,16},{16,32},{32,48},{48,64},{64,80},{80,96},{96,112},{1,17},{17... | collective-permute-start | bytes 2433032 | tf_op jit(solution)/shard_map/ppermute | solution.py:255
  43.3 13.6 %collective-permute-start.5 = (bf16[12,264,128]{2,1,0:T(8,128)(2,1)S(1)}, bf16[12,264,128]{2,1,0:T(8,128)(2,1)S(1)}, u32[]{:S(2)}, u32[]{:S(2)}) collective-permute-start(bf16[12,264,128]{2,1,0:T(8,128)(2,1)S(1)} %get-tuple-element.49), channel_id=1, source_target_pairs={{16,0},{32,16},{48,32},{64,48},{80,64},{96,80},{112,96},{17,1},{33... | collective-permute-start | bytes 2433032 | tf_op jit(solution)/shard_map/ppermute | solution.py:255
  45.3 11.6 %copy-start.12 = (bf16[256,256]{1,0:T(8,128)(2,1)S(1)}, bf16[256,256]{1,0:T(8,128)(2,1)}, u32[]{:S(2)}) copy-start(bf16[256,256]{1,0:T(8,128)(2,1)} %get-tuple-element.51.w_coarse) | copy-start | bytes 393220
  53.0 13.4 %copy-start.5 = (bf16[12,264,128]{2,1,0:T(8,128)(2,1)}, bf16[12,264,128]{2,1,0:T(8,128)(2,1)S(1)}, u32[]{:S(2)}) copy-start(bf16[12,264,128]{2,1,0:T(8,128)(2,1)S(1)} %collective-permute-done.4.cu.cut) | copy-start | bytes 2433028
  56.9 9.5 %copy-start.7 = (bf16[12,264,128]{2,1,0:T(8,128)(2,1)}, bf16[12,264,128]{2,1,0:T(8,128)(2,1)S(1)}, u32[]{:S(2)}) copy-start(bf16[12,264,128]{2,1,0:T(8,128)(2,1)S(1)} %collective-permute-done.5.cd.cdt) | copy-start | bytes 2433028
  66.4 4.8 %copy-start.1 = (bf16[12,1152,128]{2,1,0:T(8,128)(2,1)}, bf16[12,1152,128]{2,1,0:T(8,128)(2,1)S(1)}, u32[]{:S(2)}) copy-start(bf16[12,1152,128]{2,1,0:T(8,128)(2,1)S(1)} %get-tuple-element.56.own.x) | copy-start | bytes 10616836
  66.4 50.9 %collective-permute-start.6 = (bf16[12,392,128]{2,1,0:T(8,128)(2,1)}, bf16[12,392,128]{2,1,0:T(8,128)(2,1)S(1)}, u32[]{:S(2)}, u32[]{:S(2)}) collective-permute-start(bf16[12,392,128]{2,1,0:T(8,128)(2,1)} %get-tuple-element.57), channel_id=1, source_target_pairs={{0,1},{1,2},{2,3},{3,4},{4,5},{5,6},{6,7},{7,8},{8,9},{9,10},{10,1... | collective-permute-start | bytes 3612680 | tf_op jit(solution)/shard_map/ppermute | solution.py:255
  68.7 48.6 %collective-permute-start.7 = (bf16[12,392,128]{2,1,0:T(8,128)(2,1)}, bf16[12,392,128]{2,1,0:T(8,128)(2,1)S(1)}, u32[]{:S(2)}, u32[]{:S(2)}) collective-permute-start(bf16[12,392,128]{2,1,0:T(8,128)(2,1)} %get-tuple-element.58), channel_id=1, source_target_pairs={{1,0},{2,1},{3,2},{4,3},{5,4},{6,5},{7,6},{8,7},{9,8},{10,9},{11,1... | collective-permute-start | bytes 3612680 | tf_op jit(solution)/shard_map/ppermute | solution.py:255
  71.2 1.0 copy-start.17
  72.2 31.1 %collective-permute-start.8 = (bf16[12,384,128]{2,1,0:T(8,128)(2,1)}, bf16[12,384,128]{2,1,0:T(8,128)(2,1)}, u32[]{:S(2)}, u32[]{:S(2)}) collective-permute-start(bf16[12,384,128]{2,1,0:T(8,128)(2,1)} %get-tuple-element.60), channel_id=1, source_target_pairs={{0,16},{16,32},{32,48},{48,64},{64,80},{80,96},{96,112},{1,17},{17... | collective-permute-start | bytes 3538952 | tf_op jit(solution)/shard_map/ppermute | solution.py:255
  75.1 27.8 %all-to-all-start = ((bf16[128,2,768]{2,1,0:T(2,128)(2,1)}), bf16[128,2,768]{2,1,0:T(2,128)(2,1)S(1)}, u32[]{:S(2)}, u32[]{:S(2)}) async-start(bf16[128,2,768]{2,1,0:T(2,128)(2,1)} %reshape.41), calls=%async_computation | async-start | bytes 786432 | tf_op jit(solution)/shard_map/all_to_all | solution.py:367
  87.4 44.1 %collective-permute-start.11 = (bf16[12,384,128]{2,1,0:T(8,128)(2,1)}, bf16[12,384,128]{2,1,0:T(8,128)(2,1)}, u32[]{:S(2)}, u32[]{:S(2)}) collective-permute-start(bf16[12,384,128]{2,1,0:T(8,128)(2,1)} %copy-done.17), channel_id=1, source_target_pairs={{16,0},{32,16},{48,32},{64,48},{80,64},{96,80},{112,96},{17,1},{33... | collective-permute-start | bytes 3538952 | tf_op jit(solution)/shard_map/ppermute | solution.py:255
  104.3 25.5 %all-to-all-start.1 = ((bf16[128,2,768]{2,1,0:T(2,128)(2,1)}), bf16[128,2,768]{2,1,0:T(2,128)(2,1)}, u32[]{:S(2)}, u32[]{:S(2)}) async-start(bf16[128,2,768]{2,1,0:T(2,128)(2,1)} %broadcast_in_dim.42), calls=%async_computation.1 | async-start | bytes 786432 | tf_op jit(solution)/shard_map/all_to_all | solution.py:371
  117.3 6.9 %copy-start.6 = (bf16[12,264,128]{2,1,0:T(8,128)(2,1)S(1)}, bf16[12,264,128]{2,1,0:T(8,128)(2,1)}, u32[]{:S(2)}) copy-start(bf16[12,264,128]{2,1,0:T(8,128)(2,1)} %copy-done.5) | copy-start | bytes 2433028
  117.3 6.9 %copy-start.8 = (bf16[12,264,128]{2,1,0:T(8,128)(2,1)S(1)}, bf16[12,264,128]{2,1,0:T(8,128)(2,1)}, u32[]{:S(2)}) copy-start(bf16[12,264,128]{2,1,0:T(8,128)(2,1)} %copy-done.7) | copy-start | bytes 2433028
  117.3 6.9 %copy-start.10 = (bf16[9,6,128,128]{3,2,1,0:T(8,128)(2,1)S(1)}, bf16[9,6,128,128]{3,2,1,0:T(8,128)(2,1)}, u32[]{:S(2)}) copy-start(bf16[9,6,128,128]{3,2,1,0:T(8,128)(2,1)} %adj.7) | copy-start | bytes 5308420
  117.3 6.9 %copy-start.15 = (s32[54]{0:T(128)S(1)}, s32[54]{0:T(128)}, u32[]{:S(2)}) copy-start(s32[54]{0:T(128)} %copy-done.14) | copy-start | bytes 652
  117.4 6.9 %copy-start.2 = (bf16[12,392,128]{2,1,0:T(8,128)(2,1)}, bf16[12,392,128]{2,1,0:T(8,128)(2,1)S(1)}, u32[]{:S(2)}) copy-start(bf16[12,392,128]{2,1,0:T(8,128)(2,1)S(1)} %collective-permute-done.6.lt.lb.ylt.yl) | copy-start | bytes 3612676
  117.4 6.8 %copy-start.3 = (bf16[12,392,128]{2,1,0:T(8,128)(2,1)}, bf16[12,392,128]{2,1,0:T(8,128)(2,1)S(1)}, u32[]{:S(2)}) copy-start(bf16[12,392,128]{2,1,0:T(8,128)(2,1)S(1)} %collective-permute-done.7.rt.rb.yrt.yr) | copy-start | bytes 3612676
  118.5 13.3 %collective-permute-start.9 = (bf16[12,264,128]{2,1,0:T(8,128)(2,1)}, bf16[12,264,128]{2,1,0:T(8,128)(2,1)}, u32[]{:S(2)}, u32[]{:S(2)}) collective-permute-start(bf16[12,264,128]{2,1,0:T(8,128)(2,1)} %get-tuple-element.64), channel_id=1, source_target_pairs={{0,16},{16,32},{32,48},{48,64},{64,80},{80,96},{96,112},{1,17},{17... | collective-permute-start | bytes 2433032 | tf_op jit(solution)/shard_map/ppermute | solution.py:255
  122.3 13.7 %collective-permute-start.10 = (bf16[12,264,128]{2,1,0:T(8,128)(2,1)S(1)}, bf16[12,264,128]{2,1,0:T(8,128)(2,1)}, u32[]{:S(2)}, u32[]{:S(2)}) collective-permute-start(bf16[12,264,128]{2,1,0:T(8,128)(2,1)S(1)} %get-tuple-element.65), channel_id=1, source_target_pairs={{16,0},{32,16},{48,32},{64,48},{80,64},{96,80},{112,96},{17,1},{33... | collective-permute-start | bytes 2433032 | tf_op jit(solution)/shard_map/ppermute | solution.py:255
  126.3 0.7 copy-start.13

commit v4 on v3

--- a/solution.py
+++ b/solution.py
@@ -269,10 +269,10 @@
 
 
 def sides(x):
-    block = lambda k: pl.BlockSpec((PAIR, BLK, C), lambda p, *_: (p, k, 0))
-    return call(sides_kernel, "pack_sides", x.shape[0], [x] * (2 * GB),
+    block = lambda k: pl.BlockSpec((2, BLK, C), lambda p, *_: (p, k, 0))
+    return call(sides_kernel, "pack_sides", x.shape[0] // 2 * PAIR, [x] * (2 * GB),
                 [block(a * GB + b) for b in (GB - 1, 0) for a in range(GB)],
-                [sds((x.shape[0], SIDE, C))] * 2, [by_step(SIDE)] * 2, [], 1, vmem=60)
+                [sds((x.shape[0], SIDE, C))] * 2, [pl.BlockSpec((2, SIDE, C), lambda p, *_: (p, 0, 0))] * 2, [], 1, vmem=60)
 
 
 def rows_kernel(x, top, bottom):

time: 148 us -> 150 us (1.014)
  Pallas kernels: 49 us -> 51.2 us
    pallas_call x12, Pallas kernels: 49 us -> 51.2 us  [call(): pl.pallas_call(kernel, grid_spec=pltpu.PrefetchScalarGridSpec(num_scalar_...]
where the time goes in v4:
time: 150 us; the launch traced here: 149 us
  starting transfers between devices  59 us (39%)
  Pallas kernels  51.2 us (34%)
  waiting for transfers between devices  26.5 us (18%)
  local copies, waits for them, and re-layouts  9.05 us (6%)
  other arithmetic  3.24 us (2%)
    pallas_call x12, Pallas kernels, call(): pl.pallas_call(kernel, grid_spec=pltpu.PrefetchScalarGridSpec(num_scalar_...  51.2 us
    ppermute x12, starting transfers between devices, shift(): lax.ppermute(block, axis, pairs if up else [(b, a) for a, b in pairs])  33.6 us
    ppermute x12, waiting for transfers between devices, shift(): lax.ppermute(block, axis, pairs if up else [(b, a) for a, b in pairs])  19.7 us
    all_to_all x1, starting transfers between devices, on_device(): lax.all_to_all(everyone, ('rx', 'ry'), split_axis=0, concat_axis=0, tiled...  13.1 us
    all_to_all x1, starting transfers between devices, on_device(): lax.all_to_all(part, ('rx', 'ry'), split_axis=0, concat_axis=0, tiled=True)  12.3 us
    unnamed x56, local copies, waits for them, and re-layouts  6.44 us
    all_to_all x1, waiting for transfers between devices, on_device(): lax.all_to_all(part, ('rx', 'ry'), split_axis=0, concat_axis=0, tiled=True)  4.03 us
  transfers between devices with their start and end apart: 14, of which 8 were waited for; matrix products, arithmetic and copies ran while one was open for 6% of the time, Pallas kernels for 16%

profile of v4, /device:TPU:1, one launch (start us, length us, event | category | flops | bytes accessed | tf_op | source)
XLA Modules:
  0.0 149.5 jit_solution(9840233146844839340)
XLA Ops:
  0.0 5.3 %pack_sides.1 = (bf16[12,384,128]{2,1,0:T(8,128)(2,1)}, bf16[12,384,128]{2,1,0:T(8,128)(2,1)}) custom-call(bf16[12,1152,128]{2,1,0:T(8,128)(2,1)} %bitcast.20, bf16[12,1152,128]{2,1,0:T(8,128)(2,1)} %bitcast.21, bf16[12,1152,128]{2,1,0:T(8,128)(2,1)} %bitcast.22, bf16[12,1152,128]{2,1,0:T(8,128)(2,1)} %bitcast.23, bf16[12,1152,128]{2,1,0:T(8,128)(2,1)} %bitcast.24, ...), custom_call_target="tpu_custom_call" | custom-call | flops 1 | bytes 23592960 | tf_op jit(solution)/shard_map/pack_sides/pallas_call | solution.py:229
  5.3 5.1 %collective-permute-start.2 = (bf16[12,384,128]{2,1,0:T(8,128)(2,1)}, bf16[12,384,128]{2,1,0:T(8,128)(2,1)}, u32[]{:S(2)}, u32[]{:S(2)}) collective-permute-start(bf16[12,384,128]{2,1,0:T(8,128)(2,1)} %get-tuple-element.37), channel_id=1, source_target_pairs={{0,1},{1,2},{2,3},{3,4},{4,5},{5,6},{6,7},{7,8},{8,9},{9,10},{10,1... | collective-permute-start | bytes 3538952 | tf_op jit(solution)/shard_map/ppermute | solution.py:255
  10.3 1.4 collective-permute-start.3
  11.8 1.5 %pack_rows.2 = (bf16[12,384,128]{2,1,0:T(8,128)(2,1)}, bf16[12,384,128]{2,1,0:T(8,128)(2,1)}) custom-call(bf16[12,1152,128]{2,1,0:T(8,128)(2,1)S(1)} %bitcast.26), custom_call_target="tpu_custom_call" | custom-call | flops 17179869184 | bytes 5898240 | tf_op jit(solution)/shard_map/pack_rows/pallas_call | solution.py:229
  13.3 3.9 %collective-permute-start = (bf16[12,384,128]{2,1,0:T(8,128)(2,1)}, bf16[12,384,128]{2,1,0:T(8,128)(2,1)}, u32[]{:S(2)}, u32[]{:S(2)}) collective-permute-start(bf16[12,384,128]{2,1,0:T(8,128)(2,1)} %get-tuple-element.40), channel_id=1, source_target_pairs={{0,16},{16,32},{32,48},{48,64},{64,80},{80,96},{96,112},{1,17},{17... | collective-permute-start | bytes 3538952 | tf_op jit(solution)/shard_map/ppermute | solution.py:255
  17.2 1.9 %collective-permute-start.1 = (bf16[12,384,128]{2,1,0:T(8,128)(2,1)}, bf16[12,384,128]{2,1,0:T(8,128)(2,1)}, u32[]{:S(2)}, u32[]{:S(2)}) collective-permute-start(bf16[12,384,128]{2,1,0:T(8,128)(2,1)} %get-tuple-element.41), channel_id=1, source_target_pairs={{16,0},{32,16},{48,32},{64,48},{80,64},{96,80},{112,96},{17,1},{33... | collective-permute-start | bytes 3538952 | tf_op jit(solution)/shard_map/ppermute | solution.py:255
  19.2 0.2 select_reduce_fusion
  19.4 0.9 fusion.2.hot
  20.3 0.7 fusion.11.w_out
  21.0 0.1 fusion.14
  21.1 0.7 fusion.9
  21.8 1.4 copy.13
  23.1 0.8 reshape.38.codes
  23.9 1.5 copy-done.9
  25.4 2.0 %late_weights.1.late = bf16[12,128,384]{2,1,0:T(8,128)(2,1)S(1)} custom-call(s32[54]{0:T(128)S(1)} %reshape.38.codes, bf16[9,6,128,128]{3,2,1,0:T(8,128)(2,1)S(1)} %copy-done.9), custom_call_target="tpu_custom_call" | custom-call | flops 1048576 | bytes 2949336 | tf_op jit(solution)/shard_map/late_weights/pallas_call | solution.py:229
  27.5 0.2 fusion.unpool
  27.7 2.9 %collective-permute-done.xu = bf16[12,384,128]{2,1,0:T(8,128)(2,1)} collective-permute-done((bf16[12,384,128]{2,1,0:T(8,128)(2,1)}, bf16[12,384,128]{2,1,0:T(8,128)(2,1)}, u32[]{:S(2)}, u32[]{:S(2)}) %collective-permute-start) | collective-permute-done | bytes 1179680 | tf_op jit(solution)/shard_map/ppermute | solution.py:255
  30.7 4.7 %collective-permute-done.1.xd = bf16[12,384,128]{2,1,0:T(8,128)(2,1)} collective-permute-done((bf16[12,384,128]{2,1,0:T(8,128)(2,1)}, bf16[12,384,128]{2,1,0:T(8,128)(2,1)}, u32[]{:S(2)}, u32[]{:S(2)}) %collective-permute-start.1) | collective-permute-done | bytes 1179680 | tf_op jit(solution)/shard_map/ppermute | solution.py:255
  35.4 3.8 %collective-permute-done.3.rt.rb.yr = bf16[12,384,128]{2,1,0:T(8,128)(2,1)} collective-permute-done((bf16[12,384,128]{2,1,0:T(8,128)(2,1)}, bf16[12,384,128]{2,1,0:T(8,128)(2,1)}, u32[]{:S(2)}, u32[]{:S(2)}) %collective-permute-start.3) | collective-permute-done | bytes 1179680 | tf_op jit(solution)/shard_map/ppermute | solution.py:255
  39.2 1.5 %pack_corners.2 = (bf16[12,264,128]{2,1,0:T(8,128)(2,1)S(1)}, bf16[12,264,128]{2,1,0:T(8,128)(2,1)S(1)}) custom-call(bf16[12,384,128]{2,1,0:T(8,128)(2,1)} %collective-permute-done.2.lt.lb.yl, bf16[12,384,128]{2,1,0:T(8,128)(2,1)} %collective-permute-done.2.lt.lb.yl, bf16[12,384,128]{2,1,0:T(8,128)(2,1)} %collective-permute-done.3.rt.rb.yr, ...), custom_call_target="tpu_custom_call" | custom-call | flops 1 | bytes 6344704 | tf_op jit(solution)/shard_map/pack_corners/pallas_call | solution.py:229
  40.7 4.9 %collective-permute-start.4 = (bf16[12,264,128]{2,1,0:T(8,128)(2,1)S(1)}, bf16[12,264,128]{2,1,0:T(8,128)(2,1)S(1)}, u32[]{:S(2)}, u32[]{:S(2)}) collective-permute-start(bf16[12,264,128]{2,1,0:T(8,128)(2,1)S(1)} %get-tuple-element.48), channel_id=1, source_target_pairs={{0,16},{16,32},{32,48},{48,64},{64,80},{80,96},{96,112},{1,17},{17... | collective-permute-start | bytes 2433032 | tf_op jit(solution)/shard_map/ppermute | solution.py:255
  45.6 1.9 %collective-permute-start.5 = (bf16[12,264,128]{2,1,0:T(8,128)(2,1)S(1)}, bf16[12,264,128]{2,1,0:T(8,128)(2,1)S(1)}, u32[]{:S(2)}, u32[]{:S(2)}) collective-permute-start(bf16[12,264,128]{2,1,0:T(8,128)(2,1)S(1)} %get-tuple-element.49), channel_id=1, source_target_pairs={{16,0},{32,16},{48,32},{64,48},{80,64},{96,80},{112,96},{17,1},{33... | collective-permute-start | bytes 2433032 | tf_op jit(solution)/shard_map/ppermute | solution.py:255
  47.6 7.7 %encode_early.1 = (bf16[12,768,128]{2,1,0:T(8,128)(2,1)S(1)}, bf16[12,384,128]{2,1,0:T(8,128)(2,1)S(1)}) custom-call(s32[54]{0:T(128)S(1)} %reshape.38.codes, bf16[12,1152,128]{2,1,0:T(8,128)(2,1)S(1)} %bitcast.27, bf16[12,384,128]{2,1,0:T(8,128)(2,1)} %collective-permute-done.xu, bf16[12,384,128]{2,1,0:T(8,128)(2,1)} %collective-permute-done.1.xd, ...), custom_call_target="tpu_custom_call" | custom-call | flops 2866544640 | bytes 11338456 | tf_op jit(solution)/shard_map/encode_early/pallas_call | solution.py:229
  55.3 3.9 %collective-permute-done.5.cd.cdt = bf16[12,264,128]{2,1,0:T(8,128)(2,1)S(1)} collective-permute-done((bf16[12,264,128]{2,1,0:T(8,128)(2,1)S(1)}, bf16[12,264,128]{2,1,0:T(8,128)(2,1)S(1)}, u32[]{:S(2)}, u32[]{:S(2)}) %collective-permute-start.5) | collective-permute-done | bytes 811040 | tf_op jit(solution)/shard_map/ppermute | solution.py:255
  59.2 9.5 %encode_late.1 = (bf16[12,1152,128]{2,1,0:T(8,128)(2,1)S(1)}, bf16[12,392,128]{2,1,0:T(8,128)(2,1)}, bf16[12,392,128]{2,1,0:T(8,128)(2,1)}, bf16[128,1536]{1,0:T(8,128)(2,1)S(1)}) custom-call(bf16[12,1152,128]{2,1,0:T(8,128)(2,1)S(1)} %bitcast.28, bf16[12,768,128]{2,1,0:T(8,128)(2,1)S(1)} %get-tuple-element.45.acc, ...), custom_call_target="tpu_custom_call" | custom-call | flops 1981808640 | bytes 21168640 | tf_op jit(solution)/shard_map/encode_late/pallas_call | solution.py:229
  68.7 2.3 %collective-permute-start.6 = (bf16[12,392,128]{2,1,0:T(8,128)(2,1)}, bf16[12,392,128]{2,1,0:T(8,128)(2,1)S(1)}, u32[]{:S(2)}, u32[]{:S(2)}) collective-permute-start(bf16[12,392,128]{2,1,0:T(8,128)(2,1)} %get-tuple-element.57), channel_id=1, source_target_pairs={{0,1},{1,2},{2,3},{3,4},{4,5},{5,6},{6,7},{7,8},{8,9},{9,10},{10,1... | collective-permute-start | bytes 3612680 | tf_op jit(solution)/shard_map/ppermute | solution.py:255
  71.0 1.3 collective-permute-start.7
  72.3 1.1 pack_rows.3
  73.5 1.0 copy-done.17
  74.5 2.0 %collective-permute-start.8 = (bf16[12,384,128]{2,1,0:T(8,128)(2,1)}, bf16[12,384,128]{2,1,0:T(8,128)(2,1)}, u32[]{:S(2)}, u32[]{:S(2)}) collective-permute-start(bf16[12,384,128]{2,1,0:T(8,128)(2,1)} %get-tuple-element.60), channel_id=1, source_target_pairs={{0,16},{16,32},{32,48},{48,64},{64,80},{80,96},{96,112},{1,17},{17... | collective-permute-start | bytes 3538952 | tf_op jit(solution)/shard_map/ppermute | solution.py:255
  76.5 0.9 reshape.41
  77.4 12.3 %all-to-all-start = ((bf16[128,2,768]{2,1,0:T(2,128)(2,1)}), bf16[128,2,768]{2,1,0:T(2,128)(2,1)S(1)}, u32[]{:S(2)}, u32[]{:S(2)}) async-start(bf16[128,2,768]{2,1,0:T(2,128)(2,1)} %reshape.41), calls=%async_computation | async-start | bytes 786432 | tf_op jit(solution)/shard_map/all_to_all | solution.py:367
  89.7 3.2 %collective-permute-start.11 = (bf16[12,384,128]{2,1,0:T(8,128)(2,1)}, bf16[12,384,128]{2,1,0:T(8,128)(2,1)}, u32[]{:S(2)}, u32[]{:S(2)}) collective-permute-start(bf16[12,384,128]{2,1,0:T(8,128)(2,1)} %copy-done.17), channel_id=1, source_target_pairs={{16,0},{32,16},{48,32},{64,48},{80,64},{96,80},{112,96},{17,1},{33... | collective-permute-start | bytes 3538952 | tf_op jit(solution)/shard_map/ppermute | solution.py:255
  92.9 8.3 %decode_early.1.acc = bf16[12,1152,128]{2,1,0:T(8,128)(2,1)} custom-call(s32[54]{0:T(128)} %copy-done.14, bf16[12,1152,128]{2,1,0:T(8,128)(2,1)} %copy-done.1, bf16[9,6,128,128]{3,2,1,0:T(8,128)(2,1)} %adj.7), custom_call_target="tpu_custom_call" | custom-call | flops 2717908992 | bytes 8847576 | tf_op jit(solution)/shard_map/decode_early/pallas_call | solution.py:229
  101.2 4.0 %all-to-all-done = bf16[128,2,768]{2,1,0:T(2,128)(2,1)S(1)} async-done(((bf16[128,2,768]{2,1,0:T(2,128)(2,1)}), bf16[128,2,768]{2,1,0:T(2,128)(2,1)S(1)}, u32[]{:S(2)}, u32[]{:S(2)}) %all-to-all-start) | async-done | bytes 393248 | tf_op jit(solution)/shard_map/all_to_all | solution.py:367
  105.2 0.4 convert_reduce_fusion
  105.6 1.0 broadcast_in_dim.42
  106.5 13.1 %all-to-all-start.1 = ((bf16[128,2,768]{2,1,0:T(2,128)(2,1)}), bf16[128,2,768]{2,1,0:T(2,128)(2,1)}, u32[]{:S(2)}, u32[]{:S(2)}) async-start(bf16[128,2,768]{2,1,0:T(2,128)(2,1)} %broadcast_in_dim.42), calls=%async_computation.1 | async-start | bytes 786432 | tf_op jit(solution)/shard_map/all_to_all | solution.py:371
  119.7 1.1 pack_corners.3
  120.8 3.8 %collective-permute-start.9 = (bf16[12,264,128]{2,1,0:T(8,128)(2,1)}, bf16[12,264,128]{2,1,0:T(8,128)(2,1)}, u32[]{:S(2)}, u32[]{:S(2)}) collective-permute-start(bf16[12,264,128]{2,1,0:T(8,128)(2,1)} %get-tuple-element.64), channel_id=1, source_target_pairs={{0,16},{16,32},{32,48},{48,64},{64,80},{80,96},{96,112},{1,17},{17... | collective-permute-start | bytes 2433032 | tf_op jit(solution)/shard_map/ppermute | solution.py:255
  124.6 1.9 %collective-permute-start.10 = (bf16[12,264,128]{2,1,0:T(8,128)(2,1)S(1)}, bf16[12,264,128]{2,1,0:T(8,128)(2,1)}, u32[]{:S(2)}, u32[]{:S(2)}) collective-permute-start(bf16[12,264,128]{2,1,0:T(8,128)(2,1)S(1)} %get-tuple-element.65), channel_id=1, source_target_pairs={{16,0},{32,16},{48,32},{64,48},{80,64},{96,80},{112,96},{17,1},{33... | collective-permute-start | bytes 2433032 | tf_op jit(solution)/shard_map/ppermute | solution.py:255
  126.6 2.0 %owner_mix.1.mown = bf16[9,128,128]{2,1,0:T(8,128)(2,1)S(1)} custom-call(s32[54]{0:T(128)S(1)} %copy-done.15, bf16[9,6,128,128]{3,2,1,0:T(8,128)(2,1)S(1)} %copy-done.10, bf16[16,128]{1,0:T(8,128)(2,1)S(1)} %pad.19.owners, bf16[12,264,128]{2,1,0:T(8,128)(2,1)S(1)} %copy-done.6, bf16[12,264,128]{2,1,0:T(8,128)(2,1)S(1)} %copy-done.8, ...), custom_call_target="tpu_custom_call" | custom-call | flops 17179869184 | bytes 6099160 | tf_op jit(solution)/shard_map/owner_mix/pallas_call | solution.py:229
  128.6 0.7 copy-done.13
  129.3 2.7 %all-to-all-done.1 = bf16[128,2,768]{2,1,0:T(2,128)(2,1)} async-done(((bf16[128,2,768]{2,1,0:T(2,128)(2,1)}), bf16[128,2,768]{2,1,0:T(2,128)(2,1)}, u32[]{:S(2)}, u32[]{:S(2)}) %all-to-all-start.1) | async-done | bytes 393248 | tf_op jit(solution)/shard_map/all_to_all | solution.py:371
  132.1 1.8 %copy.14 = bf16[16,8,2,768]{3,1,2,0:T(8,128)(2,1)} copy(bf16[16,8,2,768]{3,2,1,0:T(2,128)(2,1)} %bitcast.9) | data formatting | bytes 786432
  133.9 0.2 collective-permute-done.9.cu
  134.1 4.2 %collective-permute-done.10.cd = bf16[12,264,128]{2,1,0:T(8,128)(2,1)} collective-permute-done((bf16[12,264,128]{2,1,0:T(8,128)(2,1)S(1)}, bf16[12,264,128]{2,1,0:T(8,128)(2,1)}, u32[]{:S(2)}, u32[]{:S(2)}) %collective-permute-start.10) | collective-permute-done | bytes 811040 | tf_op jit(solution)/shard_map/ppermute | solution.py:255
  138.3 11.2 %decode_late.1 = bf16[12,1152,128]{2,1,0:T(8,128)(2,1)} custom-call(bf16[12,1152,128]{2,1,0:T(8,128)(2,1)} %copy-done.1, bf16[12,1152,128]{2,1,0:T(8,128)(2,1)} %decode_early.1.acc, bf16[12,392,128]{2,1,0:T(8,128)(2,1)} %copy-done.2, bf16[12,392,128]{2,1,0:T(8,128)(2,1)} %copy-done.3, bf16[12,264,128]{2,1,0:T(8,128)(2,1)} %collective-permute-done.9.cu, ...), custom_call_target="tpu_custom_call" | custom-call | flops 1358954496 | bytes 19333120 | tf_op jit(solution)/shard_map/decode_late/pallas_call | solution.py:229
  (66 shorter events, 0.3 us)
Async XLA Ops:
  0.0 11.8 %copy-start = (bf16[1152,12,128]{2,0,1:T(8,128)(2,1)S(1)}, bf16[1152,12,128]{2,0,1:T(8,128)(2,1)}, u32[]{:S(2)}) copy-start(bf16[1152,12,128]{2,0,1:T(8,128)(2,1)} %param.11) | copy-start | bytes 10616836
  5.3 30.1 %collective-permute-start.2 = (bf16[12,384,128]{2,1,0:T(8,128)(2,1)}, bf16[12,384,128]{2,1,0:T(8,128)(2,1)}, u32[]{:S(2)}, u32[]{:S(2)}) collective-permute-start(bf16[12,384,128]{2,1,0:T(8,128)(2,1)} %get-tuple-element.37), channel_id=1, source_target_pairs={{0,1},{1,2},{2,3},{3,4},{4,5},{5,6},{6,7},{7,8},{8,9},{9,10},{10,1... | collective-permute-start | bytes 3538952 | tf_op jit(solution)/shard_map/ppermute | solution.py:255
  10.3 8.9 %copy-start.18 = (s32[1152]{0:T(1024)S(1)}, s32[1152]{0:T(1024)}, u32[]{:S(2)}) copy-start(s32[1152]{0:T(1024)} %param.17) | copy-start | bytes 13828
  10.3 8.9 %copy-start.24 = (s32[144,1]{0,1:T(1,128)S(1)}, s32[144,1]{0,1:T(1,128)}, u32[]{:S(2)}) copy-start(s32[144,1]{0,1:T(1,128)} %param.18) | copy-start | bytes 1732
  10.3 10.0 %copy-start.20 = (bf16[128,128]{1,0:T(8,128)(2,1)S(1)}, bf16[128,128]{1,0:T(8,128)(2,1)}, u32[]{:S(2)}) copy-start(bf16[128,128]{1,0:T(8,128)(2,1)} %param.21) | copy-start | bytes 98308
  10.3 10.7 %copy-start.26 = (pred[8]{0:T(512)(128)(4,1)S(1)}, pred[8]{0:T(512)(128)(4,1)}, u32[]{:S(2)}) copy-start(pred[8]{0:T(512)(128)(4,1)} %constant.12.clone.1) | copy-start | bytes 28
  10.3 10.7 %copy-start.21 = (bf16[128,128]{1,0:T(8,128)(2,1)S(1)}, bf16[128,128]{1,0:T(8,128)(2,1)}, u32[]{:S(2)}) copy-start(bf16[128,128]{1,0:T(8,128)(2,1)} %param.15) | copy-start | bytes 98308
  10.3 10.7 %copy-start.22 = (bf16[128,128]{1,0:T(8,128)(2,1)S(1)}, bf16[128,128]{1,0:T(8,128)(2,1)}, u32[]{:S(2)}) copy-start(bf16[128,128]{1,0:T(8,128)(2,1)} %param.19) | copy-start | bytes 98308
  10.3 28.9 %collective-permute-start.3 = (bf16[12,384,128]{2,1,0:T(8,128)(2,1)}, bf16[12,384,128]{2,1,0:T(8,128)(2,1)}, u32[]{:S(2)}, u32[]{:S(2)}) collective-permute-start(bf16[12,384,128]{2,1,0:T(8,128)(2,1)} %get-tuple-element.38), channel_id=1, source_target_pairs={{1,0},{2,1},{3,2},{4,3},{5,4},{6,5},{7,6},{8,7},{9,8},{10,9},{11,1... | collective-permute-start | bytes 3538952 | tf_op jit(solution)/shard_map/ppermute | solution.py:255
  13.3 17.4 %collective-permute-start = (bf16[12,384,128]{2,1,0:T(8,128)(2,1)}, bf16[12,384,128]{2,1,0:T(8,128)(2,1)}, u32[]{:S(2)}, u32[]{:S(2)}) collective-permute-start(bf16[12,384,128]{2,1,0:T(8,128)(2,1)} %get-tuple-element.40), channel_id=1, source_target_pairs={{0,16},{16,32},{32,48},{48,64},{64,80},{80,96},{96,112},{1,17},{17... | collective-permute-start | bytes 3538952 | tf_op jit(solution)/shard_map/ppermute | solution.py:255
  17.2 18.1 %collective-permute-start.1 = (bf16[12,384,128]{2,1,0:T(8,128)(2,1)}, bf16[12,384,128]{2,1,0:T(8,128)(2,1)}, u32[]{:S(2)}, u32[]{:S(2)}) collective-permute-start(bf16[12,384,128]{2,1,0:T(8,128)(2,1)} %get-tuple-element.41), channel_id=1, source_target_pairs={{16,0},{32,16},{48,32},{64,48},{80,64},{96,80},{112,96},{17,1},{33... | collective-permute-start | bytes 3538952 | tf_op jit(solution)/shard_map/ppermute | solution.py:255
  23.9 23.6 %copy-start.14 = (s32[54]{0:T(128)}, s32[54]{0:T(128)S(1)}, u32[]{:S(2)}) copy-start(s32[54]{0:T(128)S(1)} %reshape.38.codes) | copy-start | bytes 652
  23.9 1.5 copy-start.9
  25.4 2.0 %copy-start.25 = (s32[144,1]{0,1:T(1,128)S(1)}, s32[144,1]{0,1:T(1,128)}, u32[]{:S(2)}) copy-start(s32[144,1]{0,1:T(1,128)} %param.18) | copy-start | bytes 1732
  25.4 2.0 %copy-start.19 = (s32[1152]{0:T(1024)S(1)}, s32[1152]{0:T(1024)}, u32[]{:S(2)}) copy-start(s32[1152]{0:T(1024)} %param.17) | copy-start | bytes 13828
  25.4 2.0 %copy-start.23 = (bf16[1152]{0:T(1024)(128)(2,1)S(1)}, bf16[1152]{0:T(1024)(128)(2,1)}, u32[]{:S(2)}) copy-start(bf16[1152]{0:T(1024)(128)(2,1)} %param.16) | copy-start | bytes 6916
  27.4 31.8 %copy-start.4 = (bf16[12,128,384]{2,1,0:T(8,128)(2,1)}, bf16[12,128,384]{2,1,0:T(8,128)(2,1)S(1)}, u32[]{:S(2)}) copy-start(bf16[12,128,384]{2,1,0:T(8,128)(2,1)S(1)} %late_weights.1.late) | copy-start | bytes 3538948
  35.4 12.2 %copy-start.11 = (bf16[256,256]{1,0:T(8,128)(2,1)S(1)}, bf16[256,256]{1,0:T(8,128)(2,1)}, u32[]{:S(2)}) copy-start(bf16[256,256]{1,0:T(8,128)(2,1)} %get-tuple-element.44.w_mix) | copy-start | bytes 393220
  35.4 12.2 %copy-start.16 = (f32[128]{0:T(128)S(1)}, f32[128]{0:T(128)}, u32[]{:S(2)}) copy-start(f32[128]{0:T(128)} %param.14) | copy-start | bytes 1540
  40.7 14.6 %collective-permute-start.4 = (bf16[12,264,128]{2,1,0:T(8,128)(2,1)S(1)}, bf16[12,264,128]{2,1,0:T(8,128)(2,1)S(1)}, u32[]{:S(2)}, u32[]{:S(2)}) collective-permute-start(bf16[12,264,128]{2,1,0:T(8,128)(2,1)S(1)} %get-tuple-element.48), channel_id=1, source_target_pairs={{0,16},{16,32},{32,48},{48,64},{64,80},{80,96},{96,112},{1,17},{17... | collective-permute-start | bytes 2433032 | tf_op jit(solution)/shard_map/ppermute | solution.py:255
  45.6 13.6 %collective-permute-start.5 = (bf16[12,264,128]{2,1,0:T(8,128)(2,1)S(1)}, bf16[12,264,128]{2,1,0:T(8,128)(2,1)S(1)}, u32[]{:S(2)}, u32[]{:S(2)}) collective-permute-start(bf16[12,264,128]{2,1,0:T(8,128)(2,1)S(1)} %get-tuple-element.49), channel_id=1, source_target_pairs={{16,0},{32,16},{48,32},{64,48},{80,64},{96,80},{112,96},{17,1},{33... | collective-permute-start | bytes 2433032 | tf_op jit(solution)/shard_map/ppermute | solution.py:255
  47.6 11.6 %copy-start.12 = (bf16[256,256]{1,0:T(8,128)(2,1)S(1)}, bf16[256,256]{1,0:T(8,128)(2,1)}, u32[]{:S(2)}) copy-start(bf16[256,256]{1,0:T(8,128)(2,1)} %get-tuple-element.51.w_coarse) | copy-start | bytes 393220
  55.3 13.4 %copy-start.5 = (bf16[12,264,128]{2,1,0:T(8,128)(2,1)}, bf16[12,264,128]{2,1,0:T(8,128)(2,1)S(1)}, u32[]{:S(2)}) copy-start(bf16[12,264,128]{2,1,0:T(8,128)(2,1)S(1)} %collective-permute-done.4.cu.cut) | copy-start | bytes 2433028
  59.2 9.5 %copy-start.7 = (bf16[12,264,128]{2,1,0:T(8,128)(2,1)}, bf16[12,264,128]{2,1,0:T(8,128)(2,1)S(1)}, u32[]{:S(2)}) copy-start(bf16[12,264,128]{2,1,0:T(8,128)(2,1)S(1)} %collective-permute-done.5.cd.cdt) | copy-start | bytes 2433028
  68.7 4.8 %copy-start.1 = (bf16[12,1152,128]{2,1,0:T(8,128)(2,1)}, bf16[12,1152,128]{2,1,0:T(8,128)(2,1)S(1)}, u32[]{:S(2)}) copy-start(bf16[12,1152,128]{2,1,0:T(8,128)(2,1)S(1)} %get-tuple-element.56.own.x) | copy-start | bytes 10616836
  68.7 50.9 %collective-permute-start.6 = (bf16[12,392,128]{2,1,0:T(8,128)(2,1)}, bf16[12,392,128]{2,1,0:T(8,128)(2,1)S(1)}, u32[]{:S(2)}, u32[]{:S(2)}) collective-permute-start(bf16[12,392,128]{2,1,0:T(8,128)(2,1)} %get-tuple-element.57), channel_id=1, source_target_pairs={{0,1},{1,2},{2,3},{3,4},{4,5},{5,6},{6,7},{7,8},{8,9},{9,10},{10,1... | collective-permute-start | bytes 3612680 | tf_op jit(solution)/shard_map/ppermute | solution.py:255
  71.0 48.7 %collective-permute-start.7 = (bf16[12,392,128]{2,1,0:T(8,128)(2,1)}, bf16[12,392,128]{2,1,0:T(8,128)(2,1)S(1)}, u32[]{:S(2)}, u32[]{:S(2)}) collective-permute-start(bf16[12,392,128]{2,1,0:T(8,128)(2,1)} %get-tuple-element.58), channel_id=1, source_target_pairs={{1,0},{2,1},{3,2},{4,3},{5,4},{6,5},{7,6},{8,7},{9,8},{10,9},{11,1... | collective-permute-start | bytes 3612680 | tf_op jit(solution)/shard_map/ppermute | solution.py:255
  73.5 1.0 copy-start.17
  74.5 31.1 %collective-permute-start.8 = (bf16[12,384,128]{2,1,0:T(8,128)(2,1)}, bf16[12,384,128]{2,1,0:T(8,128)(2,1)}, u32[]{:S(2)}, u32[]{:S(2)}) collective-permute-start(bf16[12,384,128]{2,1,0:T(8,128)(2,1)} %get-tuple-element.60), channel_id=1, source_target_pairs={{0,16},{16,32},{32,48},{48,64},{64,80},{80,96},{96,112},{1,17},{17... | collective-permute-start | bytes 3538952 | tf_op jit(solution)/shard_map/ppermute | solution.py:255
  77.4 27.8 %all-to-all-start = ((bf16[128,2,768]{2,1,0:T(2,128)(2,1)}), bf16[128,2,768]{2,1,0:T(2,128)(2,1)S(1)}, u32[]{:S(2)}, u32[]{:S(2)}) async-start(bf16[128,2,768]{2,1,0:T(2,128)(2,1)} %reshape.41), calls=%async_computation | async-start | bytes 786432 | tf_op jit(solution)/shard_map/all_to_all | solution.py:367
  89.7 44.2 %collective-permute-start.11 = (bf16[12,384,128]{2,1,0:T(8,128)(2,1)}, bf16[12,384,128]{2,1,0:T(8,128)(2,1)}, u32[]{:S(2)}, u32[]{:S(2)}) collective-permute-start(bf16[12,384,128]{2,1,0:T(8,128)(2,1)} %copy-done.17), channel_id=1, source_target_pairs={{16,0},{32,16},{48,32},{64,48},{80,64},{96,80},{112,96},{17,1},{33... | collective-permute-start | bytes 3538952 | tf_op jit(solution)/shard_map/ppermute | solution.py:255
  106.5 25.5 %all-to-all-start.1 = ((bf16[128,2,768]{2,1,0:T(2,128)(2,1)}), bf16[128,2,768]{2,1,0:T(2,128)(2,1)}, u32[]{:S(2)}, u32[]{:S(2)}) async-start(bf16[128,2,768]{2,1,0:T(2,128)(2,1)} %broadcast_in_dim.42), calls=%async_computation.1 | async-start | bytes 786432 | tf_op jit(solution)/shard_map/all_to_all | solution.py:371
  119.6 6.9 %copy-start.6 = (bf16[12,264,128]{2,1,0:T(8,128)(2,1)S(1)}, bf16[12,264,128]{2,1,0:T(8,128)(2,1)}, u32[]{:S(2)}) copy-start(bf16[12,264,128]{2,1,0:T(8,128)(2,1)} %copy-done.5) | copy-start | bytes 2433028
  119.6 6.9 %copy-start.8 = (bf16[12,264,128]{2,1,0:T(8,128)(2,1)S(1)}, bf16[12,264,128]{2,1,0:T(8,128)(2,1)}, u32[]{:S(2)}) copy-start(bf16[12,264,128]{2,1,0:T(8,128)(2,1)} %copy-done.7) | copy-start | bytes 2433028
  119.6 6.9 %copy-start.10 = (bf16[9,6,128,128]{3,2,1,0:T(8,128)(2,1)S(1)}, bf16[9,6,128,128]{3,2,1,0:T(8,128)(2,1)}, u32[]{:S(2)}) copy-start(bf16[9,6,128,128]{3,2,1,0:T(8,128)(2,1)} %adj.7) | copy-start | bytes 5308420
  119.6 6.9 %copy-start.15 = (s32[54]{0:T(128)S(1)}, s32[54]{0:T(128)}, u32[]{:S(2)}) copy-start(s32[54]{0:T(128)} %copy-done.14) | copy-start | bytes 652
  119.7 6.9 %copy-start.2 = (bf16[12,392,128]{2,1,0:T(8,128)(2,1)}, bf16[12,392,128]{2,1,0:T(8,128)(2,1)S(1)}, u32[]{:S(2)}) copy-start(bf16[12,392,128]{2,1,0:T(8,128)(2,1)S(1)} %collective-permute-done.6.lt.lb.ylt.yl) | copy-start | bytes 3612676
  119.7 6.8 %copy-start.3 = (bf16[12,392,128]{2,1,0:T(8,128)(2,1)}, bf16[12,392,128]{2,1,0:T(8,128)(2,1)S(1)}, u32[]{:S(2)}) copy-start(bf16[12,392,128]{2,1,0:T(8,128)(2,1)S(1)} %collective-permute-done.7.rt.rb.yrt.yr) | copy-start | bytes 3612676
  120.8 13.3 %collective-permute-start.9 = (bf16[12,264,128]{2,1,0:T(8,128)(2,1)}, bf16[12,264,128]{2,1,0:T(8,128)(2,1)}, u32[]{:S(2)}, u32[]{:S(2)}) collective-permute-start(bf16[12,264,128]{2,1,0:T(8,128)(2,1)} %get-tuple-element.64), channel_id=1, source_target_pairs={{0,16},{16,32},{32,48},{48,64},{64,80},{80,96},{96,112},{1,17},{17... | collective-permute-start | bytes 2433032 | tf_op jit(solution)/shard_map/ppermute | solution.py:255
  124.6 13.7 %collective-permute-start.10 = (bf16[12,264,128]{2,1,0:T(8,128)(2,1)S(1)}, bf16[12,264,128]{2,1,0:T(8,128)(2,1)}, u32[]{:S(2)}, u32[]{:S(2)}) collective-permute-start(bf16[12,264,128]{2,1,0:T(8,128)(2,1)S(1)} %get-tuple-element.65), channel_id=1, source_target_pairs={{16,0},{32,16},{48,32},{64,48},{80,64},{96,80},{112,96},{17,1},{33... | collective-permute-start | bytes 2433032 | tf_op jit(solution)/shard_map/ppermute | solution.py:255
  128.6 0.7 copy-start.13
